TPU v7x, 32 devices: a whole 2x2x4 slice. The times are simulated.
32 devices in a mesh: seq: 8 (over y, x, core), head: 4 (over z).
Axes of the slice: x: 2, y: 2, z: 4, core: 2. Of those that a mesh axis runs over, the one named last changes fastest.
Arguments:
- history: bfloat16 [3072, 1024], P('seq'), may hold values from -40 to 40
- w_query: bfloat16 [1024, 256], P(None, 'head'), may hold values from -0.1875 to 0.1875
- w_key: bfloat16 [1024, 256], P(None, 'head'), may hold values from -0.1875 to 0.1875
- w_value: bfloat16 [1024, 256], P(None, 'head'), may hold values from -0.1875 to 0.1875
- w_out: bfloat16 [256, 1024], P('head'), may hold values from -0.375 to 0.375
- norm_gain: float32 [1024], replicated, may hold values from 0.25 to 1.75
- neg_emb: bfloat16 [8192, 1024], P('head'), may hold values from -2 to 2
- pos_emb: bfloat16 [3072, 1024], P('seq'), may hold values from -0.59765625 to 0.59765625
- neg_ids: int32 [8192], P('head'), may hold values from 0 to 15
- target_ids: int32 [3072], P('seq'), may hold values from 0 to 15
- pad_mask: int32 [3072], P('seq'), may hold values 0 or 1
Outputs:
- user_state: bfloat16 [3072, 1024], P('seq', 'head')
- loss: float32 [3072], P('seq')
All inputs are finite; a program needn't handle non-finite values. No bound on the sum of `pad_mask` on one device may be relied on, other than what follows from the above.
Results may differ from a plain program's by a relative error of at most 0.012.
Values may be sent and summed in bfloat16 or wider, within the bound.
No kernel may reach another device: no remote copies, remote signals or barrier semaphores. Data moves between devices by JAX's collectives and lax.ppermute only.
A program may use at most 64 MiB of HBM per device.

v0:
```python
import jax
import jax.numpy as jnp
from jax import lax
from jax.sharding import PartitionSpec as P

HD = 64
WIN = 256


def from_behind(shard, axis, by):
    count = lax.axis_size(axis)
    pairs = [(i, i + by) for i in range(count) if 0 <= i + by < count]
    return lax.ppermute(shard, axis, pairs)


def on_device(
    history,
    w_query,
    w_key,
    w_value,
    w_out,
    norm_gain,
    neg_emb,
    pos_emb,
    neg_ids,
    target_ids,
    pad_mask,
):
    rows_here = history.shape[0]
    width = history.shape[1]
    local_cols = w_query.shape[1]
    heads_here = local_cols // HD
    query = jnp.dot(history, w_query, preferred_element_type=jnp.float32).astype(jnp.bfloat16)
    key = jnp.dot(history, w_key, preferred_element_type=jnp.float32).astype(jnp.bfloat16)
    value = jnp.dot(history, w_value, preferred_element_type=jnp.float32).astype(jnp.bfloat16)
    kv_last = jnp.stack([key[rows_here - WIN :], value[rows_here - WIN :]], 0)
    flag_last = pad_mask[rows_here - WIN :].astype(jnp.bfloat16)
    kv_prev, flag_prev = from_behind((kv_last, flag_last), "seq", 1)
    keys_all = jnp.concatenate([kv_prev[0], key], 0).reshape(WIN + rows_here, heads_here, HD)
    values_all = jnp.concatenate([kv_prev[1], value], 0).reshape(WIN + rows_here, heads_here, HD)
    flags_all = jnp.concatenate([flag_prev.astype(jnp.int32), pad_mask], 0)
    rows = lax.broadcasted_iota(jnp.int32, (rows_here, rows_here + WIN), 0)
    cols = lax.broadcasted_iota(jnp.int32, (rows_here, rows_here + WIN), 1)
    diff = rows + WIN - cols
    allowed = (diff >= 0) & (diff < WIN) & ((flags_all[None, :] == 1) | (diff == 0))
    scores = jnp.einsum(
        "qhd,khd->hqk",
        query.reshape(rows_here, heads_here, HD),
        keys_all,
        preferred_element_type=jnp.float32,
    ) * HD ** (-0.5)
    scores = jnp.where(allowed[None], scores, -1e30)
    top = jnp.max(scores, -1, keepdims=True)
    weights = jnp.where(allowed[None], jnp.exp(scores - top), 0.0)
    prob = (weights / jnp.sum(weights, -1, keepdims=True)).astype(jnp.bfloat16)
    heads_out = jnp.einsum("hqk,khd->qhd", prob, values_all, preferred_element_type=jnp.float32)
    heads_out = heads_out.astype(jnp.bfloat16).reshape(rows_here, local_cols)
    partial_proj = jnp.dot(heads_out, w_out, preferred_element_type=jnp.float32)
    share_cols = width // lax.axis_size("head")
    col_start = lax.axis_index("head") * share_cols
    attn = lax.psum(partial_proj.astype(jnp.bfloat16), "head").astype(jnp.float32)
    mean_sq = jnp.mean(attn * attn, 1, keepdims=True)
    user_full = (attn * lax.rsqrt(mean_sq + 1e-05) * norm_gain[None, :]).astype(jnp.bfloat16)
    user_share = lax.dynamic_slice_in_dim(user_full, col_start, share_cols, 1)
    neg_logit = lax.dot_general(
        user_full, neg_emb, (((1,), (1,)), ((), ())), preferred_element_type=jnp.float32
    )
    pos_logit = jnp.einsum("sd,sd->s", user_full, pos_emb, preferred_element_type=jnp.float32)
    hit = neg_ids[None, :] == target_ids[:, None]
    masked = jnp.where(hit, -1e30, neg_logit)
    local_top = jnp.max(masked, 1)
    global_top = lax.pmax(local_top, "head")
    upper = jnp.maximum(global_top, pos_logit)
    local_total = jnp.sum(jnp.where(hit, 0.0, jnp.exp(masked - upper[:, None])), 1)
    total = lax.psum(local_total, "head")
    lse = upper + jnp.log(total + jnp.exp(pos_logit - upper))
    return (user_share, lse - pos_logit)


def solution(mesh):
    return jax.shard_map(
        on_device,
        mesh=mesh,
        in_specs=(
            P("seq", None),
            P(None, "head"),
            P(None, "head"),
            P(None, "head"),
            P("head", None),
            P(),
            P("head", None),
            P("seq", None),
            P("head"),
            P("seq"),
            P("seq"),
        ),
        out_specs=(P("seq", "head"), P("seq")),
        check_vma=False,
    )
```

profile of v0, /device:TPU:4, one launch (start us, length us, event | category | flops | bytes accessed | tf_op | source)
XLA Modules:
  0.0 107.3 jit_solution(7094348422839087139)
XLA Ops:
  7.2 0.0 copy-start
  7.2 0.0 all-reduce.2.cloned.1.call-start
  7.2 1.1 %copy-done = bf16[384,1024]{1,0:T(8,128)(2,1)S(1)} copy-done((bf16[384,1024]{1,0:T(8,128)(2,1)S(1)}, bf16[384,1024]{1,0:T(8,128)(2,1)}, u32[]{:S(2)}) %copy-start) | copy-done | bytes 786456
  8.3 1.3 %convolution_convert_fusion.2 = bf16[384,64]{0,1:T(8,128)(2,1)S(1)} fusion(bf16[384,1024]{1,0:T(8,128)(2,1)S(1)} %copy-done, bf16[1024,64]{0,1:T(8,128)(2,1)} %param.14), kind=kOutput, calls=%fused_computation.14 | convolution fusion | flops 50356224 | bytes 966656 | tf_op jit(solution)/shard_map/dot_general | solution.py:35
  9.6 0.0 copy-start.5
  9.6 1.3 %convolution_convert_fusion.3 = bf16[384,64]{0,1:T(8,128)(2,1)S(1)} fusion(bf16[384,1024]{1,0:T(8,128)(2,1)S(1)} %copy-done, bf16[1024,64]{0,1:T(8,128)(2,1)} %param.13), kind=kOutput, calls=%fused_computation.15 | convolution fusion | flops 50356224 | bytes 966656 | tf_op jit(solution)/shard_map/dot_general | solution.py:34
  10.9 1.9 %collective-permute-start = (bf16[2,256,64]{1,2,0:T(8,128)(2,1)S(1)}, bf16[2,256,64]{1,2,0:T(8,128)(2,1)S(1)}, u32[]{:S(2)}, u32[]{:S(2)}) collective-permute-start(bf16[2,256,64]{1,2,0:T(8,128)(2,1)S(1)} %pad_maximum_fusion), channel_id=1, source_target_pairs={{0,4},{4,8},{8,12},{12,16},{16,20},{20,24},{24,28},{1,5},{5,9},{9,... | collective-permute-start | bytes 196616 | tf_op jit(solution)/shard_map/ppermute | solution.py:13
  12.8 0.7 convert.3
  13.5 3.5 %collective-permute-start.1 = (bf16[256]{0:T(256)(128)(2,1)S(1)}, bf16[256]{0:T(256)(128)(2,1)S(1)}, u32[]{:S(2)}, u32[]{:S(2)}) collective-permute-start(bf16[256]{0:T(256)(128)(2,1)S(1)} %slice.19), channel_id=1, source_target_pairs={{0,4},{4,8},{8,12},{12,16},{16,20},{20,24},{24,28},{1,5},{5,9},{9,... | collective-permute-start | bytes 1544 | tf_op jit(solution)/shard_map/ppermute | solution.py:13
  17.1 2.3 %collective-permute-done.1 = bf16[256]{0:T(256)(128)(2,1)S(1)} collective-permute-done((bf16[256]{0:T(256)(128)(2,1)S(1)}, bf16[256]{0:T(256)(128)(2,1)S(1)}, u32[]{:S(2)}, u32[]{:S(2)}) %collective-permute-start.1) | collective-permute-done | bytes 544 | tf_op jit(solution)/shard_map/ppermute | solution.py:13
  19.3 0.7 add_compare_fusion
  20.0 0.0 collective-permute-done
  20.0 1.8 %fusion.35 = (f32[384]{0:T(512)S(1)}, f32[384,640]{1,0:T(8,128)S(1)}) fusion(bf16[384,64]{0,1:T(8,128)(2,1)S(1)} %convolution_convert_fusion.3, bf16[256,64]{0,1:T(8,128)(2,1)S(1)} %get-tuple-element.5, bf16[384,1024]{1,0:T(8,128)(2,1)S(1)} %copy-done, bf16[1024,64]{0,1:T(8,128)(2,1)} %param.12, pred[640]{0:T(1024)(128)(4,1)S(1)} %add_compare_fusion, ...), kind=kOutput, calls=%fused_computation.49 | convolution fusion | flops 84434560 | bytes 1986176 | tf_op jit(solution)/shard_map/qhd,khd->hqk/dot_general | solution.py:46
  21.9 0.7 fusion.13
  22.6 0.0 copy-done.5
  22.6 0.0 copy-start.1
  22.6 0.0 copy-start.3
  22.6 2.0 %convolution_convert_fusion = bf16[384,1024]{1,0:T(8,128)(2,1)} fusion(bf16[64,1024]{1,0:T(8,128)(2,1)S(1)} %copy-done.5, f32[384,640]{1,0:T(8,128)S(1)} %get-tuple-element.7, f32[384]{0:T(512)S(1)} %fusion.13, f32[384]{0:T(512)S(1)} %get-tuple-element.6, s32[384]{0:T(512)S(1)} %iota_add_fusion, pred[640]{0:T(1024)(128)(4,1)S(1)} %add_compare_fusion, ...), kind=kOutput, calls=%fused_computation.10 | convolution fusion | flops 85073920 | bytes 1987712 | tf_op jit(solution)/shard_map/dot_general | solution.py:58
  24.6 0.0 copy-start.2
  24.6 0.0 copy-start.4
  24.6 0.0 all-reduce.2.cloned.1.call-update
  24.7 44.3 %all-reduce.2.cloned.1.call-done = bf16[384,1024]{1,0:T(8,128)(2,1)} async-done(((bf16[384,1024]{1,0:T(8,128)(2,1)}), bf16[384,1024]{1,0:T(8,128)(2,1)}) %all-reduce.2.cloned.1.call-update) | async-done | bytes 786448 | tf_op jit(solution)/shard_map/psum | solution.py:61
  69.0 1.4 %fusion.1 = f32[384]{0:T(512)S(1)} fusion(bf16[384,1024]{1,0:T(8,128)(2,1)} %all-reduce.2.cloned.1.call-done), kind=kLoop, calls=%fused_computation.5 | loop fusion | flops 1179264 | bytes 787968 | tf_op jit(solution)/shard_map/reduce_sum | solution.py:62
  70.4 0.0 copy-done.1
  70.4 0.0 copy-done.3
  70.4 1.6 %fusion.4 = (f32[384]{0:T(512)S(1)}, bf16[384,1024]{1,0:T(8,128)(2,1)S(1)}) fusion(bf16[384,1024]{1,0:T(8,128)(2,1)S(1)} %copy-done.1, f32[1024]{0:T(1024)S(1)} %copy-done.3, f32[384]{0:T(512)S(1)} %add_rsqrt_fusion, bf16[384,1024]{1,0:T(8,128)(2,1)} %all-reduce.2.cloned.1.call-done), kind=kLoop, calls=%fused_computation.9 | loop fusion | flops 3145344 | bytes 2366464 | tf_op jit(solution)/shard_map/sd,sd->s/dot_general | solution.py:68
  72.0 0.0 copy-done.2
  72.0 0.0 copy-done.4
  72.0 5.7 %fusion.36 = (f32[384]{0:T(512)S(1)}, f32[384,2048]{1,0:T(8,128)}) fusion(bf16[384,1024]{1,0:T(8,128)(2,1)S(1)} %get-tuple-element.3, bf16[2048,1024]{1,0:T(8,128)(2,1)} %param.17, s32[384]{0:T(512)S(1)} %copy-done.4, s32[2048]{0:T(1024)S(1)} %copy-done.2), kind=kOutput, calls=%fused_computation.50 | convolution fusion | flops 1612971648 | bytes 8137728 | tf_op jit(solution)/shard_map/dot_general | solution.py:65
  77.8 10.0 %pmax.7 = f32[384]{0:T(512)S(1)} all-reduce(f32[384]{0:T(512)S(1)} %get-tuple-element.8), channel_id=1, replica_groups=mesh['seq'=8,'head'=4] {'head'}, use_global_device_ids=true, to_apply=%region_5.6 | all-reduce | flops 384 | bytes 3072 | tf_op jit(solution)/shard_map/pmax | solution.py:72
  87.8 2.7 %fusion = f32[384]{0:T(512)S(1)} fusion(f32[384,2048]{1,0:T(8,128)} %get-tuple-element.9, f32[384]{0:T(512)S(1)} %max.5, s32[2048]{0:T(1024)S(1)} %copy-done.2, s32[384]{0:T(512)S(1)} %copy-done.4), kind=kLoop, calls=%fused_computation.2 | loop fusion | flops 3145344 | bytes 3158528 | tf_op jit(solution)/shard_map/reduce_sum | solution.py:74
  90.4 8.7 %psum.15 = f32[384]{0:T(512)S(1)} all-reduce(f32[384]{0:T(512)S(1)} %fusion), channel_id=1, replica_groups=mesh['seq'=8,'head'=4] {'head'}, use_global_device_ids=true, to_apply=%region_7.8 | all-reduce | flops 384 | bytes 3072 | tf_op jit(solution)/shard_map/psum | solution.py:75
  99.1 0.6 add_subtract_fusion
  99.7 0.7 constant_dynamic-slice_fusion
  (8 shorter events, 0.1 us)
Async XLA Ops:
  7.2 1.1 %copy-start = (bf16[384,1024]{1,0:T(8,128)(2,1)S(1)}, bf16[384,1024]{1,0:T(8,128)(2,1)}, u32[]{:S(2)}) copy-start(bf16[384,1024]{1,0:T(8,128)(2,1)} %param.11) | copy-start | bytes 2359300
  7.2 61.8 %all-reduce.2.cloned.1.call-start = ((), (), s32[]{:S(2)}) async-start(), calls=%async_computation | async-start | bytes 1572864 | tf_op jit(solution)/shard_map/psum | solution.py:61
  9.6 13.0 %copy-start.5 = (bf16[64,1024]{1,0:T(8,128)(2,1)S(1)}, bf16[64,1024]{1,0:T(8,128)(2,1)}, u32[]{:S(2)}) copy-start(bf16[64,1024]{1,0:T(8,128)(2,1)} %param.15) | copy-start | bytes 393220
  10.9 9.1 %collective-permute-start = (bf16[2,256,64]{1,2,0:T(8,128)(2,1)S(1)}, bf16[2,256,64]{1,2,0:T(8,128)(2,1)S(1)}, u32[]{:S(2)}, u32[]{:S(2)}) collective-permute-start(bf16[2,256,64]{1,2,0:T(8,128)(2,1)S(1)} %pad_maximum_fusion), channel_id=1, source_target_pairs={{0,4},{4,8},{8,12},{12,16},{16,20},{20,24},{24,28},{1,5},{5,9},{9,... | collective-permute-start | bytes 196616 | tf_op jit(solution)/shard_map/ppermute | solution.py:13
  13.5 5.8 %collective-permute-start.1 = (bf16[256]{0:T(256)(128)(2,1)S(1)}, bf16[256]{0:T(256)(128)(2,1)S(1)}, u32[]{:S(2)}, u32[]{:S(2)}) collective-permute-start(bf16[256]{0:T(256)(128)(2,1)S(1)} %slice.19), channel_id=1, source_target_pairs={{0,4},{4,8},{8,12},{12,16},{16,20},{20,24},{24,28},{1,5},{5,9},{9,... | collective-permute-start | bytes 1544 | tf_op jit(solution)/shard_map/ppermute | solution.py:13
  22.6 47.8 %copy-start.1 = (bf16[384,1024]{1,0:T(8,128)(2,1)S(1)}, bf16[384,1024]{1,0:T(8,128)(2,1)}, u32[]{:S(2)}) copy-start(bf16[384,1024]{1,0:T(8,128)(2,1)} %param.18) | copy-start | bytes 2359300
  22.6 47.8 %copy-start.3 = (f32[1024]{0:T(1024)S(1)}, f32[1024]{0:T(1024)}, u32[]{:S(2)}) copy-start(f32[1024]{0:T(1024)} %param.16) | copy-start | bytes 12292
  24.6 47.4 %copy-start.2 = (s32[2048]{0:T(1024)S(1)}, s32[2048]{0:T(1024)}, u32[]{:S(2)}) copy-start(s32[2048]{0:T(1024)} %param.19) | copy-start | bytes 24580
  24.6 47.4 %copy-start.4 = (s32[384]{0:T(512)S(1)}, s32[384]{0:T(512)}, u32[]{:S(2)}) copy-start(s32[384]{0:T(512)} %param.20) | copy-start | bytes 4612
Sparse Core Ops, SparseCore 0:
  24.8 44.1 all-reduce.1
where the time goes:
time: 109 us; the launch traced here: 107 us
  waiting for transfers between devices  46.6 us (43%)
  blocking collectives  18.7 us (17%)
  between operations  14.2 us (13%)
  matrix products  12.2 us (11%)
  other arithmetic  8.34 us (8%)
  starting transfers between devices  5.45 us (5%)
  local copies, waits for them, and re-layouts  1.84 us (2%)
    psum x1, waiting for transfers between devices, on_device(): lax.psum(partial_proj.astype(jnp.bfloat16), 'head').astype(jnp.float32)  44.3 us
    pmax x1, blocking collectives, on_device(): global_top = lax.pmax(local_top, 'head')  9.99 us
    psum x1, blocking collectives, on_device(): total = lax.psum(local_total, 'head')  8.73 us
    dot_general x1, matrix products, on_device(): lax.dot_general(user_full, neg_emb, (((1,), (1,)), ((), ())), preferred_e...  5.73 us
    ppermute x2, starting transfers between devices, from_behind(): return lax.ppermute(shard, axis, pairs)  5.41 us
    reduce_sum x1, other arithmetic, on_device(): jnp.sum(jnp.where(hit, 0.0, jnp.exp(masked - upper[:, None])), 1)  2.65 us
    ppermute x2, waiting for transfers between devices, from_behind(): return lax.ppermute(shard, axis, pairs)  2.27 us
  transfers between devices with their start and end apart: 3, of which 2 were waited for; matrix products, arithmetic and copies ran while one was open for 1% of the time, Pallas kernels for 0%

commit v1 on v0

v1 whole, which is shorter than its diff:
```python
import functools

import jax
import jax.numpy as jnp
from jax import lax
from jax.experimental import pallas as pl
from jax.experimental.pallas import tpu as pltpu
from jax.sharding import PartitionSpec as P

HD = 64
WIN = 256
LANES = 128
FLAG_ROWS = 16
LOW = -1e30
MIB = 1 << 20
F32 = jnp.float32
BF16 = jnp.bfloat16
WHOLE = pl.BlockSpec(memory_space=pltpu.VMEM)
RAW = pl.BlockSpec(memory_space=pl.ANY)


def dot_last(a, b):
    return lax.dot_general(a, b, (((1,), (1,)), ((), ())), preferred_element_type=F32)


def dot_plain(a, b):
    return lax.dot_general(a, b, (((1,), (0,)), ((), ())), preferred_element_type=F32)


def from_behind(shard, axis, by):
    count = lax.axis_size(axis)
    pairs = [(i, i + by) for i in range(count) if 0 <= i + by < count]
    return lax.ppermute(shard, axis, pairs)


def partners(axis):
    count = lax.axis_size(axis)
    if count & (count - 1) == 0:
        return [[(i, i ^ k) for i in range(count)] for k in range(count - 1, 0, -1)]
    return [[(i, (i + k) % count) for i in range(count)] for k in range(count - 1, 0, -1)]


def from_all(shard, axis):
    return [shard] + [lax.ppermute(shard, axis, pairs) for pairs in partners(axis)]


def project_body(hist_hbm, wq_ref, wk_ref, wv_ref, pad_ref, q_ref, own_ref, edge_ref, hist, sems):
    rows, width = hist.shape
    cols = wq_ref.shape[0]
    step = LANES
    copies = []
    for n, start in enumerate(range(0, rows, step)):
        part = pl.ds(start, step)
        copies.append(pltpu.make_async_copy(hist_hbm.at[part], hist.at[part], sems.at[n]))
        copies[-1].start()
    weights = jnp.concatenate([wq_ref[...], wk_ref[...], wv_ref[...]], 0)
    flags = jnp.broadcast_to(pad_ref[...], (FLAG_ROWS, rows)).astype(F32).astype(BF16)
    own_ref[2 * cols :, :] = flags
    edge_ref[2 * cols :, :] = flags[:, rows - WIN :]
    for n, start in enumerate(range(0, rows, step)):
        copies[n].wait()
        out = dot_last(hist[start : start + step, :], weights)
        q_ref[start : start + step, :] = out[:, :cols].astype(BF16)
        kv = out[:, cols:].T.astype(BF16)
        own_ref[: 2 * cols, start : start + step] = kv
        if start >= rows - WIN:
            at = start - (rows - WIN)
            edge_ref[: 2 * cols, at : at + step] = kv


def project(history, w_query, w_key, w_value, pad_mask):
    rows, width = history.shape
    cols = w_query.shape[1]
    tall = 2 * cols + FLAG_ROWS
    return pl.pallas_call(
        project_body,
        name="project",
        out_shape=(
            jax.ShapeDtypeStruct((rows, cols), BF16),
            jax.ShapeDtypeStruct((tall, rows), BF16),
            jax.ShapeDtypeStruct((tall, WIN), BF16),
        ),
        in_specs=[RAW, WHOLE, WHOLE, WHOLE, WHOLE],
        out_specs=(WHOLE, WHOLE, WHOLE),
        scratch_shapes=[
            pltpu.VMEM((rows, width), BF16),
            pltpu.SemaphoreType.DMA((rows // LANES,)),
        ],
        compiler_params=pltpu.CompilerParams(vmem_limit_bytes=8 * MIB),
        cost_estimate=pl.CostEstimate(flops=6 * rows * width * cols, bytes_accessed=2 * rows * width, transcendentals=0),
    )(history, w_query.T, w_key.T, w_value.T, pad_mask[None, :])


def attend_body(q_ref, own_ref, prev_ref, out_ref):
    rows, cols = q_ref.shape
    step = LANES
    span = WIN + step
    at_row = lax.broadcasted_iota(jnp.int32, (step, span), 0)
    at_col = lax.broadcasted_iota(jnp.int32, (step, span), 1)
    near = (at_col > at_row) & (at_col <= at_row + WIN)
    self_pos = at_col == at_row + WIN

    def window(lo, hi, first):
        parts = []
        if first < WIN:
            parts.append(prev_ref[lo:hi, first:WIN])
        last = first + span
        if last > WIN:
            parts.append(own_ref[lo:hi, max(first - WIN, 0) : last - WIN])
        return parts[0] if len(parts) == 1 else jnp.concatenate(parts, 1)

    for start in range(0, rows, step):
        flags = window(2 * cols, 2 * cols + FLAG_ROWS, start).astype(F32)[:1]
        allowed = near & ((flags == 1.0) | self_pos)
        for head in range(cols // HD):
            lo = head * HD
            scores = dot_plain(q_ref[start : start + step, lo : lo + HD], window(lo, lo + HD, start)) * HD**-0.5
            scores = jnp.where(allowed, scores, LOW)
            top = jnp.max(scores, 1, keepdims=True)
            weights = jnp.where(allowed, jnp.exp(scores - top), 0.0)
            prob = (weights / jnp.sum(weights, 1, keepdims=True)).astype(BF16)
            value = window(cols + lo, cols + lo + HD, start)
            out_ref[lo : lo + HD, start : start + step] = dot_last(value, prob).astype(BF16)


def attend(query, own, prev):
    rows, cols = query.shape
    return pl.pallas_call(
        attend_body,
        name="attend",
        out_shape=jax.ShapeDtypeStruct((cols, rows), BF16),
        in_specs=[WHOLE] * 3,
        out_specs=WHOLE,
        compiler_params=pltpu.CompilerParams(vmem_limit_bytes=8 * MIB),
        cost_estimate=pl.CostEstimate(flops=4 * rows * 2 * WIN * cols, bytes_accessed=6 * rows * cols, transcendentals=rows * 2 * WIN),
    )(query, own, prev)


def premix_body(count, neg_ref, *refs):
    w_refs = refs[:count]
    gain_ref, gain_here, pos_ref, ids_ref, mix_ref, turned_ref, id_ref, pos_out, scaled = refs[count:]

    @pl.when(pl.program_id(0) == 0)
    def _():
        gain = gain_ref[...]
        for n in range(count):
            piece = w_refs[n][...].astype(F32)
            tall = piece.shape[0]
            scaled[n * tall : (n + 1) * tall, :] = (piece * gain).astype(BF16)
        whole = jnp.concatenate([ref[...].astype(F32) for ref in w_refs], 0)
        turned_ref[...] = whole.T.astype(BF16)
        for n in range(ids_ref.shape[0]):
            line = jnp.broadcast_to(ids_ref[n : n + 1, :], (LANES, LANES))
            id_ref[n * LANES : (n + 1) * LANES, :] = line.T
        pos_out[...] = (pos_ref[...].astype(F32) * gain_here[...]).T

    mix_ref[...] = dot_last(neg_ref[...], scaled[...]).astype(BF16)


def premix(neg_emb, pieces, gain, gain_here, pos_here, neg_ids):
    negs, width = neg_emb.shape
    count = len(pieces)
    deep = count * pieces[0].shape[0]
    rows, share = pos_here.shape
    block = 512
    const = lambda shape: pl.BlockSpec(shape, lambda i: (0, 0))
    return pl.pallas_call(
        functools.partial(premix_body, count),
        name="premix",
        grid=(negs // block,),
        out_shape=(
            jax.ShapeDtypeStruct((negs, deep), BF16),
            jax.ShapeDtypeStruct((width, deep), BF16),
            jax.ShapeDtypeStruct((negs, LANES), jnp.int32),
            jax.ShapeDtypeStruct((share, rows), F32),
        ),
        in_specs=[pl.BlockSpec((block, width), lambda i: (i, 0))]
        + [const(p.shape) for p in pieces]
        + [const((1, width)), const((1, share)), const((rows, share)), const((negs // LANES, LANES))],
        out_specs=(
            pl.BlockSpec((block, deep), lambda i: (i, 0)),
            const((width, deep)),
            const((negs, LANES)),
            const((share, rows)),
        ),
        scratch_shapes=[pltpu.VMEM((deep, width), BF16)],
        compiler_params=pltpu.CompilerParams(vmem_limit_bytes=28 * MIB),
        cost_estimate=pl.CostEstimate(flops=2 * negs * width * deep, bytes_accessed=2 * negs * width, transcendentals=0),
    )(neg_emb, *pieces, gain[None, :], gain_here[None, :], pos_here, neg_ids.reshape(-1, LANES))


def score_body(count, *refs):
    o_refs = refs[:count]
    mix_ref, turned_ref, id_ref, pos_ref, target_ref, here_ref, stat_ref, user_ref, attn, logits = refs[count:]
    width, rows = attn.shape
    share = user_ref.shape[0]
    negs = mix_ref.shape[0]
    block = 256
    heads = jnp.concatenate([ref[...] for ref in o_refs], 0)
    total = jnp.zeros((8, rows), F32)
    for start in range(0, width, block):
        part = dot_plain(turned_ref[start : start + block, :], heads)
        attn[start : start + block, :] = part
        total += jnp.sum((part * part).reshape(block // 8, 8, rows), 0)
    scale = lax.rsqrt(jnp.sum(total, 0, keepdims=True) / width + 1e-05)
    here = pl.multiple_of(here_ref[0] * share, share)
    user = attn[pl.ds(here, share), :] * scale
    user_ref[...] = user
    pos = jnp.sum(user * pos_ref[...], 0, keepdims=True)
    target = target_ref[...]
    top = jnp.full((8, rows), LOW, F32)
    for start in range(0, negs, block):
        part = dot_plain(mix_ref[start : start + block, :], heads) * scale
        ids = id_ref[start : start + block, :]
        hit = jnp.concatenate([ids] * (rows // LANES), 1) == target
        part = jnp.where(hit, LOW, part)
        logits[start : start + block, :] = part
        top = jnp.maximum(top, jnp.max(part.reshape(block // 8, 8, rows), 0))
    top = jnp.max(top, 0, keepdims=True)
    mass = jnp.zeros((8, rows), F32)
    for start in range(0, negs, block):
        part = jnp.exp(logits[start : start + block, :] - top)
        mass += jnp.sum(part.reshape(block // 8, 8, rows), 0)
    mass = jnp.sum(mass, 0, keepdims=True)
    stat_ref[...] = jnp.concatenate([top, mass, pos, pos], 0)


def score(heads, mix, turned, id_cols, pos_turned, target_ids, here):
    count = len(heads)
    negs, deep = mix.shape
    width = turned.shape[0]
    share, rows = pos_turned.shape
    return pl.pallas_call(
        functools.partial(score_body, count),
        name="score",
        out_shape=(
            jax.ShapeDtypeStruct((4, rows), F32),
            jax.ShapeDtypeStruct((share, rows), F32),
        ),
        in_specs=[WHOLE] * (count + 5) + [pl.BlockSpec(memory_space=pltpu.SMEM)],
        out_specs=(WHOLE, WHOLE),
        scratch_shapes=[pltpu.VMEM((width, rows), F32), pltpu.VMEM((negs, rows), F32)],
        compiler_params=pltpu.CompilerParams(vmem_limit_bytes=28 * MIB),
        cost_estimate=pl.CostEstimate(flops=2 * rows * deep * (negs + width), bytes_accessed=2 * negs * deep, transcendentals=negs * rows),
    )(*heads, mix, turned, id_cols, pos_turned, target_ids[None, :], here)


def finish_body(user_ref, gain_ref, out_ref):
    out_ref[...] = (user_ref[...].T * gain_ref[...]).astype(BF16)


def finish(user, gain_here):
    share, rows = user.shape
    return pl.pallas_call(
        finish_body,
        name="finish",
        out_shape=jax.ShapeDtypeStruct((rows, share), BF16),
        in_specs=[WHOLE, WHOLE],
        out_specs=WHOLE,
        compiler_params=pltpu.CompilerParams(vmem_limit_bytes=8 * MIB),
        cost_estimate=pl.CostEstimate(flops=2 * rows * share, bytes_accessed=6 * rows * share, transcendentals=0),
    )(user, gain_here[None, :])


def on_device(
    history,
    w_query,
    w_key,
    w_value,
    w_out,
    norm_gain,
    neg_emb,
    pos_emb,
    neg_ids,
    target_ids,
    pad_mask,
):
    width = history.shape[1]
    share = width // lax.axis_size("head")
    me = lax.axis_index("head")
    pos_here = lax.dynamic_slice_in_dim(pos_emb, me * share, share, 1)
    gain_here = lax.dynamic_slice_in_dim(norm_gain, me * share, share, 0)
    pieces = from_all(w_out, "head")
    query, own, edge = project(history, w_query, w_key, w_value, pad_mask)
    prev = from_behind(edge, "seq", 1)
    heads = from_all(attend(query, own, prev), "head")
    mix, turned, id_cols, pos_turned = premix(neg_emb, pieces, norm_gain, gain_here, pos_here, neg_ids)
    stats, user = score(heads, mix, turned, id_cols, pos_turned, target_ids, me[None].astype(jnp.int32))
    all_stats = from_all(stats, "head")
    user_share = finish(user, gain_here)
    pos_logit = functools.reduce(jnp.add, [s[2] for s in all_stats])
    upper = functools.reduce(jnp.maximum, [s[0] for s in all_stats], pos_logit)
    total = functools.reduce(jnp.add, [s[1] * jnp.exp(s[0] - upper) for s in all_stats])
    loss = upper + jnp.log(total + jnp.exp(pos_logit - upper)) - pos_logit
    return (user_share, loss)


def solution(mesh):
    return jax.shard_map(
        on_device,
        mesh=mesh,
        in_specs=(
            P("seq", None),
            P(None, "head"),
            P(None, "head"),
            P(None, "head"),
            P("head", None),
            P(),
            P("head", None),
            P("seq", None),
            P("head"),
            P("seq"),
            P("seq"),
        ),
        out_specs=(P("seq", "head"), P("seq")),
        check_vma=False,
    )
```

time: 109 us -> 41.2 us (0.38); the launches traced: 107 us -> 40.8 us
  waiting for transfers between devices: 46.6 us -> 6.08 us
  blocking collectives: 18.7 us -> 0 us
  between operations: 14.2 us -> 0.73 us
  matrix products: 12.2 us -> 0 us
  starting transfers between devices: 5.45 us -> 15.3 us
  local copies, waits for them, and re-layouts: 1.84 us -> 10.5 us
  other arithmetic: 8.34 us -> 0.66 us
  Pallas kernels: 0 us -> 7.54 us
    psum x1 -> x0, waiting for transfers between devices: 44.3 us -> none  [on_device(): lax.psum(partial_proj.astype(jnp.bfloat16), 'head').astype(jnp.float32)]
    ppermute x0 -> x9, starting transfers between devices: none -> 13.4 us  [from_all(): lax.ppermute(shard, axis, pairs)]
    dot_general x5 -> x0, matrix products: 12.2 us -> none  [the longest x1 5.73 us: on_device(): lax.dot_general(user_full, neg_emb, (((1,), (1,)), ((), ())), preferred_e...]
    pmax x1 -> x0, blocking collectives: 9.99 us -> none  [on_device(): global_top = lax.pmax(local_top, 'head')]
    psum x1 -> x0, blocking collectives: 8.73 us -> none  [on_device(): total = lax.psum(local_total, 'head')]
    pallas_call x0 -> x5, Pallas kernels: none -> 7.54 us  [the longest x1 2.54 us: premix(): pl.pallas_call(functools.partial(premix_body, count), name='premix', grid...]
    unnamed x12 -> x18, local copies, waits for them, and re-layouts: 1.11 us -> 8.33 us
    reduce_sum x3 -> x0, other arithmetic: 4.71 us -> none  [the longest x1 2.65 us: on_device(): jnp.sum(jnp.where(hit, 0.0, jnp.exp(masked - upper[:, None])), 1)]
  transfers between devices with their start and end apart: 3 -> 10, of which waited for: 2 -> 3; matrix products, arithmetic and copies ran while one was open for 1% -> 5% of each run, Pallas kernels for 0% -> 15%
where the time goes in v1:
time: 41.2 us; the launch traced here: 40.8 us
  starting transfers between devices  15.3 us (37%)
  local copies, waits for them, and re-layouts  10.5 us (25%)
  Pallas kernels  7.54 us (18%)
  waiting for transfers between devices  6.08 us (15%)
  between operations  0.73 us (2%)
  other arithmetic  0.66 us (2%)
    ppermute x9, starting transfers between devices, from_all(): lax.ppermute(shard, axis, pairs)  13.4 us
    unnamed x18, local copies, waits for them, and re-layouts  8.33 us
    ppermute x1, waiting for transfers between devices, from_behind(): return lax.ppermute(shard, axis, pairs)  3.16 us
    ppermute x9, waiting for transfers between devices, from_all(): lax.ppermute(shard, axis, pairs)  2.92 us
    pallas_call x1, Pallas kernels, premix(): pl.pallas_call(functools.partial(premix_body, count), name='premix', grid...  2.54 us
    ppermute x1, starting transfers between devices, from_behind(): return lax.ppermute(shard, axis, pairs)  1.92 us
    pallas_call x1, Pallas kernels, project(): pl.pallas_call(project_body, name='project', out_shape=(jax.ShapeDtypeStr...  1.51 us
    pallas_call x1, Pallas kernels, score(): pl.pallas_call(functools.partial(score_body, count), name='score', out_sh...  1.47 us
  transfers between devices with their start and end apart: 10, of which 3 were waited for; matrix products, arithmetic and copies ran while one was open for 5% of the time, Pallas kernels for 15%

profile of v1, /device:TPU:4, one launch (start us, length us, event | category | flops | bytes accessed | tf_op | source)
XLA Modules:
  0.0 40.8 jit_solution(6294299804194006957)
XLA Ops:
  0.6 0.0 copy-start
  0.6 3.7 %collective-permute-start.4 = (bf16[64,1024]{1,0:T(8,128)(2,1)}, bf16[64,1024]{1,0:T(8,128)(2,1)S(1)}, u32[]{:S(2)}, u32[]{:S(2)}) collective-permute-start(bf16[64,1024]{1,0:T(8,128)(2,1)} %refs_0_.1), channel_id=1, source_target_pairs={{0,3},{1,2},{2,1},{3,0},{4,7},{5,6},{6,5},{7,4},{8,11},{9,10},{10,... | collective-permute-start | bytes 393224 | tf_op jit(solution)/shard_map/ppermute | solution.py:44
  4.3 0.0 collective-permute-start.5
  4.3 0.8 %collective-permute-start.6 = (bf16[64,1024]{1,0:T(8,128)(2,1)}, bf16[64,1024]{1,0:T(8,128)(2,1)S(1)}, u32[]{:S(2)}, u32[]{:S(2)}) collective-permute-start(bf16[64,1024]{1,0:T(8,128)(2,1)} %refs_0_.1), channel_id=1, source_target_pairs={{0,1},{1,0},{2,3},{3,2},{4,5},{5,4},{6,7},{7,6},{8,9},{9,8},{10,11... | collective-permute-start | bytes 393224 | tf_op jit(solution)/shard_map/ppermute | solution.py:44
  5.1 0.7 %broadcast_in_dim.16.pad_ref = s32[1,384]{1,0:T(1,128)S(1)} reshape(s32[384]{0:T(512)} %param.21) | data formatting | bytes 3072 | tf_op jit(solution)/shard_map/broadcast_in_dim | solution.py:91
  5.8 0.0 copy-start.2
  5.8 1.1 %copy-done.2 = bf16[384,1024]{1,0:T(8,128)(2,1)S(1)} copy-done((bf16[384,1024]{1,0:T(8,128)(2,1)S(1)}, bf16[384,1024]{1,0:T(8,128)(2,1)}, u32[]{:S(2)}) %copy-start.2) | copy-done | bytes 786456
  6.9 0.0 copy-start.3
  6.9 0.9 %copy-done.3 = bf16[1024,64]{0,1:T(8,128)(2,1)S(1)} copy-done((bf16[1024,64]{0,1:T(8,128)(2,1)S(1)}, bf16[1024,64]{0,1:T(8,128)(2,1)}, u32[]{:S(2)}) %copy-start.3) | copy-done | bytes 131096
  7.8 0.0 copy-start.4
  7.8 0.9 %copy-done.4 = bf16[1024,64]{0,1:T(8,128)(2,1)S(1)} copy-done((bf16[1024,64]{0,1:T(8,128)(2,1)S(1)}, bf16[1024,64]{0,1:T(8,128)(2,1)}, u32[]{:S(2)}) %copy-start.4) | copy-done | bytes 131096
  8.7 0.0 copy-start.5
  8.7 0.9 %copy-done.5 = bf16[1024,64]{0,1:T(8,128)(2,1)S(1)} copy-done((bf16[1024,64]{0,1:T(8,128)(2,1)S(1)}, bf16[1024,64]{0,1:T(8,128)(2,1)}, u32[]{:S(2)}) %copy-start.5) | copy-done | bytes 131096
  9.6 1.5 %project.1 = (bf16[384,64]{1,0:T(8,128)(2,1)S(1)}, bf16[144,384]{1,0:T(8,128)(2,1)S(1)}, bf16[144,256]{1,0:T(8,128)(2,1)S(1)}) custom-call(bf16[384,1024]{1,0:T(8,128)(2,1)S(1)} %copy-done.2, bf16[64,1024]{1,0:T(8,128)(2,1)S(1)} %bitcast.7, bf16[64,1024]{1,0:T(8,128)(2,1)S(1)} %bitcast.8, bf16[64,1024]{1,0:T(8,128)(2,1)S(1)} %bitcast.9, ...), custom_call_target="tpu_custom_call" | custom-call | flops 150994944 | bytes 786432 | tf_op jit(solution)/shard_map/project/pallas_call | solution.py:75
  11.1 1.9 %collective-permute-start = (bf16[144,256]{1,0:T(8,128)(2,1)S(1)}, bf16[144,256]{1,0:T(8,128)(2,1)S(1)}, u32[]{:S(2)}, u32[]{:S(2)}) collective-permute-start(bf16[144,256]{1,0:T(8,128)(2,1)S(1)} %get-tuple-element.13), channel_id=1, source_target_pairs={{0,4},{4,8},{8,12},{12,16},{16,20},{20,24},{24,28},{1,5},{5,9},{9,... | collective-permute-start | bytes 221192 | tf_op jit(solution)/shard_map/ppermute | solution.py:33
  13.1 0.7 %broadcast_in_dim.19.refs_8_ = s32[1,384]{1,0:T(1,128)S(1)} reshape(s32[384]{0:T(512)} %param.20) | data formatting | bytes 3072 | tf_op jit(solution)/shard_map/broadcast_in_dim | solution.py:245
  13.8 0.8 %dynamic_slice.6 = f32[256]{0:T(256)S(1)} dynamic-slice(f32[1024]{0:T(1024)} %param.16, s32[]{:T(128)S(6)} %select_n.4), dynamic_slice_sizes={256} | dynamic-slice | bytes 2052 | tf_op jit(solution)/shard_map/dynamic_slice | solution.py:282
  14.5 0.0 copy-done
  14.6 3.2 %collective-permute-done.prev_ref = bf16[144,256]{1,0:T(8,128)(2,1)S(1)} collective-permute-done((bf16[144,256]{1,0:T(8,128)(2,1)S(1)}, bf16[144,256]{1,0:T(8,128)(2,1)S(1)}, u32[]{:S(2)}, u32[]{:S(2)}) %collective-permute-start) | collective-permute-done | bytes 73760 | tf_op jit(solution)/shard_map/ppermute | solution.py:33
  17.7 1.2 %attend.1.refs_0_ = bf16[64,384]{1,0:T(8,128)(2,1)S(1)} custom-call(bf16[384,64]{1,0:T(8,128)(2,1)S(1)} %get-tuple-element.11.q_ref, bf16[144,384]{1,0:T(8,128)(2,1)S(1)} %get-tuple-element.12.own_ref, bf16[144,256]{1,0:T(8,128)(2,1)S(1)} %collective-permute-done.prev_ref), custom_call_target="tpu_custom_call" | custom-call | flops 50331648 | bytes 147456 | tf_op jit(solution)/shard_map/attend/pallas_call | solution.py:128
  18.9 3.7 %collective-permute-start.1 = (bf16[64,384]{1,0:T(8,128)(2,1)S(1)}, bf16[64,384]{1,0:T(8,128)(2,1)S(1)}, u32[]{:S(2)}, u32[]{:S(2)}) collective-permute-start(bf16[64,384]{1,0:T(8,128)(2,1)S(1)} %attend.1.refs_0_), channel_id=1, source_target_pairs={{0,3},{1,2},{2,1},{3,0},{4,7},{5,6},{6,5},{7,4},{8,11},{9,10},{10,... | collective-permute-start | bytes 147464 | tf_op jit(solution)/shard_map/ppermute | solution.py:44
  22.6 0.0 collective-permute-start.2
  22.6 0.0 collective-permute-done.4.refs_1_
  22.6 0.8 %collective-permute-start.3 = (bf16[64,384]{1,0:T(8,128)(2,1)S(1)}, bf16[64,384]{1,0:T(8,128)(2,1)S(1)}, u32[]{:S(2)}, u32[]{:S(2)}) collective-permute-start(bf16[64,384]{1,0:T(8,128)(2,1)S(1)} %attend.1.refs_0_), channel_id=1, source_target_pairs={{0,1},{1,0},{2,3},{3,2},{4,5},{5,4},{6,7},{7,6},{8,9},{9,8},{10,11... | collective-permute-start | bytes 147464 | tf_op jit(solution)/shard_map/ppermute | solution.py:44
  23.4 0.0 collective-permute-done.5.refs_2_
  23.4 0.0 collective-permute-done.6.refs_3_
  23.4 0.0 copy-start.1
  23.4 2.2 %copy-done.1 = bf16[2048,1024]{1,0:T(8,128)(2,1)S(1)} copy-done((bf16[2048,1024]{1,0:T(8,128)(2,1)S(1)}, bf16[2048,1024]{1,0:T(8,128)(2,1)}, u32[]{:S(2)}) %copy-start.1) | copy-done | bytes 4194328
  25.5 0.0 copy-start.6
  25.6 0.9 %copy-done.6 = bf16[64,1024]{1,0:T(8,128)(2,1)S(1)} copy-done((bf16[64,1024]{1,0:T(8,128)(2,1)S(1)}, bf16[64,1024]{1,0:T(8,128)(2,1)}, u32[]{:S(2)}) %copy-start.6) | copy-done | bytes 131096
  26.5 0.0 copy-start.7
  26.5 0.7 %copy-done.7 = s32[2048]{0:T(1024)S(1)} copy-done((s32[2048]{0:T(1024)S(1)}, s32[2048]{0:T(1024)}, u32[]{:S(2)}) %copy-start.7) | copy-done | bytes 8216
  27.1 0.0 copy-start.8
  27.2 0.7 %copy-done.8 = f32[1024]{0:T(1024)S(1)} copy-done((f32[1024]{0:T(1024)S(1)}, f32[1024]{0:T(1024)}, u32[]{:S(2)}) %copy-start.8) | copy-done | bytes 4120
  27.8 2.5 %premix.1 = (bf16[2048,256]{1,0:T(8,128)(2,1)S(1)}, bf16[1024,256]{1,0:T(8,128)(2,1)S(1)}, s32[2048,128]{1,0:T(8,128)S(1)}, f32[256,384]{1,0:T(8,128)S(1)}) custom-call(bf16[2048,1024]{1,0:T(8,128)(2,1)S(1)} %copy-done.1, bf16[64,1024]{1,0:T(8,128)(2,1)S(1)} %copy-done.6, bf16[64,1024]{1,0:T(8,128)(2,1)S(1)} %collective-permute-done.4.refs_1_, ...), custom_call_target="tpu_custom_call" | custom-call | flops 1073741824 | bytes 4194304 | tf_op jit(solution)/shard_map/premix/pallas_call | solution.py:167
  30.4 0.0 collective-permute-done.1.refs_1_
  30.4 0.0 collective-permute-done.2.refs_2_
  30.4 0.0 collective-permute-done.3.refs_3_
  30.4 1.5 %score.1 = (f32[4,384]{1,0:T(4,128)S(1)}, f32[256,384]{1,0:T(8,128)S(1)}) custom-call(bf16[64,384]{1,0:T(8,128)(2,1)S(1)} %attend.1.refs_0_, bf16[64,384]{1,0:T(8,128)(2,1)S(1)} %collective-permute-done.1.refs_1_, bf16[64,384]{1,0:T(8,128)(2,1)S(1)} %collective-permute-done.2.refs_2_, bf16[64,384]{1,0:T(8,128)(2,1)S(1)} %collective-permute-done.3.refs_3_, ...), custom_call_target="tpu_custom_call" | custom-call | flops 603979776 | bytes 1048576 | tf_op jit(solution)/shard_map/score/pallas_call | solution.py:233
  31.9 3.7 %collective-permute-start.7 = (f32[4,384]{1,0:T(4,128)S(1)}, f32[4,384]{1,0:T(4,128)S(1)}, u32[]{:S(2)}, u32[]{:S(2)}) collective-permute-start(f32[4,384]{1,0:T(4,128)S(1)} %get-tuple-element.19), channel_id=1, source_target_pairs={{0,3},{1,2},{2,1},{3,0},{4,7},{5,6},{6,5},{7,4},{8,11},{9,10},{10,... | collective-permute-start | bytes 18440 | tf_op jit(solution)/shard_map/ppermute | solution.py:44
  35.6 0.0 collective-permute-start.8
  35.6 0.8 %collective-permute-start.9 = (f32[4,384]{1,0:T(4,128)S(1)}, f32[4,384]{1,0:T(4,128)S(1)}, u32[]{:S(2)}, u32[]{:S(2)}) collective-permute-start(f32[4,384]{1,0:T(4,128)S(1)} %get-tuple-element.19), channel_id=1, source_target_pairs={{0,1},{1,0},{2,3},{3,2},{4,5},{5,4},{6,7},{7,6},{8,9},{9,8},{10,11... | collective-permute-start | bytes 18440 | tf_op jit(solution)/shard_map/ppermute | solution.py:44
  36.4 0.8 %finish.1 = bf16[384,256]{1,0:T(8,128)(2,1)} custom-call(f32[256,384]{1,0:T(8,128)S(1)} %get-tuple-element.18.user_ref, f32[1,256]{1,0:T(1,128)S(1)} %bitcast.11), custom_call_target="tpu_custom_call" | custom-call | flops 196608 | bytes 589824 | tf_op jit(solution)/shard_map/finish/pallas_call | solution.py:254
  37.2 0.2 collective-permute-done.7
  37.4 2.7 %collective-permute-done.8 = f32[4,384]{1,0:T(4,128)S(1)} collective-permute-done((f32[4,384]{1,0:T(4,128)S(1)}, f32[4,384]{1,0:T(4,128)S(1)}, u32[]{:S(2)}, u32[]{:S(2)}) %collective-permute-start.8) | collective-permute-done | bytes 6176 | tf_op jit(solution)/shard_map/ppermute | solution.py:44
  40.1 0.0 collective-permute-done.9
  40.1 0.1 slice_reduce_fusion.7
  40.2 0.6 %add_subtract_fusion = f32[384]{0:T(512)} fusion(f32[384]{0:T(512)S(1)} %get-tuple-element.22, f32[384]{0:T(512)S(1)} %get-tuple-element.28, f32[384]{0:T(512)S(1)} %get-tuple-element.27, f32[384]{0:T(512)S(1)} %get-tuple-element.26, f32[384]{0:T(512)S(1)} %get-tuple-element.25, f32[384]{0:T(512)S(1)} %get-tuple-element.24, f32[384]{0:T(512)S(1)} %get-tuple-element.23, ...), kind=kLoop, calls=%fused_computation | loop fusion | flops 7296 | bytes 15360 | tf_op jit(solution)/shard_map/sub | solution.py:294
  (1 shorter events, 0.0 us)
Async XLA Ops:
  0.6 13.9 %copy-start = (bf16[384,1024]{1,0:T(8,128)(2,1)S(1)}, bf16[384,1024]{1,0:T(8,128)(2,1)}, u32[]{:S(2)}) copy-start(bf16[384,1024]{1,0:T(8,128)(2,1)} %param.18) | copy-start | bytes 2359300
  0.6 21.9 %collective-permute-start.4 = (bf16[64,1024]{1,0:T(8,128)(2,1)}, bf16[64,1024]{1,0:T(8,128)(2,1)S(1)}, u32[]{:S(2)}, u32[]{:S(2)}) collective-permute-start(bf16[64,1024]{1,0:T(8,128)(2,1)} %refs_0_.1), channel_id=1, source_target_pairs={{0,3},{1,2},{2,1},{3,0},{4,7},{5,6},{6,5},{7,4},{8,11},{9,10},{10,... | collective-permute-start | bytes 393224 | tf_op jit(solution)/shard_map/ppermute | solution.py:44
  4.3 19.0 %collective-permute-start.5 = (bf16[64,1024]{1,0:T(8,128)(2,1)}, bf16[64,1024]{1,0:T(8,128)(2,1)S(1)}, u32[]{:S(2)}, u32[]{:S(2)}) collective-permute-start(bf16[64,1024]{1,0:T(8,128)(2,1)} %refs_0_.1), channel_id=1, source_target_pairs={{0,2},{1,3},{2,0},{3,1},{4,6},{5,7},{6,4},{7,5},{8,10},{9,11},{10,... | collective-permute-start | bytes 393224 | tf_op jit(solution)/shard_map/ppermute | solution.py:44
  4.3 19.0 %collective-permute-start.6 = (bf16[64,1024]{1,0:T(8,128)(2,1)}, bf16[64,1024]{1,0:T(8,128)(2,1)S(1)}, u32[]{:S(2)}, u32[]{:S(2)}) collective-permute-start(bf16[64,1024]{1,0:T(8,128)(2,1)} %refs_0_.1), channel_id=1, source_target_pairs={{0,1},{1,0},{2,3},{3,2},{4,5},{5,4},{6,7},{7,6},{8,9},{9,8},{10,11... | collective-permute-start | bytes 393224 | tf_op jit(solution)/shard_map/ppermute | solution.py:44
  5.8 1.1 %copy-start.2 = (bf16[384,1024]{1,0:T(8,128)(2,1)S(1)}, bf16[384,1024]{1,0:T(8,128)(2,1)}, u32[]{:S(2)}) copy-start(bf16[384,1024]{1,0:T(8,128)(2,1)} %hist_hbm.1) | copy-start | bytes 2359300
  6.9 0.9 %copy-start.3 = (bf16[1024,64]{0,1:T(8,128)(2,1)S(1)}, bf16[1024,64]{0,1:T(8,128)(2,1)}, u32[]{:S(2)}) copy-start(bf16[1024,64]{0,1:T(8,128)(2,1)} %param.12) | copy-start | bytes 393220
  7.8 0.9 %copy-start.4 = (bf16[1024,64]{0,1:T(8,128)(2,1)S(1)}, bf16[1024,64]{0,1:T(8,128)(2,1)}, u32[]{:S(2)}) copy-start(bf16[1024,64]{0,1:T(8,128)(2,1)} %param.13) | copy-start | bytes 393220
  8.7 0.9 %copy-start.5 = (bf16[1024,64]{0,1:T(8,128)(2,1)S(1)}, bf16[1024,64]{0,1:T(8,128)(2,1)}, u32[]{:S(2)}) copy-start(bf16[1024,64]{0,1:T(8,128)(2,1)} %param.14) | copy-start | bytes 393220
  11.1 6.6 %collective-permute-start = (bf16[144,256]{1,0:T(8,128)(2,1)S(1)}, bf16[144,256]{1,0:T(8,128)(2,1)S(1)}, u32[]{:S(2)}, u32[]{:S(2)}) collective-permute-start(bf16[144,256]{1,0:T(8,128)(2,1)S(1)} %get-tuple-element.13), channel_id=1, source_target_pairs={{0,4},{4,8},{8,12},{12,16},{16,20},{20,24},{24,28},{1,5},{5,9},{9,... | collective-permute-start | bytes 221192 | tf_op jit(solution)/shard_map/ppermute | solution.py:33
  18.9 11.5 %collective-permute-start.1 = (bf16[64,384]{1,0:T(8,128)(2,1)S(1)}, bf16[64,384]{1,0:T(8,128)(2,1)S(1)}, u32[]{:S(2)}, u32[]{:S(2)}) collective-permute-start(bf16[64,384]{1,0:T(8,128)(2,1)S(1)} %attend.1.refs_0_), channel_id=1, source_target_pairs={{0,3},{1,2},{2,1},{3,0},{4,7},{5,6},{6,5},{7,4},{8,11},{9,10},{10,... | collective-permute-start | bytes 147464 | tf_op jit(solution)/shard_map/ppermute | solution.py:44
  22.6 7.8 %collective-permute-start.2 = (bf16[64,384]{1,0:T(8,128)(2,1)S(1)}, bf16[64,384]{1,0:T(8,128)(2,1)S(1)}, u32[]{:S(2)}, u32[]{:S(2)}) collective-permute-start(bf16[64,384]{1,0:T(8,128)(2,1)S(1)} %attend.1.refs_0_), channel_id=1, source_target_pairs={{0,2},{1,3},{2,0},{3,1},{4,6},{5,7},{6,4},{7,5},{8,10},{9,11},{10,... | collective-permute-start | bytes 147464 | tf_op jit(solution)/shard_map/ppermute | solution.py:44
  22.6 7.8 %collective-permute-start.3 = (bf16[64,384]{1,0:T(8,128)(2,1)S(1)}, bf16[64,384]{1,0:T(8,128)(2,1)S(1)}, u32[]{:S(2)}, u32[]{:S(2)}) collective-permute-start(bf16[64,384]{1,0:T(8,128)(2,1)S(1)} %attend.1.refs_0_), channel_id=1, source_target_pairs={{0,1},{1,0},{2,3},{3,2},{4,5},{5,4},{6,7},{7,6},{8,9},{9,8},{10,11... | collective-permute-start | bytes 147464 | tf_op jit(solution)/shard_map/ppermute | solution.py:44
  23.4 2.2 %copy-start.1 = (bf16[2048,1024]{1,0:T(8,128)(2,1)S(1)}, bf16[2048,1024]{1,0:T(8,128)(2,1)}, u32[]{:S(2)}) copy-start(bf16[2048,1024]{1,0:T(8,128)(2,1)} %neg_ref.1) | copy-start | bytes 12582916
  25.5 0.9 %copy-start.6 = (bf16[64,1024]{1,0:T(8,128)(2,1)S(1)}, bf16[64,1024]{1,0:T(8,128)(2,1)}, u32[]{:S(2)}) copy-start(bf16[64,1024]{1,0:T(8,128)(2,1)} %refs_0_.1) | copy-start | bytes 393220
  26.5 0.7 %copy-start.7 = (s32[2048]{0:T(1024)S(1)}, s32[2048]{0:T(1024)}, u32[]{:S(2)}) copy-start(s32[2048]{0:T(1024)} %param.19) | copy-start | bytes 24580
  27.1 0.7 %copy-start.8 = (f32[1024]{0:T(1024)S(1)}, f32[1024]{0:T(1024)}, u32[]{:S(2)}) copy-start(f32[1024]{0:T(1024)} %param.16) | copy-start | bytes 12292
  31.9 5.5 %collective-permute-start.7 = (f32[4,384]{1,0:T(4,128)S(1)}, f32[4,384]{1,0:T(4,128)S(1)}, u32[]{:S(2)}, u32[]{:S(2)}) collective-permute-start(f32[4,384]{1,0:T(4,128)S(1)} %get-tuple-element.19), channel_id=1, source_target_pairs={{0,3},{1,2},{2,1},{3,0},{4,7},{5,6},{6,5},{7,4},{8,11},{9,10},{10,... | collective-permute-start | bytes 18440 | tf_op jit(solution)/shard_map/ppermute | solution.py:44
  35.6 4.5 %collective-permute-start.8 = (f32[4,384]{1,0:T(4,128)S(1)}, f32[4,384]{1,0:T(4,128)S(1)}, u32[]{:S(2)}, u32[]{:S(2)}) collective-permute-start(f32[4,384]{1,0:T(4,128)S(1)} %get-tuple-element.19), channel_id=1, source_target_pairs={{0,2},{1,3},{2,0},{3,1},{4,6},{5,7},{6,4},{7,5},{8,10},{9,11},{10,... | collective-permute-start | bytes 18440 | tf_op jit(solution)/shard_map/ppermute | solution.py:44
  35.6 4.5 %collective-permute-start.9 = (f32[4,384]{1,0:T(4,128)S(1)}, f32[4,384]{1,0:T(4,128)S(1)}, u32[]{:S(2)}, u32[]{:S(2)}) collective-permute-start(f32[4,384]{1,0:T(4,128)S(1)} %get-tuple-element.19), channel_id=1, source_target_pairs={{0,1},{1,0},{2,3},{3,2},{4,5},{5,4},{6,7},{7,6},{8,9},{9,8},{10,11... | collective-permute-start | bytes 18440 | tf_op jit(solution)/shard_map/ppermute | solution.py:44

commit v2 on v1

--- a/solution.py
+++ b/solution.py
@@ -6,6 +6,7 @@
 from jax.experimental import pallas as pl
 from jax.experimental.pallas import tpu as pltpu
 from jax.sharding import PartitionSpec as P
+
 
 HD = 64
 WIN = 256
@@ -16,7 +17,11 @@
 F32 = jnp.float32
 BF16 = jnp.bfloat16
 WHOLE = pl.BlockSpec(memory_space=pltpu.VMEM)
-RAW = pl.BlockSpec(memory_space=pl.ANY)
+RAW = pl.BlockSpec(memory_space=pltpu.HBM)
+
+
+def stay(*arrays):
+    return [pltpu.with_memory_space_constraint(a, pltpu.HBM) for a in arrays]
 
 
 def dot_last(a, b):
@@ -36,30 +41,70 @@
 def partners(axis):
     count = lax.axis_size(axis)
     if count & (count - 1) == 0:
-        return [[(i, i ^ k) for i in range(count)] for k in range(count - 1, 0, -1)]
-    return [[(i, (i + k) % count) for i in range(count)] for k in range(count - 1, 0, -1)]
+        return [[(i, i ^ k) for i in range(count)] for k in range(1, count)]
+    return [[(i, (i + k) % count) for i in range(count)] for k in range(1, count)]
 
 
 def from_all(shard, axis):
-    return [shard] + [lax.ppermute(shard, axis, pairs) for pairs in partners(axis)]
-
-
-def project_body(hist_hbm, wq_ref, wk_ref, wv_ref, pad_ref, q_ref, own_ref, edge_ref, hist, sems):
-    rows, width = hist.shape
-    cols = wq_ref.shape[0]
+    pieces = [shard]
+    for pairs in partners(axis):
+        pieces.append(lax.ppermute(shard, axis, pairs))
+    return pieces
+
+
+def fetch_in_pairs(shard):
+    count, pairs_of = lax.axis_size("head"), lax.axis_size("seq")
+    if count & (count - 1) or pairs_of % 2:
+        return from_all(shard, "head")[1:]
+    far = []
+    for odd in range(1, count, 2):
+        moves = [(odd, odd + 1)[s % 2] for s in range(pairs_of)]
+        route = [
+            (s * count + h, s * count + (h ^ k))
+            for s, k in enumerate(moves)
+            if k < count
+            for h in range(count)
+        ]
+        far.append(lax.ppermute(shard, ("seq", "head"), route))
+    return far
+
+
+def swap_in_pairs(far, count):
+    pairs_of = lax.axis_size("seq")
+    if count & (count - 1) or pairs_of % 2:
+        return []
+    near = []
+    for n, piece in enumerate(far):
+        both = 2 * n + 2 < count
+        route = [(s, s ^ 1) for s in range(pairs_of) if both or s % 2 == 0]
+        near.append(lax.ppermute(piece, "seq", route))
+    return near
+
+
+def project_body(hist_hbm, wq_hbm, wk_hbm, wv_hbm, pad_hbm, q_ref, own_ref, edge_ref, hist, weights, pad_ref, sems):
+    rows, _ = hist.shape
+    cols = wq_hbm.shape[0]
     step = LANES
+    starts = list(range(0, rows, step))[::-1]
     copies = []
-    for n, start in enumerate(range(0, rows, step)):
+    for n, source in enumerate((wq_hbm, wk_hbm, wv_hbm)):
+        copies.append(pltpu.make_async_copy(source, weights.at[pl.ds(n * cols, cols)], sems.at[n]))
+    for n, start in enumerate(starts):
         part = pl.ds(start, step)
-        copies.append(pltpu.make_async_copy(hist_hbm.at[part], hist.at[part], sems.at[n]))
-        copies[-1].start()
-    weights = jnp.concatenate([wq_ref[...], wk_ref[...], wv_ref[...]], 0)
-    flags = jnp.broadcast_to(pad_ref[...], (FLAG_ROWS, rows)).astype(F32).astype(BF16)
+        copies.append(pltpu.make_async_copy(hist_hbm.at[part], hist.at[part], sems.at[3 + n]))
+    copies.append(pltpu.make_async_copy(pad_hbm, pad_ref, sems.at[3 + len(starts)]))
+    for copy in copies:
+        copy.start()
+    copies[-1].wait()
+    pad = jnp.concatenate([pad_ref[n : n + 1, :] for n in range(rows // LANES)], 1)
+    flags = jnp.broadcast_to(pad, (FLAG_ROWS, rows)).astype(F32).astype(BF16)
     own_ref[2 * cols :, :] = flags
     edge_ref[2 * cols :, :] = flags[:, rows - WIN :]
-    for n, start in enumerate(range(0, rows, step)):
-        copies[n].wait()
-        out = dot_last(hist[start : start + step, :], weights)
+    for copy in copies[:3]:
+        copy.wait()
+    for n, start in enumerate(starts):
+        copies[3 + n].wait()
+        out = dot_last(hist[start : start + step, :], weights[...])
         q_ref[start : start + step, :] = out[:, :cols].astype(BF16)
         kv = out[:, cols:].T.astype(BF16)
         own_ref[: 2 * cols, start : start + step] = kv
@@ -80,15 +125,17 @@
             jax.ShapeDtypeStruct((tall, rows), BF16),
             jax.ShapeDtypeStruct((tall, WIN), BF16),
         ),
-        in_specs=[RAW, WHOLE, WHOLE, WHOLE, WHOLE],
+        in_specs=[RAW] * 5,
         out_specs=(WHOLE, WHOLE, WHOLE),
         scratch_shapes=[
             pltpu.VMEM((rows, width), BF16),
-            pltpu.SemaphoreType.DMA((rows // LANES,)),
+            pltpu.VMEM((3 * cols, width), BF16),
+            pltpu.VMEM((rows // LANES, LANES), jnp.int32),
+            pltpu.SemaphoreType.DMA((4 + rows // LANES,)),
         ],
         compiler_params=pltpu.CompilerParams(vmem_limit_bytes=8 * MIB),
         cost_estimate=pl.CostEstimate(flops=6 * rows * width * cols, bytes_accessed=2 * rows * width, transcendentals=0),
-    )(history, w_query.T, w_key.T, w_value.T, pad_mask[None, :])
+    )(*stay(history, w_query.T, w_key.T, w_value.T, pad_mask.reshape(-1, LANES)))
 
 
 def attend_body(q_ref, own_ref, prev_ref, out_ref):
@@ -136,62 +183,126 @@
     )(query, own, prev)
 
 
-def premix_body(count, neg_ref, *refs):
-    w_refs = refs[:count]
-    gain_ref, gain_here, pos_ref, ids_ref, mix_ref, turned_ref, id_ref, pos_out, scaled = refs[count:]
-
-    @pl.when(pl.program_id(0) == 0)
-    def _():
-        gain = gain_ref[...]
-        for n in range(count):
-            piece = w_refs[n][...].astype(F32)
-            tall = piece.shape[0]
-            scaled[n * tall : (n + 1) * tall, :] = (piece * gain).astype(BF16)
-        whole = jnp.concatenate([ref[...].astype(F32) for ref in w_refs], 0)
-        turned_ref[...] = whole.T.astype(BF16)
-        for n in range(ids_ref.shape[0]):
-            line = jnp.broadcast_to(ids_ref[n : n + 1, :], (LANES, LANES))
-            id_ref[n * LANES : (n + 1) * LANES, :] = line.T
-        pos_out[...] = (pos_ref[...].astype(F32) * gain_here[...]).T
-
-    mix_ref[...] = dot_last(neg_ref[...], scaled[...]).astype(BF16)
-
-
-def premix(neg_emb, pieces, gain, gain_here, pos_here, neg_ids):
+def prepare_body(pos_hbm, gain_hbm, ids_hbm, target_hbm, id_ref, pos_out, gain_out, target_out, pos, gain, ids_ref, target_ref, sems):
+    rows, share = pos.shape
+    here = pl.ds(0, share)
+    if pos_hbm.shape[1] != share:
+        here = pl.ds(pl.multiple_of(lax.axis_index("head") * share, share), share)
+    copy_pos = pltpu.make_async_copy(pos_hbm.at[:, here], pos, sems.at[0])
+    copy_gain = pltpu.make_async_copy(gain_hbm.at[:, here], gain, sems.at[1])
+    copy_ids = pltpu.make_async_copy(ids_hbm, ids_ref, sems.at[2])
+    copy_target = pltpu.make_async_copy(target_hbm, target_ref, sems.at[3])
+    copy_ids.start()
+    copy_target.start()
+    copy_pos.start()
+    copy_gain.start()
+    copy_ids.wait()
+    copy_target.wait()
+    target_out[...] = jnp.concatenate([target_ref[n : n + 1, :] for n in range(rows // LANES)], 1)
+    for n in range(ids_ref.shape[0]):
+        line = jnp.broadcast_to(ids_ref[n : n + 1, :], (LANES, LANES))
+        id_ref[n * LANES : (n + 1) * LANES, :] = line.T
+    copy_pos.wait()
+    copy_gain.wait()
+    gain_out[...] = gain[...]
+    pos_out[...] = (pos[...].astype(F32) * gain[...]).T
+
+
+def prepare(pos_emb, norm_gain, neg_ids, target_ids, share):
+    rows, _ = pos_emb.shape
+    negs = neg_ids.shape[0]
+    if share % LANES:
+        pos_emb = lax.dynamic_slice_in_dim(pos_emb, lax.axis_index("head") * share, share, 1)
+        norm_gain = lax.dynamic_slice_in_dim(norm_gain, lax.axis_index("head") * share, share, 0)
+    return pl.pallas_call(
+        prepare_body,
+        name="prepare",
+        out_shape=(
+            jax.ShapeDtypeStruct((negs, LANES), jnp.int32),
+            jax.ShapeDtypeStruct((share, rows), F32),
+            jax.ShapeDtypeStruct((1, share), F32),
+            jax.ShapeDtypeStruct((1, rows), jnp.int32),
+        ),
+        in_specs=[RAW] * 4,
+        out_specs=(WHOLE,) * 4,
+        scratch_shapes=[
+            pltpu.VMEM((rows, share), BF16),
+            pltpu.VMEM((1, share), F32),
+            pltpu.VMEM((negs // LANES, LANES), jnp.int32),
+            pltpu.VMEM((rows // LANES, LANES), jnp.int32),
+            pltpu.SemaphoreType.DMA((4,)),
+        ],
+        compiler_params=pltpu.CompilerParams(vmem_limit_bytes=8 * MIB),
+        cost_estimate=pl.CostEstimate(flops=rows * share, bytes_accessed=2 * rows * share, transcendentals=0),
+    )(*stay(pos_emb, norm_gain[None, :], neg_ids.reshape(-1, LANES), target_ids.reshape(-1, LANES)))
+
+
+def premix_body(count, paired, neg_hbm, own_hbm, gain_hbm, *refs):
+    n_far = count // 2 if paired else count - 1
+    far, near = refs[:n_far], refs[n_far : 2 * n_far if paired else n_far]
+    mix_ref, turned_ref, scaled, negs, own, gain, sems = refs[n_far + len(near) :]
+    total, _ = negs.shape
+    tall = own.shape[0]
+    block = 256
+    copies = [
+        pltpu.make_async_copy(own_hbm, own, sems.at[0]),
+        pltpu.make_async_copy(gain_hbm, gain, sems.at[1]),
+    ]
+    for n, start in enumerate(range(0, total, block)):
+        part = pl.ds(start, block)
+        copies.append(pltpu.make_async_copy(neg_hbm.at[part], negs.at[part], sems.at[2 + n]))
+    for copy in copies:
+        copy.start()
+    first = lax.axis_index("seq") % 2 == 0
+    copies[0].wait()
+    copies[1].wait()
+    for k in range(count):
+        if k == 0:
+            piece = own[...].astype(F32)
+        elif paired:
+            mine, theirs = far[(k - 1) // 2][...].astype(F32), near[(k - 1) // 2][...].astype(F32)
+            piece = jnp.where(first, mine, theirs) if k % 2 else jnp.where(first, theirs, mine)
+        else:
+            piece = far[k - 1][...].astype(F32)
+        scaled[k * tall : (k + 1) * tall, :] = (piece * gain[...]).astype(BF16)
+        if k % 2:
+            pair = jnp.concatenate([last, piece], 0)
+            turned_ref[:, (k - 1) * tall : (k + 1) * tall] = pair.T.astype(BF16)
+        last = piece
+    for n, start in enumerate(range(0, total, block)):
+        copies[2 + n].wait()
+        mix_ref[start : start + block, :] = dot_last(negs[start : start + block, :], scaled[...]).astype(BF16)
+
+
+def premix(neg_emb, own, far, near, norm_gain):
     negs, width = neg_emb.shape
-    count = len(pieces)
-    deep = count * pieces[0].shape[0]
-    rows, share = pos_here.shape
-    block = 512
-    const = lambda shape: pl.BlockSpec(shape, lambda i: (0, 0))
-    return pl.pallas_call(
-        functools.partial(premix_body, count),
+    count = lax.axis_size("head")
+    tall = own.shape[0]
+    deep = count * tall
+    return pl.pallas_call(
+        functools.partial(premix_body, count, bool(near)),
         name="premix",
-        grid=(negs // block,),
         out_shape=(
             jax.ShapeDtypeStruct((negs, deep), BF16),
             jax.ShapeDtypeStruct((width, deep), BF16),
-            jax.ShapeDtypeStruct((negs, LANES), jnp.int32),
-            jax.ShapeDtypeStruct((share, rows), F32),
         ),
-        in_specs=[pl.BlockSpec((block, width), lambda i: (i, 0))]
-        + [const(p.shape) for p in pieces]
-        + [const((1, width)), const((1, share)), const((rows, share)), const((negs // LANES, LANES))],
-        out_specs=(
-            pl.BlockSpec((block, deep), lambda i: (i, 0)),
-            const((width, deep)),
-            const((negs, LANES)),
-            const((share, rows)),
-        ),
-        scratch_shapes=[pltpu.VMEM((deep, width), BF16)],
+        in_specs=[RAW, RAW, RAW] + [WHOLE] * (len(far) + len(near)),
+        out_specs=(WHOLE, WHOLE),
+        scratch_shapes=[
+            pltpu.VMEM((deep, width), BF16),
+            pltpu.VMEM((negs, width), BF16),
+            pltpu.VMEM((tall, width), BF16),
+            pltpu.VMEM((1, width), F32),
+            pltpu.SemaphoreType.DMA((2 + negs // 256,)),
+        ],
         compiler_params=pltpu.CompilerParams(vmem_limit_bytes=28 * MIB),
         cost_estimate=pl.CostEstimate(flops=2 * negs * width * deep, bytes_accessed=2 * negs * width, transcendentals=0),
-    )(neg_emb, *pieces, gain[None, :], gain_here[None, :], pos_here, neg_ids.reshape(-1, LANES))
+    )(*stay(neg_emb, own, norm_gain[None, :]), *far, *near)
 
 
 def score_body(count, *refs):
     o_refs = refs[:count]
-    mix_ref, turned_ref, id_ref, pos_ref, target_ref, here_ref, stat_ref, user_ref, attn, logits = refs[count:]
+    mix_ref, turned_ref, id_ref, pos_ref, target_ref, stat_ref, user_ref, attn, logits = refs[count:]
     width, rows = attn.shape
     share = user_ref.shape[0]
     negs = mix_ref.shape[0]
@@ -203,7 +314,7 @@
         attn[start : start + block, :] = part
         total += jnp.sum((part * part).reshape(block // 8, 8, rows), 0)
     scale = lax.rsqrt(jnp.sum(total, 0, keepdims=True) / width + 1e-05)
-    here = pl.multiple_of(here_ref[0] * share, share)
+    here = pl.multiple_of(lax.axis_index("head") * share, share)
     user = attn[pl.ds(here, share), :] * scale
     user_ref[...] = user
     pos = jnp.sum(user * pos_ref[...], 0, keepdims=True)
@@ -225,7 +336,7 @@
     stat_ref[...] = jnp.concatenate([top, mass, pos, pos], 0)
 
 
-def score(heads, mix, turned, id_cols, pos_turned, target_ids, here):
+def score(heads, mix, turned, id_cols, pos_turned, target):
     count = len(heads)
     negs, deep = mix.shape
     width = turned.shape[0]
@@ -237,12 +348,12 @@
             jax.ShapeDtypeStruct((4, rows), F32),
             jax.ShapeDtypeStruct((share, rows), F32),
         ),
-        in_specs=[WHOLE] * (count + 5) + [pl.BlockSpec(memory_space=pltpu.SMEM)],
+        in_specs=[WHOLE] * (count + 5),
         out_specs=(WHOLE, WHOLE),
         scratch_shapes=[pltpu.VMEM((width, rows), F32), pltpu.VMEM((negs, rows), F32)],
         compiler_params=pltpu.CompilerParams(vmem_limit_bytes=28 * MIB),
         cost_estimate=pl.CostEstimate(flops=2 * rows * deep * (negs + width), bytes_accessed=2 * negs * deep, transcendentals=negs * rows),
-    )(*heads, mix, turned, id_cols, pos_turned, target_ids[None, :], here)
+    )(*heads, mix, turned, id_cols, pos_turned, target)
 
 
 def finish_body(user_ref, gain_ref, out_ref):
@@ -259,7 +370,7 @@
         out_specs=WHOLE,
         compiler_params=pltpu.CompilerParams(vmem_limit_bytes=8 * MIB),
         cost_estimate=pl.CostEstimate(flops=2 * rows * share, bytes_accessed=6 * rows * share, transcendentals=0),
-    )(user, gain_here[None, :])
+    )(user, gain_here)
 
 
 def on_device(
@@ -276,16 +387,16 @@
     pad_mask,
 ):
     width = history.shape[1]
-    share = width // lax.axis_size("head")
-    me = lax.axis_index("head")
-    pos_here = lax.dynamic_slice_in_dim(pos_emb, me * share, share, 1)
-    gain_here = lax.dynamic_slice_in_dim(norm_gain, me * share, share, 0)
-    pieces = from_all(w_out, "head")
+    count = lax.axis_size("head")
     query, own, edge = project(history, w_query, w_key, w_value, pad_mask)
     prev = from_behind(edge, "seq", 1)
-    heads = from_all(attend(query, own, prev), "head")
-    mix, turned, id_cols, pos_turned = premix(neg_emb, pieces, norm_gain, gain_here, pos_here, neg_ids)
-    stats, user = score(heads, mix, turned, id_cols, pos_turned, target_ids, me[None].astype(jnp.int32))
+    far = fetch_in_pairs(w_out)
+    id_cols, pos_turned, gain_here, target = prepare(pos_emb, norm_gain, neg_ids, target_ids, width // count)
+    mine = attend(query, own, prev)
+    heads = from_all(mine, "head")
+    near = swap_in_pairs(far, count)
+    mix, turned = premix(neg_emb, w_out, far, near, norm_gain)
+    stats, user = score(heads, mix, turned, id_cols, pos_turned, target)
     all_stats = from_all(stats, "head")
     user_share = finish(user, gain_here)
     pos_logit = functools.reduce(jnp.add, [s[2] for s in all_stats])

time: 41.2 us -> 41.9 us (1.017)
  local copies, waits for them, and re-layouts: 10.5 us -> 0 us
  Pallas kernels: 7.54 us -> 12.3 us
  waiting for transfers between devices: 6.08 us -> 9.75 us
  starting transfers between devices: 15.3 us -> 18.1 us
    unnamed x18 -> x0, local copies, waits for them, and re-layouts: 8.33 us -> none
    pallas_call x1 -> x2, Pallas kernels: 2.54 us -> 6.11 us  [the longest x1 4.86 us: premix(): pl.pallas_call(functools.partial(premix_body, count, bool(near)), name='p...]
    ppermute x9 -> x10, waiting for transfers between devices: 2.92 us -> 6.36 us  [the longest x2 4.57 us: fetch_in_pairs(): far.append(lax.ppermute(shard, ('seq', 'head'), route))]
    ppermute x9 -> x10, starting transfers between devices: 13.4 us -> 16.2 us  [the longest x6 8.91 us: from_all(): pieces.append(lax.ppermute(shard, axis, pairs))]
    broadcast_in_dim x2 -> x0, local copies, waits for them, and re-layouts: 1.37 us -> none  [the longest x1 0.69 us: score(): target_ids[None, :]]
    pallas_call x1, Pallas kernels: 1.51 us -> 2.62 us  [project(): pl.pallas_call(project_body, name='project', out_shape=(jax.ShapeDtypeStr...]
    dynamic_slice x2 -> x0, local copies, waits for them, and re-layouts: 0.79 us -> none  [the longest x1 0.76 us: on_device(): gain_here = lax.dynamic_slice_in_dim(norm_gain, me * share, share, 0)]
  transfers between devices with their start and end apart: 10 -> 11, of which waited for: 3 -> 5; matrix products, arithmetic and copies ran while one was open for 5% -> 0% of each run, Pallas kernels for 15% -> 26%
where the time goes in v2:
time: 41.9 us; the launch traced here: 41.6 us
  starting transfers between devices  18.1 us (43%)
  Pallas kernels  12.3 us (29%)
  waiting for transfers between devices  9.75 us (23%)
  between operations  0.72 us (2%)
  other arithmetic  0.66 us (2%)
    ppermute x6, starting transfers between devices, from_all(): pieces.append(lax.ppermute(shard, axis, pairs))  8.91 us
    ppermute x2, starting transfers between devices, fetch_in_pairs(): far.append(lax.ppermute(shard, ('seq', 'head'), route))  6.01 us
    pallas_call x1, Pallas kernels, premix(): pl.pallas_call(functools.partial(premix_body, count, bool(near)), name='p...  4.86 us
    ppermute x2, waiting for transfers between devices, fetch_in_pairs(): far.append(lax.ppermute(shard, ('seq', 'head'), route))  4.57 us
    ppermute x1, waiting for transfers between devices, from_behind(): return lax.ppermute(shard, axis, pairs)  3.39 us
    pallas_call x1, Pallas kernels, project(): pl.pallas_call(project_body, name='project', out_shape=(jax.ShapeDtypeStr...  2.62 us
    ppermute x1, starting transfers between devices, from_behind(): return lax.ppermute(shard, axis, pairs)  1.92 us
    ppermute x6, waiting for transfers between devices, from_all(): pieces.append(lax.ppermute(shard, axis, pairs))  1.78 us
  transfers between devices with their start and end apart: 11, of which 5 were waited for; matrix products, arithmetic and copies ran while one was open for 0% of the time, Pallas kernels for 26%

profile of v2, /device:TPU:4, one launch (start us, length us, event | category | flops | bytes accessed | tf_op | source)
XLA Modules:
  0.0 41.6 jit_solution(13196711959116147305)
XLA Ops:
  0.6 1.6 %collective-permute-start.4 = (bf16[64,1024]{1,0:T(8,128)(2,1)}, bf16[64,1024]{1,0:T(8,128)(2,1)S(1)}, u32[]{:S(2)}, u32[]{:S(2)}) collective-permute-start(bf16[64,1024]{1,0:T(8,128)(2,1)} %own_hbm.1), channel_id=1, source_target_pairs={{0,1},{1,0},{2,3},{3,2},{4,6},{5,7},{6,4},{7,5},{8,9},{9,8},{10,11... | collective-permute-start | bytes 393224 | tf_op jit(solution)/shard_map/ppermute | solution.py:68
  2.3 4.4 %collective-permute-start.5 = (bf16[64,1024]{1,0:T(8,128)(2,1)}, bf16[64,1024]{1,0:T(8,128)(2,1)S(1)}, u32[]{:S(2)}, u32[]{:S(2)}) collective-permute-start(bf16[64,1024]{1,0:T(8,128)(2,1)} %own_hbm.1), channel_id=1, source_target_pairs={{0,3},{1,2},{2,1},{3,0},{8,11},{9,10},{10,9},{11,8},{16,19},{17,18... | collective-permute-start | bytes 393224 | tf_op jit(solution)/shard_map/ppermute | solution.py:68
  6.7 0.2 collective-permute-done.4.refs_0_
  6.9 0.0 collective-permute-start.6
  6.9 4.3 %collective-permute-done.5.refs_1_ = bf16[64,1024]{1,0:T(8,128)(2,1)S(1)} collective-permute-done((bf16[64,1024]{1,0:T(8,128)(2,1)}, bf16[64,1024]{1,0:T(8,128)(2,1)S(1)}, u32[]{:S(2)}, u32[]{:S(2)}) %collective-permute-start.5) | collective-permute-done | bytes 131104 | tf_op jit(solution)/shard_map/ppermute | solution.py:68
  11.2 1.3 %collective-permute-start.7 = (bf16[64,1024]{1,0:T(8,128)(2,1)S(1)}, bf16[64,1024]{1,0:T(8,128)(2,1)S(1)}, u32[]{:S(2)}, u32[]{:S(2)}) collective-permute-start(bf16[64,1024]{1,0:T(8,128)(2,1)S(1)} %collective-permute-done.5.refs_1_), channel_id=1, source_target_pairs={{0,4},{8,12},{16,20},{24,28},{1,5},{9,13},{17,21},{25,29},{2,6},{1... | collective-permute-start | bytes 393224 | tf_op jit(solution)/shard_map/ppermute | solution.py:80
  12.5 2.6 %project.1 = (bf16[384,64]{1,0:T(8,128)(2,1)S(1)}, bf16[144,384]{1,0:T(8,128)(2,1)S(1)}, bf16[144,256]{1,0:T(8,128)(2,1)S(1)}) custom-call(bf16[384,1024]{1,0:T(8,128)(2,1)} %hist_hbm.1, bf16[64,1024]{1,0:T(8,128)(2,1)} %bitcast.7, bf16[64,1024]{1,0:T(8,128)(2,1)} %bitcast.8, bf16[64,1024]{1,0:T(8,128)(2,1)} %bitcast.9, s32[3,128]{1,0:T(4,128)} %bitcast.13), custom_call_target="tpu_custom_call" | custom-call | flops 150994944 | bytes 786432 | tf_op jit(solution)/shard_map/project/pallas_call | solution.py:120
  15.2 1.9 %collective-permute-start = (bf16[144,256]{1,0:T(8,128)(2,1)S(1)}, bf16[144,256]{1,0:T(8,128)(2,1)S(1)}, u32[]{:S(2)}, u32[]{:S(2)}) collective-permute-start(bf16[144,256]{1,0:T(8,128)(2,1)S(1)} %get-tuple-element.15), channel_id=1, source_target_pairs={{0,4},{4,8},{8,12},{12,16},{16,20},{20,24},{24,28},{1,5},{5,9},{9,... | collective-permute-start | bytes 221192 | tf_op jit(solution)/shard_map/ppermute | solution.py:38
  17.1 1.2 %prepare.1 = (s32[2048,128]{1,0:T(8,128)S(1)}, f32[256,384]{1,0:T(8,128)S(1)}, f32[1,256]{1,0:T(1,128)S(1)}, s32[1,384]{1,0:T(1,128)S(1)}) custom-call(bf16[384,1024]{1,0:T(8,128)(2,1)} %pos_hbm.1, f32[1,1024]{1,0:T(1,128)} %bitcast.10, s32[16,128]{1,0:T(8,128)} %bitcast.12, s32[3,128]{1,0:T(4,128)} %bitcast.14), custom_call_target="tpu_custom_call" | custom-call | flops 98304 | bytes 196608 | tf_op jit(solution)/shard_map/prepare/pallas_call | solution.py:217
  18.3 3.4 %collective-permute-done.prev_ref = bf16[144,256]{1,0:T(8,128)(2,1)S(1)} collective-permute-done((bf16[144,256]{1,0:T(8,128)(2,1)S(1)}, bf16[144,256]{1,0:T(8,128)(2,1)S(1)}, u32[]{:S(2)}, u32[]{:S(2)}) %collective-permute-start) | collective-permute-done | bytes 73760 | tf_op jit(solution)/shard_map/ppermute | solution.py:38
  21.7 1.2 %attend.1.refs_0_ = bf16[64,384]{1,0:T(8,128)(2,1)S(1)} custom-call(bf16[384,64]{1,0:T(8,128)(2,1)S(1)} %get-tuple-element.13.q_ref, bf16[144,384]{1,0:T(8,128)(2,1)S(1)} %get-tuple-element.14.own_ref, bf16[144,256]{1,0:T(8,128)(2,1)S(1)} %collective-permute-done.prev_ref), custom_call_target="tpu_custom_call" | custom-call | flops 50331648 | bytes 147456 | tf_op jit(solution)/shard_map/attend/pallas_call | solution.py:175
  22.9 2.5 %collective-permute-start.3 = (bf16[64,384]{1,0:T(8,128)(2,1)S(1)}, bf16[64,384]{1,0:T(8,128)(2,1)S(1)}, u32[]{:S(2)}, u32[]{:S(2)}) collective-permute-start(bf16[64,384]{1,0:T(8,128)(2,1)S(1)} %attend.1.refs_0_), channel_id=1, source_target_pairs={{0,3},{1,2},{2,1},{3,0},{4,7},{5,6},{6,5},{7,4},{8,11},{9,10},{10,... | collective-permute-start | bytes 147464 | tf_op jit(solution)/shard_map/ppermute | solution.py:51
  25.4 0.0 collective-permute-start.2
  25.4 1.9 %collective-permute-start.1 = (bf16[64,384]{1,0:T(8,128)(2,1)S(1)}, bf16[64,384]{1,0:T(8,128)(2,1)S(1)}, u32[]{:S(2)}, u32[]{:S(2)}) collective-permute-start(bf16[64,384]{1,0:T(8,128)(2,1)S(1)} %attend.1.refs_0_), channel_id=1, source_target_pairs={{0,1},{1,0},{2,3},{3,2},{4,5},{5,4},{6,7},{7,6},{8,9},{9,8},{10,11... | collective-permute-start | bytes 147464 | tf_op jit(solution)/shard_map/ppermute | solution.py:51
  27.4 0.0 collective-permute-done.6.refs_2_
  27.4 0.0 collective-permute-done.7.refs_3_
  27.4 4.9 %premix.1 = (bf16[2048,256]{1,0:T(8,128)(2,1)S(1)}, bf16[1024,256]{1,0:T(8,128)(2,1)S(1)}) custom-call(bf16[2048,1024]{1,0:T(8,128)(2,1)} %neg_hbm.1, bf16[64,1024]{1,0:T(8,128)(2,1)} %own_hbm.1, f32[1,1024]{1,0:T(1,128)} %bitcast.11, bf16[64,1024]{1,0:T(8,128)(2,1)S(1)} %collective-permute-done.4.refs_0_, ...), custom_call_target="tpu_custom_call" | custom-call | flops 1073741824 | bytes 4194304 | tf_op jit(solution)/shard_map/premix/pallas_call | solution.py:282
  32.2 0.0 collective-permute-done.3.refs_3_
  32.2 0.0 collective-permute-done.2.refs_2_
  32.2 0.0 collective-permute-done.1.refs_1_
  32.3 1.6 %score.1 = (f32[4,384]{1,0:T(4,128)S(1)}, f32[256,384]{1,0:T(8,128)S(1)}) custom-call(bf16[64,384]{1,0:T(8,128)(2,1)S(1)} %attend.1.refs_0_, bf16[64,384]{1,0:T(8,128)(2,1)S(1)} %collective-permute-done.1.refs_1_, bf16[64,384]{1,0:T(8,128)(2,1)S(1)} %collective-permute-done.2.refs_2_, bf16[64,384]{1,0:T(8,128)(2,1)S(1)} %collective-permute-done.3.refs_3_, ...), custom_call_target="tpu_custom_call" | custom-call | flops 603979776 | bytes 1048576 | tf_op jit(solution)/shard_map/score/pallas_call | solution.py:344
  33.9 2.5 %collective-permute-start.10 = (f32[4,384]{1,0:T(4,128)S(1)}, f32[4,384]{1,0:T(4,128)S(1)}, u32[]{:S(2)}, u32[]{:S(2)}) collective-permute-start(f32[4,384]{1,0:T(4,128)S(1)} %get-tuple-element.23), channel_id=1, source_target_pairs={{0,3},{1,2},{2,1},{3,0},{4,7},{5,6},{6,5},{7,4},{8,11},{9,10},{10,... | collective-permute-start | bytes 18440 | tf_op jit(solution)/shard_map/ppermute | solution.py:51
  36.4 0.0 collective-permute-start.9
  36.4 1.9 %collective-permute-start.8 = (f32[4,384]{1,0:T(4,128)S(1)}, f32[4,384]{1,0:T(4,128)S(1)}, u32[]{:S(2)}, u32[]{:S(2)}) collective-permute-start(f32[4,384]{1,0:T(4,128)S(1)} %get-tuple-element.23), channel_id=1, source_target_pairs={{0,1},{1,0},{2,3},{3,2},{4,5},{5,4},{6,7},{7,6},{8,9},{9,8},{10,11... | collective-permute-start | bytes 18440 | tf_op jit(solution)/shard_map/ppermute | solution.py:51
  38.3 0.8 %finish.1 = bf16[384,256]{1,0:T(8,128)(2,1)} custom-call(f32[256,384]{1,0:T(8,128)S(1)} %get-tuple-element.21.user_ref, f32[1,256]{1,0:T(1,128)S(1)} %get-tuple-element.22.gain_ref), custom_call_target="tpu_custom_call" | custom-call | flops 196608 | bytes 589824 | tf_op jit(solution)/shard_map/finish/pallas_call | solution.py:365
  39.2 0.2 collective-permute-done.10
  39.3 1.6 %collective-permute-done.9 = f32[4,384]{1,0:T(4,128)S(1)} collective-permute-done((f32[4,384]{1,0:T(4,128)S(1)}, f32[4,384]{1,0:T(4,128)S(1)}, u32[]{:S(2)}, u32[]{:S(2)}) %collective-permute-start.9) | collective-permute-done | bytes 6176 | tf_op jit(solution)/shard_map/ppermute | solution.py:51
  40.9 0.0 collective-permute-done.8
  40.9 0.1 slice_reduce_fusion.7
  41.0 0.6 %add_subtract_fusion = f32[384]{0:T(512)} fusion(f32[384]{0:T(512)S(1)} %get-tuple-element.26, f32[384]{0:T(512)S(1)} %get-tuple-element.32, f32[384]{0:T(512)S(1)} %get-tuple-element.31, f32[384]{0:T(512)S(1)} %get-tuple-element.30, f32[384]{0:T(512)S(1)} %get-tuple-element.29, f32[384]{0:T(512)S(1)} %get-tuple-element.28, f32[384]{0:T(512)S(1)} %get-tuple-element.27, ...), kind=kLoop, calls=%fused_computation | loop fusion | flops 7296 | bytes 15360 | tf_op jit(solution)/shard_map/sub | solution.py:405
Async XLA Ops:
  0.6 6.3 %collective-permute-start.4 = (bf16[64,1024]{1,0:T(8,128)(2,1)}, bf16[64,1024]{1,0:T(8,128)(2,1)S(1)}, u32[]{:S(2)}, u32[]{:S(2)}) collective-permute-start(bf16[64,1024]{1,0:T(8,128)(2,1)} %own_hbm.1), channel_id=1, source_target_pairs={{0,1},{1,0},{2,3},{3,2},{4,6},{5,7},{6,4},{7,5},{8,9},{9,8},{10,11... | collective-permute-start | bytes 393224 | tf_op jit(solution)/shard_map/ppermute | solution.py:68
  2.3 9.0 %collective-permute-start.5 = (bf16[64,1024]{1,0:T(8,128)(2,1)}, bf16[64,1024]{1,0:T(8,128)(2,1)S(1)}, u32[]{:S(2)}, u32[]{:S(2)}) collective-permute-start(bf16[64,1024]{1,0:T(8,128)(2,1)} %own_hbm.1), channel_id=1, source_target_pairs={{0,3},{1,2},{2,1},{3,0},{8,11},{9,10},{10,9},{11,8},{16,19},{17,18... | collective-permute-start | bytes 393224 | tf_op jit(solution)/shard_map/ppermute | solution.py:68
  6.9 20.5 %collective-permute-start.6 = (bf16[64,1024]{1,0:T(8,128)(2,1)S(1)}, bf16[64,1024]{1,0:T(8,128)(2,1)S(1)}, u32[]{:S(2)}, u32[]{:S(2)}) collective-permute-start(bf16[64,1024]{1,0:T(8,128)(2,1)S(1)} %collective-permute-done.4.refs_0_), channel_id=1, source_target_pairs={{0,4},{4,0},{8,12},{12,8},{16,20},{20,16},{24,28},{28,24},{1,5},{5... | collective-permute-start | bytes 393224 | tf_op jit(solution)/shard_map/ppermute | solution.py:80
  11.2 16.1 %collective-permute-start.7 = (bf16[64,1024]{1,0:T(8,128)(2,1)S(1)}, bf16[64,1024]{1,0:T(8,128)(2,1)S(1)}, u32[]{:S(2)}, u32[]{:S(2)}) collective-permute-start(bf16[64,1024]{1,0:T(8,128)(2,1)S(1)} %collective-permute-done.5.refs_1_), channel_id=1, source_target_pairs={{0,4},{8,12},{16,20},{24,28},{1,5},{9,13},{17,21},{25,29},{2,6},{1... | collective-permute-start | bytes 393224 | tf_op jit(solution)/shard_map/ppermute | solution.py:80
  15.2 6.6 %collective-permute-start = (bf16[144,256]{1,0:T(8,128)(2,1)S(1)}, bf16[144,256]{1,0:T(8,128)(2,1)S(1)}, u32[]{:S(2)}, u32[]{:S(2)}) collective-permute-start(bf16[144,256]{1,0:T(8,128)(2,1)S(1)} %get-tuple-element.15), channel_id=1, source_target_pairs={{0,4},{4,8},{8,12},{12,16},{16,20},{20,24},{24,28},{1,5},{5,9},{9,... | collective-permute-start | bytes 221192 | tf_op jit(solution)/shard_map/ppermute | solution.py:38
  22.9 9.3 %collective-permute-start.3 = (bf16[64,384]{1,0:T(8,128)(2,1)S(1)}, bf16[64,384]{1,0:T(8,128)(2,1)S(1)}, u32[]{:S(2)}, u32[]{:S(2)}) collective-permute-start(bf16[64,384]{1,0:T(8,128)(2,1)S(1)} %attend.1.refs_0_), channel_id=1, source_target_pairs={{0,3},{1,2},{2,1},{3,0},{4,7},{5,6},{6,5},{7,4},{8,11},{9,10},{10,... | collective-permute-start | bytes 147464 | tf_op jit(solution)/shard_map/ppermute | solution.py:51
  25.4 6.8 %collective-permute-start.2 = (bf16[64,384]{1,0:T(8,128)(2,1)S(1)}, bf16[64,384]{1,0:T(8,128)(2,1)S(1)}, u32[]{:S(2)}, u32[]{:S(2)}) collective-permute-start(bf16[64,384]{1,0:T(8,128)(2,1)S(1)} %attend.1.refs_0_), channel_id=1, source_target_pairs={{0,2},{1,3},{2,0},{3,1},{4,6},{5,7},{6,4},{7,5},{8,10},{9,11},{10,... | collective-permute-start | bytes 147464 | tf_op jit(solution)/shard_map/ppermute | solution.py:51
  25.4 6.8 %collective-permute-start.1 = (bf16[64,384]{1,0:T(8,128)(2,1)S(1)}, bf16[64,384]{1,0:T(8,128)(2,1)S(1)}, u32[]{:S(2)}, u32[]{:S(2)}) collective-permute-start(bf16[64,384]{1,0:T(8,128)(2,1)S(1)} %attend.1.refs_0_), channel_id=1, source_target_pairs={{0,1},{1,0},{2,3},{3,2},{4,5},{5,4},{6,7},{7,6},{8,9},{9,8},{10,11... | collective-permute-start | bytes 147464 | tf_op jit(solution)/shard_map/ppermute | solution.py:51
  33.9 5.5 %collective-permute-start.10 = (f32[4,384]{1,0:T(4,128)S(1)}, f32[4,384]{1,0:T(4,128)S(1)}, u32[]{:S(2)}, u32[]{:S(2)}) collective-permute-start(f32[4,384]{1,0:T(4,128)S(1)} %get-tuple-element.23), channel_id=1, source_target_pairs={{0,3},{1,2},{2,1},{3,0},{4,7},{5,6},{6,5},{7,4},{8,11},{9,10},{10,... | collective-permute-start | bytes 18440 | tf_op jit(solution)/shard_map/ppermute | solution.py:51
  36.4 4.5 %collective-permute-start.9 = (f32[4,384]{1,0:T(4,128)S(1)}, f32[4,384]{1,0:T(4,128)S(1)}, u32[]{:S(2)}, u32[]{:S(2)}) collective-permute-start(f32[4,384]{1,0:T(4,128)S(1)} %get-tuple-element.23), channel_id=1, source_target_pairs={{0,2},{1,3},{2,0},{3,1},{4,6},{5,7},{6,4},{7,5},{8,10},{9,11},{10,... | collective-permute-start | bytes 18440 | tf_op jit(solution)/shard_map/ppermute | solution.py:51
  36.4 4.5 %collective-permute-start.8 = (f32[4,384]{1,0:T(4,128)S(1)}, f32[4,384]{1,0:T(4,128)S(1)}, u32[]{:S(2)}, u32[]{:S(2)}) collective-permute-start(f32[4,384]{1,0:T(4,128)S(1)} %get-tuple-element.23), channel_id=1, source_target_pairs={{0,1},{1,0},{2,3},{3,2},{4,5},{5,4},{6,7},{7,6},{8,9},{9,8},{10,11... | collective-permute-start | bytes 18440 | tf_op jit(solution)/shard_map/ppermute | solution.py:51

commit v3 on v2

--- a/solution.py
+++ b/solution.py
@@ -50,35 +50,6 @@
     for pairs in partners(axis):
         pieces.append(lax.ppermute(shard, axis, pairs))
     return pieces
-
-
-def fetch_in_pairs(shard):
-    count, pairs_of = lax.axis_size("head"), lax.axis_size("seq")
-    if count & (count - 1) or pairs_of % 2:
-        return from_all(shard, "head")[1:]
-    far = []
-    for odd in range(1, count, 2):
-        moves = [(odd, odd + 1)[s % 2] for s in range(pairs_of)]
-        route = [
-            (s * count + h, s * count + (h ^ k))
-            for s, k in enumerate(moves)
-            if k < count
-            for h in range(count)
-        ]
-        far.append(lax.ppermute(shard, ("seq", "head"), route))
-    return far
-
-
-def swap_in_pairs(far, count):
-    pairs_of = lax.axis_size("seq")
-    if count & (count - 1) or pairs_of % 2:
-        return []
-    near = []
-    for n, piece in enumerate(far):
-        both = 2 * n + 2 < count
-        route = [(s, s ^ 1) for s in range(pairs_of) if both or s % 2 == 0]
-        near.append(lax.ppermute(piece, "seq", route))
-    return near
 
 
 def project_body(hist_hbm, wq_hbm, wk_hbm, wv_hbm, pad_hbm, q_ref, own_ref, edge_ref, hist, weights, pad_ref, sems):
@@ -183,37 +154,42 @@
     )(query, own, prev)
 
 
-def prepare_body(pos_hbm, gain_hbm, ids_hbm, target_hbm, id_ref, pos_out, gain_out, target_out, pos, gain, ids_ref, target_ref, sems):
+def prepare_body(pos_hbm, gain_hbm, ids_hbm, target_hbm, own_hbm, neg_hbm, id_ref, pos_out, gain_out, target_out, own_out, all_out, neg_out, pos, ids_ref, target_ref, sems):
     rows, share = pos.shape
     here = pl.ds(0, share)
     if pos_hbm.shape[1] != share:
         here = pl.ds(pl.multiple_of(lax.axis_index("head") * share, share), share)
-    copy_pos = pltpu.make_async_copy(pos_hbm.at[:, here], pos, sems.at[0])
-    copy_gain = pltpu.make_async_copy(gain_hbm.at[:, here], gain, sems.at[1])
-    copy_ids = pltpu.make_async_copy(ids_hbm, ids_ref, sems.at[2])
-    copy_target = pltpu.make_async_copy(target_hbm, target_ref, sems.at[3])
-    copy_ids.start()
-    copy_target.start()
-    copy_pos.start()
-    copy_gain.start()
-    copy_ids.wait()
-    copy_target.wait()
+    moves = (
+        (ids_hbm, ids_ref),
+        (target_hbm, target_ref),
+        (gain_hbm, all_out),
+        (pos_hbm.at[:, here], pos),
+        (own_hbm, own_out),
+        (neg_hbm.at[pl.ds(0, neg_out.shape[0])], neg_out),
+    )
+    copies = [pltpu.make_async_copy(a, b, sems.at[n]) for n, (a, b) in enumerate(moves)]
+    for copy in copies:
+        copy.start()
+    copies[0].wait()
+    copies[1].wait()
     target_out[...] = jnp.concatenate([target_ref[n : n + 1, :] for n in range(rows // LANES)], 1)
     for n in range(ids_ref.shape[0]):
         line = jnp.broadcast_to(ids_ref[n : n + 1, :], (LANES, LANES))
         id_ref[n * LANES : (n + 1) * LANES, :] = line.T
-    copy_pos.wait()
-    copy_gain.wait()
-    gain_out[...] = gain[...]
-    pos_out[...] = (pos[...].astype(F32) * gain[...]).T
-
-
-def prepare(pos_emb, norm_gain, neg_ids, target_ids, share):
-    rows, _ = pos_emb.shape
+    copies[2].wait()
+    copies[3].wait()
+    gain = all_out[:, here]
+    gain_out[...] = gain
+    pos_out[...] = (pos[...].astype(F32) * gain).T
+    copies[4].wait()
+    copies[5].wait()
+
+
+def prepare(pos_emb, norm_gain, neg_ids, target_ids, own, neg_emb, share):
+    rows, width = pos_emb.shape
     negs = neg_ids.shape[0]
     if share % LANES:
         pos_emb = lax.dynamic_slice_in_dim(pos_emb, lax.axis_index("head") * share, share, 1)
-        norm_gain = lax.dynamic_slice_in_dim(norm_gain, lax.axis_index("head") * share, share, 0)
     return pl.pallas_call(
         prepare_body,
         name="prepare",
@@ -222,82 +198,74 @@
             jax.ShapeDtypeStruct((share, rows), F32),
             jax.ShapeDtypeStruct((1, share), F32),
             jax.ShapeDtypeStruct((1, rows), jnp.int32),
-        ),
-        in_specs=[RAW] * 4,
-        out_specs=(WHOLE,) * 4,
+            jax.ShapeDtypeStruct(own.shape, BF16),
+            jax.ShapeDtypeStruct((1, width), F32),
+            jax.ShapeDtypeStruct((negs // 2, width), BF16),
+        ),
+        in_specs=[RAW] * 6,
+        out_specs=(WHOLE,) * 7,
         scratch_shapes=[
             pltpu.VMEM((rows, share), BF16),
-            pltpu.VMEM((1, share), F32),
             pltpu.VMEM((negs // LANES, LANES), jnp.int32),
             pltpu.VMEM((rows // LANES, LANES), jnp.int32),
-            pltpu.SemaphoreType.DMA((4,)),
+            pltpu.SemaphoreType.DMA((6,)),
         ],
-        compiler_params=pltpu.CompilerParams(vmem_limit_bytes=8 * MIB),
-        cost_estimate=pl.CostEstimate(flops=rows * share, bytes_accessed=2 * rows * share, transcendentals=0),
-    )(*stay(pos_emb, norm_gain[None, :], neg_ids.reshape(-1, LANES), target_ids.reshape(-1, LANES)))
-
-
-def premix_body(count, paired, neg_hbm, own_hbm, gain_hbm, *refs):
-    n_far = count // 2 if paired else count - 1
-    far, near = refs[:n_far], refs[n_far : 2 * n_far if paired else n_far]
-    mix_ref, turned_ref, scaled, negs, own, gain, sems = refs[n_far + len(near) :]
-    total, _ = negs.shape
-    tall = own.shape[0]
+        compiler_params=pltpu.CompilerParams(vmem_limit_bytes=12 * MIB),
+        cost_estimate=pl.CostEstimate(flops=rows * share, bytes_accessed=negs * width, transcendentals=0),
+    )(*stay(pos_emb, norm_gain[None, :], neg_ids.reshape(-1, LANES), target_ids.reshape(-1, LANES), own, neg_emb))
+
+
+def premix_body(count, neg_hbm, first_ref, gain_ref, *refs):
+    pieces, (mix_ref, turned_ref, scaled, negs, sems) = refs[:count], refs[count:]
+    ahead, width = first_ref.shape
+    tall = pieces[0].shape[0]
     block = 256
-    copies = [
-        pltpu.make_async_copy(own_hbm, own, sems.at[0]),
-        pltpu.make_async_copy(gain_hbm, gain, sems.at[1]),
-    ]
+    copies = {}
+    for n, start in enumerate(range(0, negs.shape[0], block)):
+        copies[ahead + start] = pltpu.make_async_copy(
+            neg_hbm.at[pl.ds(ahead + start, block)], negs.at[pl.ds(start, block)], sems.at[n]
+        )
+    for copy in copies.values():
+        copy.start()
+    gain = gain_ref[...]
+    for k in range(count):
+        scaled[k * tall : (k + 1) * tall, :] = (pieces[k][...].astype(F32) * gain).astype(BF16)
+    total = ahead + negs.shape[0]
+    turn = width // (total // block)
     for n, start in enumerate(range(0, total, block)):
-        part = pl.ds(start, block)
-        copies.append(pltpu.make_async_copy(neg_hbm.at[part], negs.at[part], sems.at[2 + n]))
-    for copy in copies:
-        copy.start()
-    first = lax.axis_index("seq") % 2 == 0
-    copies[0].wait()
-    copies[1].wait()
-    for k in range(count):
-        if k == 0:
-            piece = own[...].astype(F32)
-        elif paired:
-            mine, theirs = far[(k - 1) // 2][...].astype(F32), near[(k - 1) // 2][...].astype(F32)
-            piece = jnp.where(first, mine, theirs) if k % 2 else jnp.where(first, theirs, mine)
+        if start < ahead:
+            part = first_ref[start : start + block, :]
         else:
-            piece = far[k - 1][...].astype(F32)
-        scaled[k * tall : (k + 1) * tall, :] = (piece * gain[...]).astype(BF16)
-        if k % 2:
-            pair = jnp.concatenate([last, piece], 0)
-            turned_ref[:, (k - 1) * tall : (k + 1) * tall] = pair.T.astype(BF16)
-        last = piece
-    for n, start in enumerate(range(0, total, block)):
-        copies[2 + n].wait()
-        mix_ref[start : start + block, :] = dot_last(negs[start : start + block, :], scaled[...]).astype(BF16)
-
-
-def premix(neg_emb, own, far, near, norm_gain):
+            copies[start].wait()
+            part = negs[start - ahead : start - ahead + block, :]
+        mix_ref[start : start + block, :] = dot_last(part, scaled[...]).astype(BF16)
+        cols = slice(n * turn, (n + 1) * turn)
+        whole = jnp.concatenate([ref[:, cols].astype(F32) for ref in pieces], 0)
+        turned_ref[cols, :] = whole.T.astype(BF16)
+
+
+def premix(neg_emb, first, gain_row, pieces):
     negs, width = neg_emb.shape
-    count = lax.axis_size("head")
-    tall = own.shape[0]
-    deep = count * tall
-    return pl.pallas_call(
-        functools.partial(premix_body, count, bool(near)),
+    count = len(pieces)
+    deep = count * pieces[0].shape[0]
+    rest = negs - first.shape[0]
+    return pl.pallas_call(
+        functools.partial(premix_body, count),
         name="premix",
         out_shape=(
             jax.ShapeDtypeStruct((negs, deep), BF16),
             jax.ShapeDtypeStruct((width, deep), BF16),
         ),
-        in_specs=[RAW, RAW, RAW] + [WHOLE] * (len(far) + len(near)),
+        in_specs=[RAW] + [WHOLE] * (2 + count),
         out_specs=(WHOLE, WHOLE),
         scratch_shapes=[
             pltpu.VMEM((deep, width), BF16),
-            pltpu.VMEM((negs, width), BF16),
-            pltpu.VMEM((tall, width), BF16),
-            pltpu.VMEM((1, width), F32),
-            pltpu.SemaphoreType.DMA((2 + negs // 256,)),
+            pltpu.VMEM((rest, width), BF16),
+            pltpu.SemaphoreType.DMA((rest // 256,)),
         ],
         compiler_params=pltpu.CompilerParams(vmem_limit_bytes=28 * MIB),
         cost_estimate=pl.CostEstimate(flops=2 * negs * width * deep, bytes_accessed=2 * negs * width, transcendentals=0),
-    )(*stay(neg_emb, own, norm_gain[None, :]), *far, *near)
+    )(*stay(neg_emb), first, gain_row, *pieces)
 
 
 def score_body(count, *refs):
@@ -390,12 +358,13 @@
     count = lax.axis_size("head")
     query, own, edge = project(history, w_query, w_key, w_value, pad_mask)
     prev = from_behind(edge, "seq", 1)
-    far = fetch_in_pairs(w_out)
-    id_cols, pos_turned, gain_here, target = prepare(pos_emb, norm_gain, neg_ids, target_ids, width // count)
+    pieces = from_all(w_out, "head")
+    id_cols, pos_turned, gain_here, target, pieces[0], gain_row, first = prepare(
+        pos_emb, norm_gain, neg_ids, target_ids, w_out, neg_emb, width // count
+    )
     mine = attend(query, own, prev)
     heads = from_all(mine, "head")
-    near = swap_in_pairs(far, count)
-    mix, turned = premix(neg_emb, w_out, far, near, norm_gain)
+    mix, turned = premix(neg_emb, first, gain_row, pieces)
     stats, user = score(heads, mix, turned, id_cols, pos_turned, target)
     all_stats = from_all(stats, "head")
     user_share = finish(user, gain_here)

time: 41.9 us -> 35.7 us (0.85)
  starting transfers between devices: 18.1 us -> 15.3 us
  waiting for transfers between devices: 9.75 us -> 7.14 us
  Pallas kernels: 12.3 us -> 11.6 us
    ppermute x4 -> x0, starting transfers between devices: 7.3 us -> none  [the longest x2 6.01 us: fetch_in_pairs(): far.append(lax.ppermute(shard, ('seq', 'head'), route))]
    ppermute x4 -> x0, waiting for transfers between devices: 4.58 us -> none  [the longest x2 4.57 us: fetch_in_pairs(): far.append(lax.ppermute(shard, ('seq', 'head'), route))]
    ppermute x6 -> x9, starting transfers between devices: 8.91 us -> 13.3 us  [from_all(): pieces.append(lax.ppermute(shard, axis, pairs))]
    ppermute x6 -> x9, waiting for transfers between devices: 1.78 us -> 4.39 us  [from_all(): pieces.append(lax.ppermute(shard, axis, pairs))]
    pallas_call x1, Pallas kernels: 4.86 us -> 3.52 us  [premix(): pl.pallas_call(functools.partial(premix_body, count), name='premix', out_...]
    ppermute x1, waiting for transfers between devices: 3.39 us -> 2.75 us  [from_behind(): return lax.ppermute(shard, axis, pairs)]
    pallas_call x1, Pallas kernels: 1.25 us -> 1.88 us  [prepare(): pl.pallas_call(prepare_body, name='prepare', out_shape=(jax.ShapeDtypeStr...]
  transfers between devices with their start and end apart: 11 -> 10, of which waited for: 5 -> 3; matrix products, arithmetic and copies ran while one was open for 0% -> 0% of each run, Pallas kernels for 26% -> 28%
where the time goes in v3:
time: 35.7 us; the launch traced here: 35.4 us
  starting transfers between devices  15.3 us (43%)
  Pallas kernels  11.6 us (32%)
  waiting for transfers between devices  7.14 us (20%)
  between operations  0.71 us (2%)
  other arithmetic  0.66 us (2%)
    ppermute x9, starting transfers between devices, from_all(): pieces.append(lax.ppermute(shard, axis, pairs))  13.3 us
    ppermute x9, waiting for transfers between devices, from_all(): pieces.append(lax.ppermute(shard, axis, pairs))  4.39 us
    pallas_call x1, Pallas kernels, premix(): pl.pallas_call(functools.partial(premix_body, count), name='premix', out_...  3.52 us
    ppermute x1, waiting for transfers between devices, from_behind(): return lax.ppermute(shard, axis, pairs)  2.75 us
    pallas_call x1, Pallas kernels, project(): pl.pallas_call(project_body, name='project', out_shape=(jax.ShapeDtypeStr...  2.61 us
    ppermute x1, starting transfers between devices, from_behind(): return lax.ppermute(shard, axis, pairs)  1.92 us
    pallas_call x1, Pallas kernels, prepare(): pl.pallas_call(prepare_body, name='prepare', out_shape=(jax.ShapeDtypeStr...  1.88 us
    pallas_call x1, Pallas kernels, score(): pl.pallas_call(functools.partial(score_body, count), name='score', out_sh...  1.59 us
  transfers between devices with their start and end apart: 10, of which 3 were waited for; matrix products, arithmetic and copies ran while one was open for 0% of the time, Pallas kernels for 28%

profile of v3, /device:TPU:4, one launch (start us, length us, event | category | flops | bytes accessed | tf_op | source)
XLA Modules:
  0.0 35.4 jit_solution(7592621335242101139)
XLA Ops:
  0.6 1.6 %collective-permute-start.4 = (bf16[64,1024]{1,0:T(8,128)(2,1)}, bf16[64,1024]{1,0:T(8,128)(2,1)S(1)}, u32[]{:S(2)}, u32[]{:S(2)}) collective-permute-start(bf16[64,1024]{1,0:T(8,128)(2,1)} %own_hbm.1), channel_id=1, source_target_pairs={{0,1},{1,0},{2,3},{3,2},{4,5},{5,4},{6,7},{7,6},{8,9},{9,8},{10,11... | collective-permute-start | bytes 393224 | tf_op jit(solution)/shard_map/ppermute | solution.py:51
  2.3 2.6 %collective-permute-start.5 = (bf16[64,1024]{1,0:T(8,128)(2,1)}, bf16[64,1024]{1,0:T(8,128)(2,1)S(1)}, u32[]{:S(2)}, u32[]{:S(2)}) collective-permute-start(bf16[64,1024]{1,0:T(8,128)(2,1)} %own_hbm.1), channel_id=1, source_target_pairs={{0,2},{1,3},{2,0},{3,1},{4,6},{5,7},{6,4},{7,5},{8,10},{9,11},{10,... | collective-permute-start | bytes 393224 | tf_op jit(solution)/shard_map/ppermute | solution.py:51
  4.9 0.2 collective-permute-start.6
  5.1 2.6 %project.1 = (bf16[384,64]{1,0:T(8,128)(2,1)S(1)}, bf16[144,384]{1,0:T(8,128)(2,1)S(1)}, bf16[144,256]{1,0:T(8,128)(2,1)S(1)}) custom-call(bf16[384,1024]{1,0:T(8,128)(2,1)} %hist_hbm.1, bf16[64,1024]{1,0:T(8,128)(2,1)} %bitcast.7, bf16[64,1024]{1,0:T(8,128)(2,1)} %bitcast.8, bf16[64,1024]{1,0:T(8,128)(2,1)} %bitcast.9, s32[3,128]{1,0:T(4,128)} %bitcast.12), custom_call_target="tpu_custom_call" | custom-call | flops 150994944 | bytes 786432 | tf_op jit(solution)/shard_map/project/pallas_call | solution.py:91
  7.7 1.9 %collective-permute-start = (bf16[144,256]{1,0:T(8,128)(2,1)S(1)}, bf16[144,256]{1,0:T(8,128)(2,1)S(1)}, u32[]{:S(2)}, u32[]{:S(2)}) collective-permute-start(bf16[144,256]{1,0:T(8,128)(2,1)S(1)} %get-tuple-element.18), channel_id=1, source_target_pairs={{0,4},{4,8},{8,12},{12,16},{16,20},{20,24},{24,28},{1,5},{5,9},{9,... | collective-permute-start | bytes 221192 | tf_op jit(solution)/shard_map/ppermute | solution.py:38
  9.6 1.9 %prepare.1 = (s32[2048,128]{1,0:T(8,128)S(1)}, f32[256,384]{1,0:T(8,128)S(1)}, f32[1,256]{1,0:T(1,128)S(1)}, s32[1,384]{1,0:T(1,128)S(1)}, bf16[64,1024]{1,0:T(8...) custom-call(bf16[384,1024]{1,0:T(8,128)(2,1)} %pos_hbm.1, f32[1,1024]{1,0:T(1,128)} %bitcast.11, ...), custom_call_target="tpu_custom_call" | custom-call | flops 98304 | bytes 2097152 | tf_op jit(solution)/shard_map/prepare/pallas_call | solution.py:193
  11.5 2.8 %collective-permute-done.prev_ref = bf16[144,256]{1,0:T(8,128)(2,1)S(1)} collective-permute-done((bf16[144,256]{1,0:T(8,128)(2,1)S(1)}, bf16[144,256]{1,0:T(8,128)(2,1)S(1)}, u32[]{:S(2)}, u32[]{:S(2)}) %collective-permute-start) | collective-permute-done | bytes 73760 | tf_op jit(solution)/shard_map/ppermute | solution.py:38
  14.3 1.2 %attend.1.refs_0_ = bf16[64,384]{1,0:T(8,128)(2,1)S(1)} custom-call(bf16[384,64]{1,0:T(8,128)(2,1)S(1)} %get-tuple-element.16.q_ref, bf16[144,384]{1,0:T(8,128)(2,1)S(1)} %get-tuple-element.17.own_ref, bf16[144,256]{1,0:T(8,128)(2,1)S(1)} %collective-permute-done.prev_ref), custom_call_target="tpu_custom_call" | custom-call | flops 50331648 | bytes 147456 | tf_op jit(solution)/shard_map/attend/pallas_call | solution.py:146
  15.5 0.7 %collective-permute-start.1 = (bf16[64,384]{1,0:T(8,128)(2,1)S(1)}, bf16[64,384]{1,0:T(8,128)(2,1)S(1)}, u32[]{:S(2)}, u32[]{:S(2)}) collective-permute-start(bf16[64,384]{1,0:T(8,128)(2,1)S(1)} %attend.1.refs_0_), channel_id=1, source_target_pairs={{0,1},{1,0},{2,3},{3,2},{4,5},{5,4},{6,7},{7,6},{8,9},{9,8},{10,11... | collective-permute-start | bytes 147464 | tf_op jit(solution)/shard_map/ppermute | solution.py:51
  16.2 3.5 %collective-permute-start.2 = (bf16[64,384]{1,0:T(8,128)(2,1)S(1)}, bf16[64,384]{1,0:T(8,128)(2,1)S(1)}, u32[]{:S(2)}, u32[]{:S(2)}) collective-permute-start(bf16[64,384]{1,0:T(8,128)(2,1)S(1)} %attend.1.refs_0_), channel_id=1, source_target_pairs={{0,2},{1,3},{2,0},{3,1},{4,6},{5,7},{6,4},{7,5},{8,10},{9,11},{10,... | collective-permute-start | bytes 147464 | tf_op jit(solution)/shard_map/ppermute | solution.py:51
  19.7 0.0 collective-permute-done.4.refs_1_
  19.7 0.2 collective-permute-start.3
  19.9 0.0 collective-permute-done.5.refs_2_
  19.9 0.0 collective-permute-done.6.refs_3_
  19.9 3.5 %premix.1 = (bf16[2048,256]{1,0:T(8,128)(2,1)S(1)}, bf16[1024,256]{1,0:T(8,128)(2,1)S(1)}) custom-call(bf16[2048,1024]{1,0:T(8,128)(2,1)} %neg_hbm.3, bf16[1024,1024]{1,0:T(8,128)(2,1)S(1)} %get-tuple-element.19.first_ref, f32[1,1024]{1,0:T(1,128)S(1)} %get-tuple-element.20.gain_ref, bf16[64,1024]{1,0:T(8,128)(2,1)S(1)} %get-tuple-element.21.refs_0_, ...), custom_call_target="tpu_custom_call" | custom-call | flops 1073741824 | bytes 4194304 | tf_op jit(solution)/shard_map/premix/pallas_call | solution.py:252
  23.5 0.0 collective-permute-done.1.refs_1_
  23.5 0.0 collective-permute-done.2.refs_2_
  23.5 2.1 %collective-permute-done.3.refs_3_ = bf16[64,384]{1,0:T(8,128)(2,1)S(1)} collective-permute-done((bf16[64,384]{1,0:T(8,128)(2,1)S(1)}, bf16[64,384]{1,0:T(8,128)(2,1)S(1)}, u32[]{:S(2)}, u32[]{:S(2)}) %collective-permute-start.3) | collective-permute-done | bytes 49184 | tf_op jit(solution)/shard_map/ppermute | solution.py:51
  25.6 1.6 %score.1 = (f32[4,384]{1,0:T(4,128)S(1)}, f32[256,384]{1,0:T(8,128)S(1)}) custom-call(bf16[64,384]{1,0:T(8,128)(2,1)S(1)} %attend.1.refs_0_, bf16[64,384]{1,0:T(8,128)(2,1)S(1)} %collective-permute-done.1.refs_1_, bf16[64,384]{1,0:T(8,128)(2,1)S(1)} %collective-permute-done.2.refs_2_, bf16[64,384]{1,0:T(8,128)(2,1)S(1)} %collective-permute-done.3.refs_3_, ...), custom_call_target="tpu_custom_call" | custom-call | flops 603979776 | bytes 1048576 | tf_op jit(solution)/shard_map/score/pallas_call | solution.py:312
  27.2 0.1 collective-permute-start.7
  27.3 2.1 %collective-permute-start.8 = (f32[4,384]{1,0:T(4,128)S(1)}, f32[4,384]{1,0:T(4,128)S(1)}, u32[]{:S(2)}, u32[]{:S(2)}) collective-permute-start(f32[4,384]{1,0:T(4,128)S(1)} %get-tuple-element.29), channel_id=1, source_target_pairs={{0,2},{1,3},{2,0},{3,1},{4,6},{5,7},{6,4},{7,5},{8,10},{9,11},{10,... | collective-permute-start | bytes 18440 | tf_op jit(solution)/shard_map/ppermute | solution.py:51
  29.3 2.3 %collective-permute-start.9 = (f32[4,384]{1,0:T(4,128)S(1)}, f32[4,384]{1,0:T(4,128)S(1)}, u32[]{:S(2)}, u32[]{:S(2)}) collective-permute-start(f32[4,384]{1,0:T(4,128)S(1)} %get-tuple-element.29), channel_id=1, source_target_pairs={{0,3},{1,2},{2,1},{3,0},{4,7},{5,6},{6,5},{7,4},{8,11},{9,10},{10,... | collective-permute-start | bytes 18440 | tf_op jit(solution)/shard_map/ppermute | solution.py:51
  31.6 0.8 %finish.1 = bf16[384,256]{1,0:T(8,128)(2,1)} custom-call(f32[256,384]{1,0:T(8,128)S(1)} %get-tuple-element.27.user_ref, f32[1,256]{1,0:T(1,128)S(1)} %get-tuple-element.28.gain_ref), custom_call_target="tpu_custom_call" | custom-call | flops 196608 | bytes 589824 | tf_op jit(solution)/shard_map/finish/pallas_call | solution.py:333
  32.5 0.0 collective-permute-done.7
  32.5 0.0 collective-permute-done.8
  32.5 2.3 %collective-permute-done.9 = f32[4,384]{1,0:T(4,128)S(1)} collective-permute-done((f32[4,384]{1,0:T(4,128)S(1)}, f32[4,384]{1,0:T(4,128)S(1)}, u32[]{:S(2)}, u32[]{:S(2)}) %collective-permute-start.9) | collective-permute-done | bytes 6176 | tf_op jit(solution)/shard_map/ppermute | solution.py:51
  34.7 0.1 slice_reduce_fusion.7
  34.8 0.6 %add_subtract_fusion = f32[384]{0:T(512)} fusion(f32[384]{0:T(512)S(1)} %get-tuple-element.32, f32[384]{0:T(512)S(1)} %get-tuple-element.38, f32[384]{0:T(512)S(1)} %get-tuple-element.37, f32[384]{0:T(512)S(1)} %get-tuple-element.36, f32[384]{0:T(512)S(1)} %get-tuple-element.35, f32[384]{0:T(512)S(1)} %get-tuple-element.34, f32[384]{0:T(512)S(1)} %get-tuple-element.33, ...), kind=kLoop, calls=%fused_computation | loop fusion | flops 7296 | bytes 15360 | tf_op jit(solution)/shard_map/sub | solution.py:374
Async XLA Ops:
  0.6 19.1 %collective-permute-start.4 = (bf16[64,1024]{1,0:T(8,128)(2,1)}, bf16[64,1024]{1,0:T(8,128)(2,1)S(1)}, u32[]{:S(2)}, u32[]{:S(2)}) collective-permute-start(bf16[64,1024]{1,0:T(8,128)(2,1)} %own_hbm.1), channel_id=1, source_target_pairs={{0,1},{1,0},{2,3},{3,2},{4,5},{5,4},{6,7},{7,6},{8,9},{9,8},{10,11... | collective-permute-start | bytes 393224 | tf_op jit(solution)/shard_map/ppermute | solution.py:51
  2.3 17.6 %collective-permute-start.5 = (bf16[64,1024]{1,0:T(8,128)(2,1)}, bf16[64,1024]{1,0:T(8,128)(2,1)S(1)}, u32[]{:S(2)}, u32[]{:S(2)}) collective-permute-start(bf16[64,1024]{1,0:T(8,128)(2,1)} %own_hbm.1), channel_id=1, source_target_pairs={{0,2},{1,3},{2,0},{3,1},{4,6},{5,7},{6,4},{7,5},{8,10},{9,11},{10,... | collective-permute-start | bytes 393224 | tf_op jit(solution)/shard_map/ppermute | solution.py:51
  4.9 15.1 %collective-permute-start.6 = (bf16[64,1024]{1,0:T(8,128)(2,1)}, bf16[64,1024]{1,0:T(8,128)(2,1)S(1)}, u32[]{:S(2)}, u32[]{:S(2)}) collective-permute-start(bf16[64,1024]{1,0:T(8,128)(2,1)} %own_hbm.1), channel_id=1, source_target_pairs={{0,3},{1,2},{2,1},{3,0},{4,7},{5,6},{6,5},{7,4},{8,11},{9,10},{10,... | collective-permute-start | bytes 393224 | tf_op jit(solution)/shard_map/ppermute | solution.py:51
  7.7 6.6 %collective-permute-start = (bf16[144,256]{1,0:T(8,128)(2,1)S(1)}, bf16[144,256]{1,0:T(8,128)(2,1)S(1)}, u32[]{:S(2)}, u32[]{:S(2)}) collective-permute-start(bf16[144,256]{1,0:T(8,128)(2,1)S(1)} %get-tuple-element.18), channel_id=1, source_target_pairs={{0,4},{4,8},{8,12},{12,16},{16,20},{20,24},{24,28},{1,5},{5,9},{9,... | collective-permute-start | bytes 221192 | tf_op jit(solution)/shard_map/ppermute | solution.py:38
  15.5 8.0 %collective-permute-start.1 = (bf16[64,384]{1,0:T(8,128)(2,1)S(1)}, bf16[64,384]{1,0:T(8,128)(2,1)S(1)}, u32[]{:S(2)}, u32[]{:S(2)}) collective-permute-start(bf16[64,384]{1,0:T(8,128)(2,1)S(1)} %attend.1.refs_0_), channel_id=1, source_target_pairs={{0,1},{1,0},{2,3},{3,2},{4,5},{5,4},{6,7},{7,6},{8,9},{9,8},{10,11... | collective-permute-start | bytes 147464 | tf_op jit(solution)/shard_map/ppermute | solution.py:51
  16.2 7.3 %collective-permute-start.2 = (bf16[64,384]{1,0:T(8,128)(2,1)S(1)}, bf16[64,384]{1,0:T(8,128)(2,1)S(1)}, u32[]{:S(2)}, u32[]{:S(2)}) collective-permute-start(bf16[64,384]{1,0:T(8,128)(2,1)S(1)} %attend.1.refs_0_), channel_id=1, source_target_pairs={{0,2},{1,3},{2,0},{3,1},{4,6},{5,7},{6,4},{7,5},{8,10},{9,11},{10,... | collective-permute-start | bytes 147464 | tf_op jit(solution)/shard_map/ppermute | solution.py:51
  19.7 5.9 %collective-permute-start.3 = (bf16[64,384]{1,0:T(8,128)(2,1)S(1)}, bf16[64,384]{1,0:T(8,128)(2,1)S(1)}, u32[]{:S(2)}, u32[]{:S(2)}) collective-permute-start(bf16[64,384]{1,0:T(8,128)(2,1)S(1)} %attend.1.refs_0_), channel_id=1, source_target_pairs={{0,3},{1,2},{2,1},{3,0},{4,7},{5,6},{6,5},{7,4},{8,11},{9,10},{10,... | collective-permute-start | bytes 147464 | tf_op jit(solution)/shard_map/ppermute | solution.py:51
  27.2 5.3 %collective-permute-start.7 = (f32[4,384]{1,0:T(4,128)S(1)}, f32[4,384]{1,0:T(4,128)S(1)}, u32[]{:S(2)}, u32[]{:S(2)}) collective-permute-start(f32[4,384]{1,0:T(4,128)S(1)} %get-tuple-element.29), channel_id=1, source_target_pairs={{0,1},{1,0},{2,3},{3,2},{4,5},{5,4},{6,7},{7,6},{8,9},{9,8},{10,11... | collective-permute-start | bytes 18440 | tf_op jit(solution)/shard_map/ppermute | solution.py:51
  27.3 5.2 %collective-permute-start.8 = (f32[4,384]{1,0:T(4,128)S(1)}, f32[4,384]{1,0:T(4,128)S(1)}, u32[]{:S(2)}, u32[]{:S(2)}) collective-permute-start(f32[4,384]{1,0:T(4,128)S(1)} %get-tuple-element.29), channel_id=1, source_target_pairs={{0,2},{1,3},{2,0},{3,1},{4,6},{5,7},{6,4},{7,5},{8,10},{9,11},{10,... | collective-permute-start | bytes 18440 | tf_op jit(solution)/shard_map/ppermute | solution.py:51
  29.3 5.4 %collective-permute-start.9 = (f32[4,384]{1,0:T(4,128)S(1)}, f32[4,384]{1,0:T(4,128)S(1)}, u32[]{:S(2)}, u32[]{:S(2)}) collective-permute-start(f32[4,384]{1,0:T(4,128)S(1)} %get-tuple-element.29), channel_id=1, source_target_pairs={{0,3},{1,2},{2,1},{3,0},{4,7},{5,6},{6,5},{7,4},{8,11},{9,10},{10,... | collective-permute-start | bytes 18440 | tf_op jit(solution)/shard_map/ppermute | solution.py:51

commit v4 on v3

--- a/solution.py
+++ b/solution.py
@@ -14,6 +14,7 @@
 FLAG_ROWS = 16
 LOW = -1e30
 MIB = 1 << 20
+AHEAD = 4 * 10**9
 F32 = jnp.float32
 BF16 = jnp.bfloat16
 WHOLE = pl.BlockSpec(memory_space=pltpu.VMEM)
@@ -52,29 +53,76 @@
     return pieces
 
 
-def project_body(hist_hbm, wq_hbm, wk_hbm, wv_hbm, pad_hbm, q_ref, own_ref, edge_ref, hist, weights, pad_ref, sems):
+def is_paired(count, slabs):
+    return count & (count - 1) == 0 and slabs % 2 == 0
+
+
+def fetch_in_pairs(shard, half):
+    count, slabs = lax.axis_size("head"), lax.axis_size("seq")
+    if not is_paired(count, slabs):
+        return from_all(shard, "head")[1:]
+    far = []
+    for odd in range(1, count, 2):
+        last = odd + 1 == count
+        route = [
+            (s * count + h, s * count + (h ^ (odd if last else odd + s % 2)))
+            for s in range(slabs)
+            for h in range(count)
+        ]
+        far.append(lax.ppermute(half if last else shard, ("seq", "head"), route))
+    return far
+
+
+def swap_in_pairs(far, count):
+    slabs = lax.axis_size("seq")
+    if not is_paired(count, slabs):
+        return []
+    near = []
+    for piece in far:
+        near.append(lax.ppermute(piece, "seq", [(s, s ^ 1) for s in range(slabs)]))
+    return near
+
+
+def front_body(*refs):
+    hist_hbm, wq_hbm, wk_hbm, wv_hbm, pad_hbm, pos_hbm, gain_hbm, ids_hbm, target_hbm, out_hbm = refs[:10]
+    q_ref, own_ref, edge_ref, id_ref, pos_out, gain_out, target_out, gain_row, half_ref = refs[10:19]
+    hist, weights, pos, pad_ref, ids_ref, target_ref, sems = refs[19:]
     rows, _ = hist.shape
     cols = wq_hbm.shape[0]
+    share = pos.shape[1]
     step = LANES
+    here = pl.ds(0, share)
+    if pos_hbm.shape[1] != share:
+        here = pl.ds(pl.multiple_of(lax.axis_index("head") * share, share), share)
     starts = list(range(0, rows, step))[::-1]
-    copies = []
+    moves = [(ids_hbm, ids_ref), (target_hbm, target_ref), (pad_hbm, pad_ref), (gain_hbm, gain_row)]
+    moves.append((pos_hbm.at[:, here], pos))
+    half = half_ref.shape[0]
+    part = lax.axis_index("seq") % (out_hbm.shape[0] // half)
+    moves.append((out_hbm.at[pl.ds(pl.multiple_of(part * half, half), half)], half_ref))
     for n, source in enumerate((wq_hbm, wk_hbm, wv_hbm)):
-        copies.append(pltpu.make_async_copy(source, weights.at[pl.ds(n * cols, cols)], sems.at[n]))
-    for n, start in enumerate(starts):
-        part = pl.ds(start, step)
-        copies.append(pltpu.make_async_copy(hist_hbm.at[part], hist.at[part], sems.at[3 + n]))
-    copies.append(pltpu.make_async_copy(pad_hbm, pad_ref, sems.at[3 + len(starts)]))
+        moves.append((source, weights.at[pl.ds(n * cols, cols)]))
+    for start in starts:
+        moves.append((hist_hbm.at[pl.ds(start, step)], hist.at[pl.ds(start, step)]))
+    copies = [pltpu.make_async_copy(a, b, sems.at[n]) for n, (a, b) in enumerate(moves)]
     for copy in copies:
         copy.start()
-    copies[-1].wait()
+    for copy in copies[:3]:
+        copy.wait()
+    for n in range(ids_ref.shape[0]):
+        line = jnp.broadcast_to(ids_ref[n : n + 1, :], (LANES, LANES))
+        id_ref[n * LANES : (n + 1) * LANES, :] = line.T
+    target_out[...] = jnp.concatenate([target_ref[n : n + 1, :] for n in range(rows // LANES)], 1)
     pad = jnp.concatenate([pad_ref[n : n + 1, :] for n in range(rows // LANES)], 1)
     flags = jnp.broadcast_to(pad, (FLAG_ROWS, rows)).astype(F32).astype(BF16)
     own_ref[2 * cols :, :] = flags
     edge_ref[2 * cols :, :] = flags[:, rows - WIN :]
-    for copy in copies[:3]:
+    for copy in copies[3:]:
         copy.wait()
-    for n, start in enumerate(starts):
-        copies[3 + n].wait()
+    gain_here = gain_row[:, here]
+    gain_out[...] = gain_here
+    pos_out[...] = (pos[...].astype(F32) * gain_here).T
+    for start in starts:
         out = dot_last(hist[start : start + step, :], weights[...])
         q_ref[start : start + step, :] = out[:, :cols].astype(BF16)
         kv = out[:, cols:].T.astype(BF16)
@@ -84,29 +132,46 @@
             edge_ref[: 2 * cols, at : at + step] = kv
 
 
-def project(history, w_query, w_key, w_value, pad_mask):
+def front(history, w_query, w_key, w_value, pad_mask, pos_emb, norm_gain, neg_ids, target_ids, w_out, share):
     rows, width = history.shape
+    negs = neg_ids.shape[0]
+    half = w_out.shape[0] // 2
     cols = w_query.shape[1]
     tall = 2 * cols + FLAG_ROWS
-    return pl.pallas_call(
-        project_body,
-        name="project",
+    if share % LANES:
+        pos_emb = lax.dynamic_slice_in_dim(pos_emb, lax.axis_index("head") * share, share, 1)
+    by_lanes = lambda a: a.reshape(-1, LANES)
+    return pl.pallas_call(
+        front_body,
+        name="front",
         out_shape=(
             jax.ShapeDtypeStruct((rows, cols), BF16),
             jax.ShapeDtypeStruct((tall, rows), BF16),
             jax.ShapeDtypeStruct((tall, WIN), BF16),
+            jax.ShapeDtypeStruct((negs, LANES), jnp.int32),
+            jax.ShapeDtypeStruct((share, rows), F32),
+            jax.ShapeDtypeStruct((1, share), F32),
+            jax.ShapeDtypeStruct((1, rows), jnp.int32),
+            jax.ShapeDtypeStruct((1, width), F32),
+            jax.ShapeDtypeStruct((half, width), BF16),
         ),
-        in_specs=[RAW] * 5,
-        out_specs=(WHOLE, WHOLE, WHOLE),
+        in_specs=[RAW] * 10,
+        out_specs=(WHOLE,) * 9,
         scratch_shapes=[
             pltpu.VMEM((rows, width), BF16),
             pltpu.VMEM((3 * cols, width), BF16),
+            pltpu.VMEM((rows, share), BF16),
             pltpu.VMEM((rows // LANES, LANES), jnp.int32),
-            pltpu.SemaphoreType.DMA((4 + rows // LANES,)),
+            pltpu.VMEM((negs // LANES, LANES), jnp.int32),
+            pltpu.VMEM((rows // LANES, LANES), jnp.int32),
+            pltpu.SemaphoreType.DMA((9 + rows // LANES,)),
         ],
-        compiler_params=pltpu.CompilerParams(vmem_limit_bytes=8 * MIB),
-        cost_estimate=pl.CostEstimate(flops=6 * rows * width * cols, bytes_accessed=2 * rows * width, transcendentals=0),
-    )(*stay(history, w_query.T, w_key.T, w_value.T, pad_mask.reshape(-1, LANES)))
+        compiler_params=pltpu.CompilerParams(vmem_limit_bytes=12 * MIB),
+        cost_estimate=pl.CostEstimate(flops=AHEAD, bytes_accessed=4 * rows * width, transcendentals=0),
+    )(
+        *stay(history, w_query.T, w_key.T, w_value.T, by_lanes(pad_mask)),
+        *stay(pos_emb, norm_gain[None, :], by_lanes(neg_ids), by_lanes(target_ids), w_out),
+    )
 
 
 def attend_body(q_ref, own_ref, prev_ref, out_ref):
@@ -150,122 +215,55 @@
         in_specs=[WHOLE] * 3,
         out_specs=WHOLE,
         compiler_params=pltpu.CompilerParams(vmem_limit_bytes=8 * MIB),
-        cost_estimate=pl.CostEstimate(flops=4 * rows * 2 * WIN * cols, bytes_accessed=6 * rows * cols, transcendentals=rows * 2 * WIN),
+        cost_estimate=pl.CostEstimate(flops=AHEAD, bytes_accessed=6 * rows * cols, transcendentals=rows * 2 * WIN),
     )(query, own, prev)
 
 
-def prepare_body(pos_hbm, gain_hbm, ids_hbm, target_hbm, own_hbm, neg_hbm, id_ref, pos_out, gain_out, target_out, own_out, all_out, neg_out, pos, ids_ref, target_ref, sems):
-    rows, share = pos.shape
-    here = pl.ds(0, share)
-    if pos_hbm.shape[1] != share:
-        here = pl.ds(pl.multiple_of(lax.axis_index("head") * share, share), share)
-    moves = (
-        (ids_hbm, ids_ref),
-        (target_hbm, target_ref),
-        (gain_hbm, all_out),
-        (pos_hbm.at[:, here], pos),
-        (own_hbm, own_out),
-        (neg_hbm.at[pl.ds(0, neg_out.shape[0])], neg_out),
-    )
-    copies = [pltpu.make_async_copy(a, b, sems.at[n]) for n, (a, b) in enumerate(moves)]
-    for copy in copies:
-        copy.start()
-    copies[0].wait()
-    copies[1].wait()
-    target_out[...] = jnp.concatenate([target_ref[n : n + 1, :] for n in range(rows // LANES)], 1)
-    for n in range(ids_ref.shape[0]):
-        line = jnp.broadcast_to(ids_ref[n : n + 1, :], (LANES, LANES))
-        id_ref[n * LANES : (n + 1) * LANES, :] = line.T
-    copies[2].wait()
-    copies[3].wait()
-    gain = all_out[:, here]
-    gain_out[...] = gain
-    pos_out[...] = (pos[...].astype(F32) * gain).T
-    copies[4].wait()
-    copies[5].wait()
-
-
-def prepare(pos_emb, norm_gain, neg_ids, target_ids, own, neg_emb, share):
-    rows, width = pos_emb.shape
-    negs = neg_ids.shape[0]
-    if share % LANES:
-        pos_emb = lax.dynamic_slice_in_dim(pos_emb, lax.axis_index("head") * share, share, 1)
-    return pl.pallas_call(
-        prepare_body,
-        name="prepare",
-        out_shape=(
-            jax.ShapeDtypeStruct((negs, LANES), jnp.int32),
-            jax.ShapeDtypeStruct((share, rows), F32),
-            jax.ShapeDtypeStruct((1, share), F32),
-            jax.ShapeDtypeStruct((1, rows), jnp.int32),
-            jax.ShapeDtypeStruct(own.shape, BF16),
-            jax.ShapeDtypeStruct((1, width), F32),
-            jax.ShapeDtypeStruct((negs // 2, width), BF16),
-        ),
-        in_specs=[RAW] * 6,
-        out_specs=(WHOLE,) * 7,
-        scratch_shapes=[
-            pltpu.VMEM((rows, share), BF16),
-            pltpu.VMEM((negs // LANES, LANES), jnp.int32),
-            pltpu.VMEM((rows // LANES, LANES), jnp.int32),
-            pltpu.SemaphoreType.DMA((6,)),
-        ],
-        compiler_params=pltpu.CompilerParams(vmem_limit_bytes=12 * MIB),
-        cost_estimate=pl.CostEstimate(flops=rows * share, bytes_accessed=negs * width, transcendentals=0),
-    )(*stay(pos_emb, norm_gain[None, :], neg_ids.reshape(-1, LANES), target_ids.reshape(-1, LANES), own, neg_emb))
-
-
-def premix_body(count, neg_hbm, first_ref, gain_ref, *refs):
-    pieces, (mix_ref, turned_ref, scaled, negs, sems) = refs[:count], refs[count:]
-    ahead, width = first_ref.shape
-    tall = pieces[0].shape[0]
+def premix_body(count, split, neg_ref, gain_ref, own_ref, *refs):
+    far, near, (mix_ref, turned_ref, scaled, held) = refs[:split[0]], refs[split[0] : sum(split)], refs[sum(split) :]
+    total, width = neg_ref.shape
+    tall = own_ref.shape[0]
     block = 256
-    copies = {}
-    for n, start in enumerate(range(0, negs.shape[0], block)):
-        copies[ahead + start] = pltpu.make_async_copy(
-            neg_hbm.at[pl.ds(ahead + start, block)], negs.at[pl.ds(start, block)], sems.at[n]
-        )
-    for copy in copies.values():
-        copy.start()
     gain = gain_ref[...]
+    first = lax.axis_index("seq") % 2 == 0
+    pieces = [own_ref]
+    for k in range(1, count):
+        if not near:
+            pieces.append(far[k - 1])
+            continue
+        mine, theirs = far[(k - 1) // 2][...], near[(k - 1) // 2][...]
+        even, odd = jnp.where(first, mine, theirs), jnp.where(first, theirs, mine)
+        held[k - 1] = jnp.concatenate([even, odd], 0) if k == count - 1 else even if k % 2 else odd
+        pieces.append(held.at[k - 1])
     for k in range(count):
         scaled[k * tall : (k + 1) * tall, :] = (pieces[k][...].astype(F32) * gain).astype(BF16)
-    total = ahead + negs.shape[0]
     turn = width // (total // block)
     for n, start in enumerate(range(0, total, block)):
-        if start < ahead:
-            part = first_ref[start : start + block, :]
-        else:
-            copies[start].wait()
-            part = negs[start - ahead : start - ahead + block, :]
+        part = neg_ref[start : start + block, :]
         mix_ref[start : start + block, :] = dot_last(part, scaled[...]).astype(BF16)
         cols = slice(n * turn, (n + 1) * turn)
         whole = jnp.concatenate([ref[:, cols].astype(F32) for ref in pieces], 0)
         turned_ref[cols, :] = whole.T.astype(BF16)
 
 
-def premix(neg_emb, first, gain_row, pieces):
+def premix(neg_emb, gain_row, own, far, near):
     negs, width = neg_emb.shape
-    count = len(pieces)
-    deep = count * pieces[0].shape[0]
-    rest = negs - first.shape[0]
-    return pl.pallas_call(
-        functools.partial(premix_body, count),
+    count = lax.axis_size("head")
+    tall = own.shape[0]
+    deep = count * tall
+    return pl.pallas_call(
+        functools.partial(premix_body, count, (len(far), len(near))),
         name="premix",
         out_shape=(
             jax.ShapeDtypeStruct((negs, deep), BF16),
             jax.ShapeDtypeStruct((width, deep), BF16),
         ),
-        in_specs=[RAW] + [WHOLE] * (2 + count),
+        in_specs=[WHOLE] * (3 + len(far) + len(near)),
         out_specs=(WHOLE, WHOLE),
-        scratch_shapes=[
-            pltpu.VMEM((deep, width), BF16),
-            pltpu.VMEM((rest, width), BF16),
-            pltpu.SemaphoreType.DMA((rest // 256,)),
-        ],
-        compiler_params=pltpu.CompilerParams(vmem_limit_bytes=28 * MIB),
+        scratch_shapes=[pltpu.VMEM((deep, width), BF16), pltpu.VMEM((count - 1, tall, width), BF16)],
+        compiler_params=pltpu.CompilerParams(vmem_limit_bytes=20 * MIB),
         cost_estimate=pl.CostEstimate(flops=2 * negs * width * deep, bytes_accessed=2 * negs * width, transcendentals=0),
-    )(*stay(neg_emb), first, gain_row, *pieces)
+    )(neg_emb, gain_row, own, *far, *near)
 
 
 def score_body(count, *refs):
@@ -356,15 +354,15 @@
 ):
     width = history.shape[1]
     count = lax.axis_size("head")
-    query, own, edge = project(history, w_query, w_key, w_value, pad_mask)
+    query, own, edge, id_cols, pos_turned, gain_here, target, gain_row, half = front(
+        history, w_query, w_key, w_value, pad_mask, pos_emb, norm_gain, neg_ids, target_ids, w_out, width // count
+    )
     prev = from_behind(edge, "seq", 1)
-    pieces = from_all(w_out, "head")
-    id_cols, pos_turned, gain_here, target, pieces[0], gain_row, first = prepare(
-        pos_emb, norm_gain, neg_ids, target_ids, w_out, neg_emb, width // count
-    )
+    far = fetch_in_pairs(w_out, half)
     mine = attend(query, own, prev)
     heads = from_all(mine, "head")
-    mix, turned = premix(neg_emb, first, gain_row, pieces)
+    near = swap_in_pairs(far, count)
+    mix, turned = premix(neg_emb, gain_row, w_out, far, near)
     stats, user = score(heads, mix, turned, id_cols, pos_turned, target)
     all_stats = from_all(stats, "head")
     user_share = finish(user, gain_here)

time: 35.7 us -> 33.6 us (0.941)
  the two profiles are of different devices: /device:TPU:4 before, /device:TPU:0 now
where the time goes in v4:
time: 33.6 us; the launch traced here: 33.4 us
  starting transfers between devices  16.4 us (49%)
  waiting for transfers between devices  8.3 us (25%)
  Pallas kernels  7.3 us (22%)
  between operations  0.69 us (2%)
  other arithmetic  0.66 us (2%)
    ppermute x6, starting transfers between devices, from_all(): pieces.append(lax.ppermute(shard, axis, pairs))  8.91 us
    ppermute x2, waiting for transfers between devices, fetch_in_pairs(): far.append(lax.ppermute(half if last else shard, ('seq', 'head'), route))  5.46 us
    ppermute x2, starting transfers between devices, fetch_in_pairs(): far.append(lax.ppermute(half if last else shard, ('seq', 'head'), route))  4.53 us
    ppermute x6, waiting for transfers between devices, from_all(): pieces.append(lax.ppermute(shard, axis, pairs))  2.83 us
    ppermute x1, starting transfers between devices, from_behind(): return lax.ppermute(shard, axis, pairs)  2.48 us
    pallas_call x1, Pallas kernels, front(): pl.pallas_call(front_body, name='front', out_shape=(jax.ShapeDtypeStruct(...  2.38 us
    pallas_call x1, Pallas kernels, score(): pl.pallas_call(functools.partial(score_body, count), name='score', out_sh...  1.58 us
    pallas_call x1, Pallas kernels, premix(): pl.pallas_call(functools.partial(premix_body, count, (len(far), len(near)...  1.33 us
  transfers between devices with their start and end apart: 11, of which 5 were waited for; matrix products, arithmetic and copies ran while one was open for 0% of the time, Pallas kernels for 17%

profile of v4, /device:TPU:0, one launch (start us, length us, event | category | flops | bytes accessed | tf_op | source)
XLA Modules:
  0.0 33.4 jit_solution(16758317796578480778)
XLA Ops:
  0.6 3.1 %collective-permute-start.4 = (bf16[64,1024]{1,0:T(8,128)(2,1)}, bf16[64,1024]{1,0:T(8,128)(2,1)S(1)}, u32[]{:S(2)}, u32[]{:S(2)}) collective-permute-start(bf16[64,1024]{1,0:T(8,128)(2,1)} %own_ref.1), channel_id=1, source_target_pairs={{0,1},{1,0},{2,3},{3,2},{4,6},{5,7},{6,4},{7,5},{8,9},{9,8},{10,11... | collective-permute-start | bytes 393224 | tf_op jit(solution)/shard_map/ppermute | solution.py:72
  3.8 2.4 %front.1 = (bf16[384,64]{1,0:T(8,128)(2,1)S(1)}, bf16[144,384]{1,0:T(8,128)(2,1)S(1)}, bf16[144,256]{1,0:T(8,128)(2,1)S(1)}, s32[2048,128]{1,0:T(8,128)S(1)}, f3...) custom-call(bf16[384,1024]{1,0:T(8,128)(2,1)} %refs_0_.1, ...), custom_call_target="tpu_custom_call" | custom-call | flops 4000000000 | bytes 1572864 | tf_op jit(solution)/shard_map/front/pallas_call | solution.py:144
  6.1 2.5 %collective-permute-start = (bf16[144,256]{1,0:T(8,128)(2,1)S(1)}, bf16[144,256]{1,0:T(8,128)(2,1)S(1)}, u32[]{:S(2)}, u32[]{:S(2)}) collective-permute-start(bf16[144,256]{1,0:T(8,128)(2,1)S(1)} %get-tuple-element.17), channel_id=1, source_target_pairs={{0,4},{4,8},{8,12},{12,16},{16,20},{20,24},{24,28},{1,5},{5,9},{9,... | collective-permute-start | bytes 221192 | tf_op jit(solution)/shard_map/ppermute | solution.py:39
  8.6 1.4 %collective-permute-start.5 = (bf16[32,1024]{1,0:T(8,128)(2,1)S(1)}, bf16[32,1024]{1,0:T(8,128)(2,1)S(1)}, u32[]{:S(2)}, u32[]{:S(2)}) collective-permute-start(bf16[32,1024]{1,0:T(8,128)(2,1)S(1)} %get-tuple-element.19), channel_id=1, source_target_pairs={{0,3},{1,2},{2,1},{3,0},{4,7},{5,6},{6,5},{7,4},{8,11},{9,10},{10,... | collective-permute-start | bytes 196616 | tf_op jit(solution)/shard_map/ppermute | solution.py:72
  10.0 5.5 %collective-permute-done.5.refs_1_ = bf16[32,1024]{1,0:T(8,128)(2,1)S(1)} collective-permute-done((bf16[32,1024]{1,0:T(8,128)(2,1)S(1)}, bf16[32,1024]{1,0:T(8,128)(2,1)S(1)}, u32[]{:S(2)}, u32[]{:S(2)}) %collective-permute-start.5) | collective-permute-done | bytes 65568 | tf_op jit(solution)/shard_map/ppermute | solution.py:72
  15.5 0.1 collective-permute-start.7
  15.5 0.0 collective-permute-done.4.refs_0_
  15.5 0.5 %collective-permute-start.6 = (bf16[64,1024]{1,0:T(8,128)(2,1)S(1)}, bf16[64,1024]{1,0:T(8,128)(2,1)S(1)}, u32[]{:S(2)}, u32[]{:S(2)}) collective-permute-start(bf16[64,1024]{1,0:T(8,128)(2,1)S(1)} %collective-permute-done.4.refs_0_), channel_id=1, source_target_pairs={{0,4},{4,0},{8,12},{12,8},{16,20},{20,16},{24,28},{28,24},{1,5},{5... | collective-permute-start | bytes 393224 | tf_op jit(solution)/shard_map/ppermute | solution.py:82
  16.0 0.0 collective-permute-done.prev_ref
  16.0 0.0 copy-start
  16.0 0.0 copy-start.1
  16.0 1.2 %attend.1.refs_0_ = bf16[64,384]{1,0:T(8,128)(2,1)S(1)} custom-call(bf16[384,64]{1,0:T(8,128)(2,1)S(1)} %get-tuple-element.15.q_ref, bf16[144,384]{1,0:T(8,128)(2,1)S(1)} %get-tuple-element.16.own_ref, bf16[144,256]{1,0:T(8,128)(2,1)S(1)} %collective-permute-done.prev_ref), custom_call_target="tpu_custom_call" | custom-call | flops 4000000000 | bytes 147456 | tf_op jit(solution)/shard_map/attend/pallas_call | solution.py:211
  17.2 1.3 %collective-permute-start.3 = (bf16[64,384]{1,0:T(8,128)(2,1)S(1)}, bf16[64,384]{1,0:T(8,128)(2,1)S(1)}, u32[]{:S(2)}, u32[]{:S(2)}) collective-permute-start(bf16[64,384]{1,0:T(8,128)(2,1)S(1)} %attend.1.refs_0_), channel_id=1, source_target_pairs={{0,3},{1,2},{2,1},{3,0},{4,7},{5,6},{6,5},{7,4},{8,11},{9,10},{10,... | collective-permute-start | bytes 147464 | tf_op jit(solution)/shard_map/ppermute | solution.py:52
  18.5 1.3 %collective-permute-start.2 = (bf16[64,384]{1,0:T(8,128)(2,1)S(1)}, bf16[64,384]{1,0:T(8,128)(2,1)S(1)}, u32[]{:S(2)}, u32[]{:S(2)}) collective-permute-start(bf16[64,384]{1,0:T(8,128)(2,1)S(1)} %attend.1.refs_0_), channel_id=1, source_target_pairs={{0,2},{1,3},{2,0},{3,1},{4,6},{5,7},{6,4},{7,5},{8,10},{9,11},{10,... | collective-permute-start | bytes 147464 | tf_op jit(solution)/shard_map/ppermute | solution.py:52
  19.8 1.9 %collective-permute-start.1 = (bf16[64,384]{1,0:T(8,128)(2,1)S(1)}, bf16[64,384]{1,0:T(8,128)(2,1)S(1)}, u32[]{:S(2)}, u32[]{:S(2)}) collective-permute-start(bf16[64,384]{1,0:T(8,128)(2,1)S(1)} %attend.1.refs_0_), channel_id=1, source_target_pairs={{0,1},{1,0},{2,3},{3,2},{4,5},{5,4},{6,7},{7,6},{8,9},{9,8},{10,11... | collective-permute-start | bytes 147464 | tf_op jit(solution)/shard_map/ppermute | solution.py:52
  21.6 0.0 collective-permute-done.7.refs_3_
  21.6 0.0 collective-permute-done.6.refs_2_
  21.7 0.0 copy-done
  21.7 0.0 copy-done.1
  21.7 1.3 %premix.1 = (bf16[2048,256]{1,0:T(8,128)(2,1)S(1)}, bf16[1024,256]{1,0:T(8,128)(2,1)S(1)}) custom-call(bf16[2048,1024]{1,0:T(8,128)(2,1)S(1)} %copy-done, f32[1,1024]{1,0:T(1,128)S(1)} %get-tuple-element.18.gain_ref, bf16[64,1024]{1,0:T(8,128)(2,1)S(1)} %copy-done.1, bf16[64,1024]{1,0:T(8,128)(2,1)S(1)} %collective-permute-done.4.refs_0_, ...), custom_call_target="tpu_custom_call" | custom-call | flops 1073741824 | bytes 4194304 | tf_op jit(solution)/shard_map/premix/pallas_call | solution.py:254
  23.0 0.4 %collective-permute-done.3.refs_3_ = bf16[64,384]{1,0:T(8,128)(2,1)S(1)} collective-permute-done((bf16[64,384]{1,0:T(8,128)(2,1)S(1)}, bf16[64,384]{1,0:T(8,128)(2,1)S(1)}, u32[]{:S(2)}, u32[]{:S(2)}) %collective-permute-start.3) | collective-permute-done | bytes 49184 | tf_op jit(solution)/shard_map/ppermute | solution.py:52
  23.4 1.6 %collective-permute-done.2.refs_2_ = bf16[64,384]{1,0:T(8,128)(2,1)S(1)} collective-permute-done((bf16[64,384]{1,0:T(8,128)(2,1)S(1)}, bf16[64,384]{1,0:T(8,128)(2,1)S(1)}, u32[]{:S(2)}, u32[]{:S(2)}) %collective-permute-start.2) | collective-permute-done | bytes 49184 | tf_op jit(solution)/shard_map/ppermute | solution.py:52
  25.0 0.0 collective-permute-done.1.refs_1_
  25.0 1.6 %score.1 = (f32[4,384]{1,0:T(4,128)S(1)}, f32[256,384]{1,0:T(8,128)S(1)}) custom-call(bf16[64,384]{1,0:T(8,128)(2,1)S(1)} %attend.1.refs_0_, bf16[64,384]{1,0:T(8,128)(2,1)S(1)} %collective-permute-done.1.refs_1_, bf16[64,384]{1,0:T(8,128)(2,1)S(1)} %collective-permute-done.2.refs_2_, bf16[64,384]{1,0:T(8,128)(2,1)S(1)} %collective-permute-done.3.refs_3_, ...), custom_call_target="tpu_custom_call" | custom-call | flops 603979776 | bytes 1048576 | tf_op jit(solution)/shard_map/score/pallas_call | solution.py:310
  26.6 1.6 %collective-permute-start.10 = (f32[4,384]{1,0:T(4,128)S(1)}, f32[4,384]{1,0:T(4,128)S(1)}, u32[]{:S(2)}, u32[]{:S(2)}) collective-permute-start(f32[4,384]{1,0:T(4,128)S(1)} %get-tuple-element.27), channel_id=1, source_target_pairs={{0,3},{1,2},{2,1},{3,0},{4,7},{5,6},{6,5},{7,4},{8,11},{9,10},{10,... | collective-permute-start | bytes 18440 | tf_op jit(solution)/shard_map/ppermute | solution.py:52
  28.2 0.7 %collective-permute-start.9 = (f32[4,384]{1,0:T(4,128)S(1)}, f32[4,384]{1,0:T(4,128)S(1)}, u32[]{:S(2)}, u32[]{:S(2)}) collective-permute-start(f32[4,384]{1,0:T(4,128)S(1)} %get-tuple-element.27), channel_id=1, source_target_pairs={{0,2},{1,3},{2,0},{3,1},{4,6},{5,7},{6,4},{7,5},{8,10},{9,11},{10,... | collective-permute-start | bytes 18440 | tf_op jit(solution)/shard_map/ppermute | solution.py:52
  28.8 2.2 %collective-permute-start.8 = (f32[4,384]{1,0:T(4,128)S(1)}, f32[4,384]{1,0:T(4,128)S(1)}, u32[]{:S(2)}, u32[]{:S(2)}) collective-permute-start(f32[4,384]{1,0:T(4,128)S(1)} %get-tuple-element.27), channel_id=1, source_target_pairs={{0,1},{1,0},{2,3},{3,2},{4,5},{5,4},{6,7},{7,6},{8,9},{9,8},{10,11... | collective-permute-start | bytes 18440 | tf_op jit(solution)/shard_map/ppermute | solution.py:52
  31.0 0.8 %finish.1 = bf16[384,256]{1,0:T(8,128)(2,1)} custom-call(f32[256,384]{1,0:T(8,128)S(1)} %get-tuple-element.25.user_ref, f32[1,256]{1,0:T(1,128)S(1)} %get-tuple-element.26.gain_ref), custom_call_target="tpu_custom_call" | custom-call | flops 196608 | bytes 589824 | tf_op jit(solution)/shard_map/finish/pallas_call | solution.py:331
  31.9 0.2 collective-permute-done.10
  32.1 0.6 %collective-permute-done.9 = f32[4,384]{1,0:T(4,128)S(1)} collective-permute-done((f32[4,384]{1,0:T(4,128)S(1)}, f32[4,384]{1,0:T(4,128)S(1)}, u32[]{:S(2)}, u32[]{:S(2)}) %collective-permute-start.9) | collective-permute-done | bytes 6176 | tf_op jit(solution)/shard_map/ppermute | solution.py:52
  32.7 0.0 collective-permute-done.8
  32.7 0.1 slice_reduce_fusion.7
  32.8 0.6 %add_subtract_fusion = f32[384]{0:T(512)} fusion(f32[384]{0:T(512)S(1)} %get-tuple-element.30, f32[384]{0:T(512)S(1)} %get-tuple-element.36, f32[384]{0:T(512)S(1)} %get-tuple-element.35, f32[384]{0:T(512)S(1)} %get-tuple-element.34, f32[384]{0:T(512)S(1)} %get-tuple-element.33, f32[384]{0:T(512)S(1)} %get-tuple-element.32, f32[384]{0:T(512)S(1)} %get-tuple-element.31, ...), kind=kLoop, calls=%fused_computation | loop fusion | flops 7296 | bytes 15360 | tf_op jit(solution)/shard_map/sub | solution.py:372
Async XLA Ops:
  0.6 14.9 %collective-permute-start.4 = (bf16[64,1024]{1,0:T(8,128)(2,1)}, bf16[64,1024]{1,0:T(8,128)(2,1)S(1)}, u32[]{:S(2)}, u32[]{:S(2)}) collective-permute-start(bf16[64,1024]{1,0:T(8,128)(2,1)} %own_ref.1), channel_id=1, source_target_pairs={{0,1},{1,0},{2,3},{3,2},{4,6},{5,7},{6,4},{7,5},{8,9},{9,8},{10,11... | collective-permute-start | bytes 393224 | tf_op jit(solution)/shard_map/ppermute | solution.py:72
  6.1 9.9 %collective-permute-start = (bf16[144,256]{1,0:T(8,128)(2,1)S(1)}, bf16[144,256]{1,0:T(8,128)(2,1)S(1)}, u32[]{:S(2)}, u32[]{:S(2)}) collective-permute-start(bf16[144,256]{1,0:T(8,128)(2,1)S(1)} %get-tuple-element.17), channel_id=1, source_target_pairs={{0,4},{4,8},{8,12},{12,16},{16,20},{20,24},{24,28},{1,5},{5,9},{9,... | collective-permute-start | bytes 221192 | tf_op jit(solution)/shard_map/ppermute | solution.py:39
  8.6 6.9 %collective-permute-start.5 = (bf16[32,1024]{1,0:T(8,128)(2,1)S(1)}, bf16[32,1024]{1,0:T(8,128)(2,1)S(1)}, u32[]{:S(2)}, u32[]{:S(2)}) collective-permute-start(bf16[32,1024]{1,0:T(8,128)(2,1)S(1)} %get-tuple-element.19), channel_id=1, source_target_pairs={{0,3},{1,2},{2,1},{3,0},{4,7},{5,6},{6,5},{7,4},{8,11},{9,10},{10,... | collective-permute-start | bytes 196616 | tf_op jit(solution)/shard_map/ppermute | solution.py:72
  15.5 6.2 %collective-permute-start.7 = (bf16[32,1024]{1,0:T(8,128)(2,1)S(1)}, bf16[32,1024]{1,0:T(8,128)(2,1)S(1)}, u32[]{:S(2)}, u32[]{:S(2)}) collective-permute-start(bf16[32,1024]{1,0:T(8,128)(2,1)S(1)} %collective-permute-done.5.refs_1_), channel_id=1, source_target_pairs={{0,4},{4,0},{8,12},{12,8},{16,20},{20,16},{24,28},{28,24},{1,5},{5... | collective-permute-start | bytes 196616 | tf_op jit(solution)/shard_map/ppermute | solution.py:82
  15.5 6.1 %collective-permute-start.6 = (bf16[64,1024]{1,0:T(8,128)(2,1)S(1)}, bf16[64,1024]{1,0:T(8,128)(2,1)S(1)}, u32[]{:S(2)}, u32[]{:S(2)}) collective-permute-start(bf16[64,1024]{1,0:T(8,128)(2,1)S(1)} %collective-permute-done.4.refs_0_), channel_id=1, source_target_pairs={{0,4},{4,0},{8,12},{12,8},{16,20},{20,16},{24,28},{28,24},{1,5},{5... | collective-permute-start | bytes 393224 | tf_op jit(solution)/shard_map/ppermute | solution.py:82
  16.0 5.6 %copy-start = (bf16[2048,1024]{1,0:T(8,128)(2,1)S(1)}, bf16[2048,1024]{1,0:T(8,128)(2,1)}, u32[]{:S(2)}) copy-start(bf16[2048,1024]{1,0:T(8,128)(2,1)} %neg_ref.1) | copy-start | bytes 12582916
  16.0 5.7 %copy-start.1 = (bf16[64,1024]{1,0:T(8,128)(2,1)S(1)}, bf16[64,1024]{1,0:T(8,128)(2,1)}, u32[]{:S(2)}) copy-start(bf16[64,1024]{1,0:T(8,128)(2,1)} %own_ref.1) | copy-start | bytes 393220
  17.2 6.2 %collective-permute-start.3 = (bf16[64,384]{1,0:T(8,128)(2,1)S(1)}, bf16[64,384]{1,0:T(8,128)(2,1)S(1)}, u32[]{:S(2)}, u32[]{:S(2)}) collective-permute-start(bf16[64,384]{1,0:T(8,128)(2,1)S(1)} %attend.1.refs_0_), channel_id=1, source_target_pairs={{0,3},{1,2},{2,1},{3,0},{4,7},{5,6},{6,5},{7,4},{8,11},{9,10},{10,... | collective-permute-start | bytes 147464 | tf_op jit(solution)/shard_map/ppermute | solution.py:52
  18.5 6.5 %collective-permute-start.2 = (bf16[64,384]{1,0:T(8,128)(2,1)S(1)}, bf16[64,384]{1,0:T(8,128)(2,1)S(1)}, u32[]{:S(2)}, u32[]{:S(2)}) collective-permute-start(bf16[64,384]{1,0:T(8,128)(2,1)S(1)} %attend.1.refs_0_), channel_id=1, source_target_pairs={{0,2},{1,3},{2,0},{3,1},{4,6},{5,7},{6,4},{7,5},{8,10},{9,11},{10,... | collective-permute-start | bytes 147464 | tf_op jit(solution)/shard_map/ppermute | solution.py:52
  19.8 5.2 %collective-permute-start.1 = (bf16[64,384]{1,0:T(8,128)(2,1)S(1)}, bf16[64,384]{1,0:T(8,128)(2,1)S(1)}, u32[]{:S(2)}, u32[]{:S(2)}) collective-permute-start(bf16[64,384]{1,0:T(8,128)(2,1)S(1)} %attend.1.refs_0_), channel_id=1, source_target_pairs={{0,1},{1,0},{2,3},{3,2},{4,5},{5,4},{6,7},{7,6},{8,9},{9,8},{10,11... | collective-permute-start | bytes 147464 | tf_op jit(solution)/shard_map/ppermute | solution.py:52
  26.6 5.5 %collective-permute-start.10 = (f32[4,384]{1,0:T(4,128)S(1)}, f32[4,384]{1,0:T(4,128)S(1)}, u32[]{:S(2)}, u32[]{:S(2)}) collective-permute-start(f32[4,384]{1,0:T(4,128)S(1)} %get-tuple-element.27), channel_id=1, source_target_pairs={{0,3},{1,2},{2,1},{3,0},{4,7},{5,6},{6,5},{7,4},{8,11},{9,10},{10,... | collective-permute-start | bytes 18440 | tf_op jit(solution)/shard_map/ppermute | solution.py:52
  28.2 4.5 %collective-permute-start.9 = (f32[4,384]{1,0:T(4,128)S(1)}, f32[4,384]{1,0:T(4,128)S(1)}, u32[]{:S(2)}, u32[]{:S(2)}) collective-permute-start(f32[4,384]{1,0:T(4,128)S(1)} %get-tuple-element.27), channel_id=1, source_target_pairs={{0,2},{1,3},{2,0},{3,1},{4,6},{5,7},{6,4},{7,5},{8,10},{9,11},{10,... | collective-permute-start | bytes 18440 | tf_op jit(solution)/shard_map/ppermute | solution.py:52
  28.8 3.9 %collective-permute-start.8 = (f32[4,384]{1,0:T(4,128)S(1)}, f32[4,384]{1,0:T(4,128)S(1)}, u32[]{:S(2)}, u32[]{:S(2)}) collective-permute-start(f32[4,384]{1,0:T(4,128)S(1)} %get-tuple-element.27), channel_id=1, source_target_pairs={{0,1},{1,0},{2,3},{3,2},{4,5},{5,4},{6,7},{7,6},{8,9},{9,8},{10,11... | collective-permute-start | bytes 18440 | tf_op jit(solution)/shard_map/ppermute | solution.py:52

commit v5 on v4

--- a/solution.py
+++ b/solution.py
@@ -84,63 +84,43 @@
 
 
 def front_body(*refs):
-    hist_hbm, wq_hbm, wk_hbm, wv_hbm, pad_hbm, pos_hbm, gain_hbm, ids_hbm, target_hbm, out_hbm = refs[:10]
-    q_ref, own_ref, edge_ref, id_ref, pos_out, gain_out, target_out, gain_row, half_ref = refs[10:19]
-    hist, weights, pos, pad_ref, ids_ref, target_ref, sems = refs[19:]
+    hist_hbm, wq_hbm, wk_hbm, wv_hbm, pad_hbm, out_hbm = refs[:6]
+    q_ref, own_ref, edge_ref, half_ref = refs[6:10]
+    hist, weights, pad_ref, sems = refs[10:]
     rows, _ = hist.shape
     cols = wq_hbm.shape[0]
-    share = pos.shape[1]
     step = LANES
-    here = pl.ds(0, share)
-    if pos_hbm.shape[1] != share:
-        here = pl.ds(pl.multiple_of(lax.axis_index("head") * share, share), share)
     starts = list(range(0, rows, step))[::-1]
-    moves = [(ids_hbm, ids_ref), (target_hbm, target_ref), (pad_hbm, pad_ref), (gain_hbm, gain_row)]
-    moves.append((pos_hbm.at[:, here], pos))
     half = half_ref.shape[0]
     part = lax.axis_index("seq") % (out_hbm.shape[0] // half)
-    moves.append((out_hbm.at[pl.ds(pl.multiple_of(part * half, half), half)], half_ref))
+    moves = [(pad_hbm, pad_ref)]
     for n, source in enumerate((wq_hbm, wk_hbm, wv_hbm)):
         moves.append((source, weights.at[pl.ds(n * cols, cols)]))
     for start in starts:
         moves.append((hist_hbm.at[pl.ds(start, step)], hist.at[pl.ds(start, step)]))
+    moves.append((out_hbm.at[pl.ds(pl.multiple_of(part * half, half), half)], half_ref))
     copies = [pltpu.make_async_copy(a, b, sems.at[n]) for n, (a, b) in enumerate(moves)]
     for copy in copies:
         copy.start()
-    for copy in copies[:3]:
-        copy.wait()
-    for n in range(ids_ref.shape[0]):
-        line = jnp.broadcast_to(ids_ref[n : n + 1, :], (LANES, LANES))
-        id_ref[n * LANES : (n + 1) * LANES, :] = line.T
-    target_out[...] = jnp.concatenate([target_ref[n : n + 1, :] for n in range(rows // LANES)], 1)
+    copies[0].wait()
     pad = jnp.concatenate([pad_ref[n : n + 1, :] for n in range(rows // LANES)], 1)
     flags = jnp.broadcast_to(pad, (FLAG_ROWS, rows)).astype(F32).astype(BF16)
     own_ref[2 * cols :, :] = flags
     edge_ref[2 * cols :, :] = flags[:, rows - WIN :]
-    for copy in copies[3:]:
+    for copy in copies[1:]:
         copy.wait()
-    gain_here = gain_row[:, here]
-    gain_out[...] = gain_here
-    pos_out[...] = (pos[...].astype(F32) * gain_here).T
-    for start in starts:
-        out = dot_last(hist[start : start + step, :], weights[...])
-        q_ref[start : start + step, :] = out[:, :cols].astype(BF16)
-        kv = out[:, cols:].T.astype(BF16)
-        own_ref[: 2 * cols, start : start + step] = kv
-        if start >= rows - WIN:
-            at = start - (rows - WIN)
-            edge_ref[: 2 * cols, at : at + step] = kv
-
-
-def front(history, w_query, w_key, w_value, pad_mask, pos_emb, norm_gain, neg_ids, target_ids, w_out, share):
+    out = dot_last(hist[...], weights[...])
+    q_ref[...] = out[:, :cols].astype(BF16)
+    kv = out[:, cols:].T.astype(BF16)
+    own_ref[: 2 * cols, :] = kv
+    edge_ref[: 2 * cols, :] = kv[:, rows - WIN :]
+
+
+def front(history, w_query, w_key, w_value, pad_mask, w_out):
     rows, width = history.shape
-    negs = neg_ids.shape[0]
     half = w_out.shape[0] // 2
     cols = w_query.shape[1]
     tall = 2 * cols + FLAG_ROWS
-    if share % LANES:
-        pos_emb = lax.dynamic_slice_in_dim(pos_emb, lax.axis_index("head") * share, share, 1)
-    by_lanes = lambda a: a.reshape(-1, LANES)
     return pl.pallas_call(
         front_body,
         name="front",
@@ -148,34 +128,73 @@
             jax.ShapeDtypeStruct((rows, cols), BF16),
             jax.ShapeDtypeStruct((tall, rows), BF16),
             jax.ShapeDtypeStruct((tall, WIN), BF16),
+            jax.ShapeDtypeStruct((half, width), BF16),
+        ),
+        in_specs=[RAW] * 6,
+        out_specs=(WHOLE,) * 4,
+        scratch_shapes=[
+            pltpu.VMEM((rows, width), BF16),
+            pltpu.VMEM((3 * cols, width), BF16),
+            pltpu.VMEM((rows // LANES, LANES), jnp.int32),
+            pltpu.SemaphoreType.DMA((5 + rows // LANES,)),
+        ],
+        compiler_params=pltpu.CompilerParams(vmem_limit_bytes=12 * MIB),
+        cost_estimate=pl.CostEstimate(flops=AHEAD, bytes_accessed=4 * rows * width, transcendentals=0),
+    )(*stay(history, w_query.T, w_key.T, w_value.T, pad_mask.reshape(-1, LANES), w_out))
+
+
+def prepare_body(pos_hbm, gain_hbm, ids_hbm, target_hbm, id_ref, pos_out, gain_out, target_out, gain_row, pos, ids_ref, target_ref, sems):
+    rows, share = pos.shape
+    here = pl.ds(0, share)
+    if pos_hbm.shape[1] != share:
+        here = pl.ds(pl.multiple_of(lax.axis_index("head") * share, share), share)
+    moves = ((ids_hbm, ids_ref), (target_hbm, target_ref), (gain_hbm, gain_row), (pos_hbm.at[:, here], pos))
+    copies = [pltpu.make_async_copy(a, b, sems.at[n]) for n, (a, b) in enumerate(moves)]
+    for copy in copies:
+        copy.start()
+    copies[0].wait()
+    copies[1].wait()
+    target_out[...] = jnp.concatenate([target_ref[n : n + 1, :] for n in range(rows // LANES)], 1)
+    for n in range(ids_ref.shape[0]):
+        line = jnp.broadcast_to(ids_ref[n : n + 1, :], (LANES, LANES))
+        id_ref[n * LANES : (n + 1) * LANES, :] = line.T
+    copies[2].wait()
+    copies[3].wait()
+    gain = gain_row[:, here]
+    gain_out[...] = gain
+    pos_out[...] = (pos[...].astype(F32) * gain).T
+
+
+def prepare(pos_emb, norm_gain, neg_ids, target_ids, share):
+    rows, width = pos_emb.shape
+    negs = neg_ids.shape[0]
+    if share % LANES:
+        pos_emb = lax.dynamic_slice_in_dim(pos_emb, lax.axis_index("head") * share, share, 1)
+    return pl.pallas_call(
+        prepare_body,
+        name="prepare",
+        out_shape=(
             jax.ShapeDtypeStruct((negs, LANES), jnp.int32),
             jax.ShapeDtypeStruct((share, rows), F32),
             jax.ShapeDtypeStruct((1, share), F32),
             jax.ShapeDtypeStruct((1, rows), jnp.int32),
             jax.ShapeDtypeStruct((1, width), F32),
-            jax.ShapeDtypeStruct((half, width), BF16),
         ),
-        in_specs=[RAW] * 10,
-        out_specs=(WHOLE,) * 9,
+        in_specs=[RAW] * 4,
+        out_specs=(WHOLE,) * 5,
         scratch_shapes=[
-            pltpu.VMEM((rows, width), BF16),
-            pltpu.VMEM((3 * cols, width), BF16),
             pltpu.VMEM((rows, share), BF16),
-            pltpu.VMEM((rows // LANES, LANES), jnp.int32),
             pltpu.VMEM((negs // LANES, LANES), jnp.int32),
             pltpu.VMEM((rows // LANES, LANES), jnp.int32),
-            pltpu.SemaphoreType.DMA((9 + rows // LANES,)),
+            pltpu.SemaphoreType.DMA((4,)),
         ],
-        compiler_params=pltpu.CompilerParams(vmem_limit_bytes=12 * MIB),
-        cost_estimate=pl.CostEstimate(flops=AHEAD, bytes_accessed=4 * rows * width, transcendentals=0),
-    )(
-        *stay(history, w_query.T, w_key.T, w_value.T, by_lanes(pad_mask)),
-        *stay(pos_emb, norm_gain[None, :], by_lanes(neg_ids), by_lanes(target_ids), w_out),
-    )
-
-
-def attend_body(q_ref, own_ref, prev_ref, out_ref):
-    rows, cols = q_ref.shape
+        compiler_params=pltpu.CompilerParams(vmem_limit_bytes=8 * MIB),
+        cost_estimate=pl.CostEstimate(flops=rows * share, bytes_accessed=2 * rows * share, transcendentals=0),
+    )(*stay(pos_emb, norm_gain[None, :], neg_ids.reshape(-1, LANES), target_ids.reshape(-1, LANES)))
+
+
+def attend_blocks(starts, q_ref, own_ref, prev_ref, out_ref):
+    cols = q_ref.shape[1]
     step = LANES
     span = WIN + step
     at_row = lax.broadcasted_iota(jnp.int32, (step, span), 0)
@@ -192,7 +211,7 @@
             parts.append(own_ref[lo:hi, max(first - WIN, 0) : last - WIN])
         return parts[0] if len(parts) == 1 else jnp.concatenate(parts, 1)
 
-    for start in range(0, rows, step):
+    for start in starts:
         flags = window(2 * cols, 2 * cols + FLAG_ROWS, start).astype(F32)[:1]
         allowed = near & ((flags == 1.0) | self_pos)
         for head in range(cols // HD):
@@ -203,20 +222,30 @@
             weights = jnp.where(allowed, jnp.exp(scores - top), 0.0)
             prob = (weights / jnp.sum(weights, 1, keepdims=True)).astype(BF16)
             value = window(cols + lo, cols + lo + HD, start)
-            out_ref[lo : lo + HD, start : start + step] = dot_last(value, prob).astype(BF16)
-
-
-def attend(query, own, prev):
-    rows, cols = query.shape
-    return pl.pallas_call(
-        attend_body,
-        name="attend",
-        out_shape=jax.ShapeDtypeStruct((cols, rows), BF16),
-        in_specs=[WHOLE] * 3,
+            at = start - starts[0]
+            out_ref[lo : lo + HD, at : at + step] = dot_last(value, prob).astype(BF16)
+
+
+def attend_late_body(q_ref, own_ref, out_ref):
+    rows = q_ref.shape[0]
+    attend_blocks(range(WIN, rows, LANES), q_ref, own_ref, None, out_ref)
+
+
+def attend_early_body(q_ref, own_ref, prev_ref, late_ref, out_ref):
+    out_ref[:, WIN:] = late_ref[...]
+    attend_blocks(range(0, WIN, LANES), q_ref, own_ref, prev_ref, out_ref)
+
+
+def attend(body, width, *arrays):
+    rows, cols = arrays[0].shape
+    return pl.pallas_call(
+        body,
+        out_shape=jax.ShapeDtypeStruct((cols, width), BF16),
+        in_specs=[WHOLE] * len(arrays),
         out_specs=WHOLE,
         compiler_params=pltpu.CompilerParams(vmem_limit_bytes=8 * MIB),
-        cost_estimate=pl.CostEstimate(flops=AHEAD, bytes_accessed=6 * rows * cols, transcendentals=rows * 2 * WIN),
-    )(query, own, prev)
+        cost_estimate=pl.CostEstimate(flops=AHEAD, bytes_accessed=6 * rows * cols, transcendentals=rows * WIN),
+    )(*arrays)
 
 
 def premix_body(count, split, neg_ref, gain_ref, own_ref, *refs):
@@ -354,13 +383,13 @@
 ):
     width = history.shape[1]
     count = lax.axis_size("head")
-    query, own, edge, id_cols, pos_turned, gain_here, target, gain_row, half = front(
-        history, w_query, w_key, w_value, pad_mask, pos_emb, norm_gain, neg_ids, target_ids, w_out, width // count
-    )
+    query, own, edge, half = front(history, w_query, w_key, w_value, pad_mask, w_out)
     prev = from_behind(edge, "seq", 1)
     far = fetch_in_pairs(w_out, half)
-    mine = attend(query, own, prev)
+    late = attend(attend_late_body, history.shape[0] - WIN, query, own)
+    mine = attend(attend_early_body, history.shape[0], query, own, prev, late)
     heads = from_all(mine, "head")
+    id_cols, pos_turned, gain_here, target, gain_row = prepare(pos_emb, norm_gain, neg_ids, target_ids, width // count)
     near = swap_in_pairs(far, count)
     mix, turned = premix(neg_emb, gain_row, w_out, far, near)
     stats, user = score(heads, mix, turned, id_cols, pos_turned, target)

time: 33.6 us -> 31 us (0.923)
  waiting for transfers between devices: 8.3 us -> 3.95 us
  starting transfers between devices: 16.4 us -> 17.3 us
  Pallas kernels: 7.3 us -> 8.18 us
    ppermute x2, waiting for transfers between devices: 5.46 us -> 0.95 us  [fetch_in_pairs(): far.append(lax.ppermute(half if last else shard, ('seq', 'head'), route))]
    pallas_call x1 -> x3, Pallas kernels: 1.18 us -> 2.53 us  [the longest x2 1.29 us: attend(): pl.pallas_call(body, out_shape=jax.ShapeDtypeStruct((cols, width), BF16),...]
    ppermute x1, starting transfers between devices: 2.48 us -> 1.28 us  [from_behind(): return lax.ppermute(shard, axis, pairs)]
    ppermute x2, starting transfers between devices: 4.53 us -> 5.67 us  [fetch_in_pairs(): far.append(lax.ppermute(half if last else shard, ('seq', 'head'), route))]
    ppermute x2, starting transfers between devices: 0.51 us -> 1.43 us  [swap_in_pairs(): near.append(lax.ppermute(piece, 'seq', [(s, s ^ 1) for s in range(slabs)]))]
    pallas_call x1, Pallas kernels: 2.38 us -> 1.91 us  [front(): pl.pallas_call(front_body, name='front', out_shape=(jax.ShapeDtypeStruct(...]
  transfers between devices with their start and end apart: 11 -> 11, of which waited for: 5 -> 6; matrix products, arithmetic and copies ran while one was open for 0% -> 0% of each run, Pallas kernels for 17% -> 21%
where the time goes in v5:
time: 31 us; the launch traced here: 30.8 us
  starting transfers between devices  17.3 us (56%)
  Pallas kernels  8.18 us (26%)
  waiting for transfers between devices  3.95 us (13%)
  between operations  0.72 us (2%)
  other arithmetic  0.66 us (2%)
    ppermute x6, starting transfers between devices, from_all(): pieces.append(lax.ppermute(shard, axis, pairs))  8.91 us
    ppermute x2, starting transfers between devices, fetch_in_pairs(): far.append(lax.ppermute(half if last else shard, ('seq', 'head'), route))  5.67 us
    ppermute x6, waiting for transfers between devices, from_all(): pieces.append(lax.ppermute(shard, axis, pairs))  2.99 us
    pallas_call x1, Pallas kernels, front(): pl.pallas_call(front_body, name='front', out_shape=(jax.ShapeDtypeStruct(...  1.91 us
    pallas_call x1, Pallas kernels, score(): pl.pallas_call(functools.partial(score_body, count), name='score', out_sh...  1.57 us
    ppermute x2, starting transfers between devices, swap_in_pairs(): near.append(lax.ppermute(piece, 'seq', [(s, s ^ 1) for s in range(slabs)]))  1.43 us
    pallas_call x1, Pallas kernels, premix(): pl.pallas_call(functools.partial(premix_body, count, (len(far), len(near)...  1.33 us
    pallas_call x2, Pallas kernels, attend(): pl.pallas_call(body, out_shape=jax.ShapeDtypeStruct((cols, width), BF16),...  1.29 us
  transfers between devices with their start and end apart: 11, of which 6 were waited for; matrix products, arithmetic and copies ran while one was open for 0% of the time, Pallas kernels for 21%

profile of v5, /device:TPU:0, one launch (start us, length us, event | category | flops | bytes accessed | tf_op | source)
XLA Modules:
  0.0 30.8 jit_solution(12948846404129810994)
XLA Ops:
  0.6 3.1 %collective-permute-start.4 = (bf16[64,1024]{1,0:T(8,128)(2,1)}, bf16[64,1024]{1,0:T(8,128)(2,1)S(1)}, u32[]{:S(2)}, u32[]{:S(2)}) collective-permute-start(bf16[64,1024]{1,0:T(8,128)(2,1)} %own_ref.1), channel_id=1, source_target_pairs={{0,1},{1,0},{2,3},{3,2},{4,6},{5,7},{6,4},{7,5},{8,9},{9,8},{10,11... | collective-permute-start | bytes 393224 | tf_op jit(solution)/shard_map/ppermute | solution.py:72
  3.7 1.9 %front.1 = (bf16[384,64]{1,0:T(8,128)(2,1)S(1)}, bf16[144,384]{1,0:T(8,128)(2,1)S(1)}, bf16[144,256]{1,0:T(8,128)(2,1)S(1)}, bf16[32,1024]{1,0:T(8,128)(2,1)S(1)}) custom-call(bf16[384,1024]{1,0:T(8,128)(2,1)} %refs_0_.1, bf16[64,1024]{1,0:T(8,128)(2,1)} %bitcast.10, bf16[64,1024]{1,0:T(8,128)(2,1)} %bitcast.11, bf16[64,1024]{1,0:T(8,128)(2,1)} %bitcast.12, ...), custom_call_target="tpu_custom_call" | custom-call | flops 4000000000 | bytes 1572864 | tf_op jit(solution)/shard_map/front/pallas_call | solution.py:124
  5.7 2.5 %collective-permute-start.5 = (bf16[32,1024]{1,0:T(8,128)(2,1)S(1)}, bf16[32,1024]{1,0:T(8,128)(2,1)S(1)}, u32[]{:S(2)}, u32[]{:S(2)}) collective-permute-start(bf16[32,1024]{1,0:T(8,128)(2,1)S(1)} %get-tuple-element.19), channel_id=1, source_target_pairs={{0,3},{1,2},{2,1},{3,0},{4,7},{5,6},{6,5},{7,4},{8,11},{9,10},{10,... | collective-permute-start | bytes 196616 | tf_op jit(solution)/shard_map/ppermute | solution.py:72
  8.2 1.3 %collective-permute-start = (bf16[144,256]{1,0:T(8,128)(2,1)S(1)}, bf16[144,256]{1,0:T(8,128)(2,1)S(1)}, u32[]{:S(2)}, u32[]{:S(2)}) collective-permute-start(bf16[144,256]{1,0:T(8,128)(2,1)S(1)} %get-tuple-element.17), channel_id=1, source_target_pairs={{0,4},{4,8},{8,12},{12,16},{16,20},{20,24},{24,28},{1,5},{5,9},{9,... | collective-permute-start | bytes 221192 | tf_op jit(solution)/shard_map/ppermute | solution.py:39
  9.5 0.5 %shard_map.122.late_ref = bf16[64,128]{1,0:T(8,128)(2,1)S(1)} custom-call(bf16[384,64]{1,0:T(8,128)(2,1)S(1)} %get-tuple-element.15.q_ref, bf16[144,384]{1,0:T(8,128)(2,1)S(1)} %get-tuple-element.16.own_ref), custom_call_target="tpu_custom_call" | custom-call | flops 4000000000 | bytes 147456 | tf_op jit(solution)/shard_map/pallas_call | solution.py:241
  10.0 1.2 %prepare.1 = (s32[2048,128]{1,0:T(8,128)S(1)}, f32[256,384]{1,0:T(8,128)S(1)}, f32[1,256]{1,0:T(1,128)S(1)}, s32[1,384]{1,0:T(1,128)S(1)}, f32[1,1024]{1,0:T(1,128)S(1)}) custom-call(bf16[384,1024]{1,0:T(8,128)(2,1)} %pos_hbm.1, f32[1,1024]{1,0:T(1,128)} %bitcast.8, s32[16,128]{1,0:T(8,128)} %bitcast.7, s32[3,128]{1,0:T(4,128)} %bitcast.9), custom_call_target="tpu_custom_call" | custom-call | flops 98304 | bytes 196608 | tf_op jit(solution)/shard_map/prepare/pallas_call | solution.py:173
  11.2 0.0 copy-start
  11.2 0.0 copy-start.1
  11.3 0.9 %collective-permute-done.5.refs_1_ = bf16[32,1024]{1,0:T(8,128)(2,1)S(1)} collective-permute-done((bf16[32,1024]{1,0:T(8,128)(2,1)S(1)}, bf16[32,1024]{1,0:T(8,128)(2,1)S(1)}, u32[]{:S(2)}, u32[]{:S(2)}) %collective-permute-start.5) | collective-permute-done | bytes 65568 | tf_op jit(solution)/shard_map/ppermute | solution.py:72
  12.2 1.3 %collective-permute-start.7 = (bf16[32,1024]{1,0:T(8,128)(2,1)S(1)}, bf16[32,1024]{1,0:T(8,128)(2,1)S(1)}, u32[]{:S(2)}, u32[]{:S(2)}) collective-permute-start(bf16[32,1024]{1,0:T(8,128)(2,1)S(1)} %collective-permute-done.5.refs_1_), channel_id=1, source_target_pairs={{0,4},{4,0},{8,12},{12,8},{16,20},{20,16},{24,28},{28,24},{1,5},{5... | collective-permute-start | bytes 196616 | tf_op jit(solution)/shard_map/ppermute | solution.py:82
  13.5 0.0 collective-permute-done.4.refs_0_
  13.6 0.1 collective-permute-start.6
  13.6 0.0 collective-permute-done.prev_ref
  13.6 0.8 %shard_map.123.refs_0_ = bf16[64,384]{1,0:T(8,128)(2,1)S(1)} custom-call(bf16[384,64]{1,0:T(8,128)(2,1)S(1)} %get-tuple-element.15.q_ref, bf16[144,384]{1,0:T(8,128)(2,1)S(1)} %get-tuple-element.16.own_ref, bf16[144,256]{1,0:T(8,128)(2,1)S(1)} %collective-permute-done.prev_ref, bf16[64,128]{1,0:T(8,128)(2,1)S(1)} %shard_map.122.late_ref), custom_call_target="tpu_custom_call" | custom-call | flops 4000000000 | bytes 147456 | tf_op jit(solution)/shard_map/pallas_call | solution.py:241
  14.5 1.4 %collective-permute-start.3 = (bf16[64,384]{1,0:T(8,128)(2,1)S(1)}, bf16[64,384]{1,0:T(8,128)(2,1)S(1)}, u32[]{:S(2)}, u32[]{:S(2)}) collective-permute-start(bf16[64,384]{1,0:T(8,128)(2,1)S(1)} %shard_map.123.refs_0_), channel_id=1, source_target_pairs={{0,3},{1,2},{2,1},{3,0},{4,7},{5,6},{6,5},{7,4},{8,11},{9,10},{10,... | collective-permute-start | bytes 147464 | tf_op jit(solution)/shard_map/ppermute | solution.py:52
  15.9 0.8 %collective-permute-start.2 = (bf16[64,384]{1,0:T(8,128)(2,1)S(1)}, bf16[64,384]{1,0:T(8,128)(2,1)S(1)}, u32[]{:S(2)}, u32[]{:S(2)}) collective-permute-start(bf16[64,384]{1,0:T(8,128)(2,1)S(1)} %shard_map.123.refs_0_), channel_id=1, source_target_pairs={{0,2},{1,3},{2,0},{3,1},{4,6},{5,7},{6,4},{7,5},{8,10},{9,11},{10,... | collective-permute-start | bytes 147464 | tf_op jit(solution)/shard_map/ppermute | solution.py:52
  16.7 2.2 %collective-permute-start.1 = (bf16[64,384]{1,0:T(8,128)(2,1)S(1)}, bf16[64,384]{1,0:T(8,128)(2,1)S(1)}, u32[]{:S(2)}, u32[]{:S(2)}) collective-permute-start(bf16[64,384]{1,0:T(8,128)(2,1)S(1)} %shard_map.123.refs_0_), channel_id=1, source_target_pairs={{0,1},{1,0},{2,3},{3,2},{4,5},{5,4},{6,7},{7,6},{8,9},{9,8},{10,11... | collective-permute-start | bytes 147464 | tf_op jit(solution)/shard_map/ppermute | solution.py:52
  18.9 0.0 collective-permute-done.7.refs_3_
  18.9 0.0 collective-permute-done.6.refs_2_
  18.9 0.0 copy-done
  18.9 0.0 copy-done.1
  18.9 1.3 %premix.1 = (bf16[2048,256]{1,0:T(8,128)(2,1)S(1)}, bf16[1024,256]{1,0:T(8,128)(2,1)S(1)}) custom-call(bf16[2048,1024]{1,0:T(8,128)(2,1)S(1)} %copy-done, f32[1,1024]{1,0:T(1,128)S(1)} %get-tuple-element.18.gain_ref, bf16[64,1024]{1,0:T(8,128)(2,1)S(1)} %copy-done.1, bf16[64,1024]{1,0:T(8,128)(2,1)S(1)} %collective-permute-done.4.refs_0_, ...), custom_call_target="tpu_custom_call" | custom-call | flops 1073741824 | bytes 4194304 | tf_op jit(solution)/shard_map/premix/pallas_call | solution.py:283
  20.3 0.8 %collective-permute-done.3.refs_3_ = bf16[64,384]{1,0:T(8,128)(2,1)S(1)} collective-permute-done((bf16[64,384]{1,0:T(8,128)(2,1)S(1)}, bf16[64,384]{1,0:T(8,128)(2,1)S(1)}, u32[]{:S(2)}, u32[]{:S(2)}) %collective-permute-start.3) | collective-permute-done | bytes 49184 | tf_op jit(solution)/shard_map/ppermute | solution.py:52
  21.0 1.5 %collective-permute-done.2.refs_2_ = bf16[64,384]{1,0:T(8,128)(2,1)S(1)} collective-permute-done((bf16[64,384]{1,0:T(8,128)(2,1)S(1)}, bf16[64,384]{1,0:T(8,128)(2,1)S(1)}, u32[]{:S(2)}, u32[]{:S(2)}) %collective-permute-start.2) | collective-permute-done | bytes 49184 | tf_op jit(solution)/shard_map/ppermute | solution.py:52
  22.5 0.0 collective-permute-done.1.refs_1_
  22.5 1.6 %score.1 = (f32[4,384]{1,0:T(4,128)S(1)}, f32[256,384]{1,0:T(8,128)S(1)}) custom-call(bf16[64,384]{1,0:T(8,128)(2,1)S(1)} %shard_map.123.refs_0_, bf16[64,384]{1,0:T(8,128)(2,1)S(1)} %collective-permute-done.1.refs_1_, bf16[64,384]{1,0:T(8,128)(2,1)S(1)} %collective-permute-done.2.refs_2_, bf16[64,384]{1,0:T(8,128)(2,1)S(1)} %collective-permute-done.3.refs_3_, ...), custom_call_target="tpu_custom_call" | custom-call | flops 603979776 | bytes 1048576 | tf_op jit(solution)/shard_map/score/pallas_call | solution.py:339
  24.1 1.4 %collective-permute-start.10 = (f32[4,384]{1,0:T(4,128)S(1)}, f32[4,384]{1,0:T(4,128)S(1)}, u32[]{:S(2)}, u32[]{:S(2)}) collective-permute-start(f32[4,384]{1,0:T(4,128)S(1)} %get-tuple-element.27), channel_id=1, source_target_pairs={{0,3},{1,2},{2,1},{3,0},{4,7},{5,6},{6,5},{7,4},{8,11},{9,10},{10,... | collective-permute-start | bytes 18440 | tf_op jit(solution)/shard_map/ppermute | solution.py:52
  25.5 0.6 %collective-permute-start.9 = (f32[4,384]{1,0:T(4,128)S(1)}, f32[4,384]{1,0:T(4,128)S(1)}, u32[]{:S(2)}, u32[]{:S(2)}) collective-permute-start(f32[4,384]{1,0:T(4,128)S(1)} %get-tuple-element.27), channel_id=1, source_target_pairs={{0,2},{1,3},{2,0},{3,1},{4,6},{5,7},{6,4},{7,5},{8,10},{9,11},{10,... | collective-permute-start | bytes 18440 | tf_op jit(solution)/shard_map/ppermute | solution.py:52
  26.1 2.4 %collective-permute-start.8 = (f32[4,384]{1,0:T(4,128)S(1)}, f32[4,384]{1,0:T(4,128)S(1)}, u32[]{:S(2)}, u32[]{:S(2)}) collective-permute-start(f32[4,384]{1,0:T(4,128)S(1)} %get-tuple-element.27), channel_id=1, source_target_pairs={{0,1},{1,0},{2,3},{3,2},{4,5},{5,4},{6,7},{7,6},{8,9},{9,8},{10,11... | collective-permute-start | bytes 18440 | tf_op jit(solution)/shard_map/ppermute | solution.py:52
  28.5 0.8 %finish.1 = bf16[384,256]{1,0:T(8,128)(2,1)} custom-call(f32[256,384]{1,0:T(8,128)S(1)} %get-tuple-element.25.user_ref, f32[1,256]{1,0:T(1,128)S(1)} %get-tuple-element.26.gain_ref), custom_call_target="tpu_custom_call" | custom-call | flops 196608 | bytes 589824 | tf_op jit(solution)/shard_map/finish/pallas_call | solution.py:360
  29.4 0.2 collective-permute-done.10
  29.6 0.4 %collective-permute-done.9 = f32[4,384]{1,0:T(4,128)S(1)} collective-permute-done((f32[4,384]{1,0:T(4,128)S(1)}, f32[4,384]{1,0:T(4,128)S(1)}, u32[]{:S(2)}, u32[]{:S(2)}) %collective-permute-start.9) | collective-permute-done | bytes 6176 | tf_op jit(solution)/shard_map/ppermute | solution.py:52
  30.0 0.1 collective-permute-done.8
  30.1 0.1 slice_reduce_fusion.7
  30.2 0.6 %add_subtract_fusion = f32[384]{0:T(512)} fusion(f32[384]{0:T(512)S(1)} %get-tuple-element.30, f32[384]{0:T(512)S(1)} %get-tuple-element.36, f32[384]{0:T(512)S(1)} %get-tuple-element.35, f32[384]{0:T(512)S(1)} %get-tuple-element.34, f32[384]{0:T(512)S(1)} %get-tuple-element.33, f32[384]{0:T(512)S(1)} %get-tuple-element.32, f32[384]{0:T(512)S(1)} %get-tuple-element.31, ...), kind=kLoop, calls=%fused_computation | loop fusion | flops 7296 | bytes 15360 | tf_op jit(solution)/shard_map/sub | solution.py:401
Async XLA Ops:
  0.6 12.9 %collective-permute-start.4 = (bf16[64,1024]{1,0:T(8,128)(2,1)}, bf16[64,1024]{1,0:T(8,128)(2,1)S(1)}, u32[]{:S(2)}, u32[]{:S(2)}) collective-permute-start(bf16[64,1024]{1,0:T(8,128)(2,1)} %own_ref.1), channel_id=1, source_target_pairs={{0,1},{1,0},{2,3},{3,2},{4,6},{5,7},{6,4},{7,5},{8,9},{9,8},{10,11... | collective-permute-start | bytes 393224 | tf_op jit(solution)/shard_map/ppermute | solution.py:72
  5.7 6.5 %collective-permute-start.5 = (bf16[32,1024]{1,0:T(8,128)(2,1)S(1)}, bf16[32,1024]{1,0:T(8,128)(2,1)S(1)}, u32[]{:S(2)}, u32[]{:S(2)}) collective-permute-start(bf16[32,1024]{1,0:T(8,128)(2,1)S(1)} %get-tuple-element.19), channel_id=1, source_target_pairs={{0,3},{1,2},{2,1},{3,0},{4,7},{5,6},{6,5},{7,4},{8,11},{9,10},{10,... | collective-permute-start | bytes 196616 | tf_op jit(solution)/shard_map/ppermute | solution.py:72
  8.2 5.4 %collective-permute-start = (bf16[144,256]{1,0:T(8,128)(2,1)S(1)}, bf16[144,256]{1,0:T(8,128)(2,1)S(1)}, u32[]{:S(2)}, u32[]{:S(2)}) collective-permute-start(bf16[144,256]{1,0:T(8,128)(2,1)S(1)} %get-tuple-element.17), channel_id=1, source_target_pairs={{0,4},{4,8},{8,12},{12,16},{16,20},{20,24},{24,28},{1,5},{5,9},{9,... | collective-permute-start | bytes 221192 | tf_op jit(solution)/shard_map/ppermute | solution.py:39
  11.2 7.7 %copy-start = (bf16[2048,1024]{1,0:T(8,128)(2,1)S(1)}, bf16[2048,1024]{1,0:T(8,128)(2,1)}, u32[]{:S(2)}) copy-start(bf16[2048,1024]{1,0:T(8,128)(2,1)} %neg_ref.1) | copy-start | bytes 12582916
  11.2 7.7 %copy-start.1 = (bf16[64,1024]{1,0:T(8,128)(2,1)S(1)}, bf16[64,1024]{1,0:T(8,128)(2,1)}, u32[]{:S(2)}) copy-start(bf16[64,1024]{1,0:T(8,128)(2,1)} %own_ref.1) | copy-start | bytes 393220
  12.2 6.7 %collective-permute-start.7 = (bf16[32,1024]{1,0:T(8,128)(2,1)S(1)}, bf16[32,1024]{1,0:T(8,128)(2,1)S(1)}, u32[]{:S(2)}, u32[]{:S(2)}) collective-permute-start(bf16[32,1024]{1,0:T(8,128)(2,1)S(1)} %collective-permute-done.5.refs_1_), channel_id=1, source_target_pairs={{0,4},{4,0},{8,12},{12,8},{16,20},{20,16},{24,28},{28,24},{1,5},{5... | collective-permute-start | bytes 196616 | tf_op jit(solution)/shard_map/ppermute | solution.py:82
  13.6 5.4 %collective-permute-start.6 = (bf16[64,1024]{1,0:T(8,128)(2,1)S(1)}, bf16[64,1024]{1,0:T(8,128)(2,1)S(1)}, u32[]{:S(2)}, u32[]{:S(2)}) collective-permute-start(bf16[64,1024]{1,0:T(8,128)(2,1)S(1)} %collective-permute-done.4.refs_0_), channel_id=1, source_target_pairs={{0,4},{4,0},{8,12},{12,8},{16,20},{20,16},{24,28},{28,24},{1,5},{5... | collective-permute-start | bytes 393224 | tf_op jit(solution)/shard_map/ppermute | solution.py:82
  14.5 6.6 %collective-permute-start.3 = (bf16[64,384]{1,0:T(8,128)(2,1)S(1)}, bf16[64,384]{1,0:T(8,128)(2,1)S(1)}, u32[]{:S(2)}, u32[]{:S(2)}) collective-permute-start(bf16[64,384]{1,0:T(8,128)(2,1)S(1)} %shard_map.123.refs_0_), channel_id=1, source_target_pairs={{0,3},{1,2},{2,1},{3,0},{4,7},{5,6},{6,5},{7,4},{8,11},{9,10},{10,... | collective-permute-start | bytes 147464 | tf_op jit(solution)/shard_map/ppermute | solution.py:52
  15.9 6.6 %collective-permute-start.2 = (bf16[64,384]{1,0:T(8,128)(2,1)S(1)}, bf16[64,384]{1,0:T(8,128)(2,1)S(1)}, u32[]{:S(2)}, u32[]{:S(2)}) collective-permute-start(bf16[64,384]{1,0:T(8,128)(2,1)S(1)} %shard_map.123.refs_0_), channel_id=1, source_target_pairs={{0,2},{1,3},{2,0},{3,1},{4,6},{5,7},{6,4},{7,5},{8,10},{9,11},{10,... | collective-permute-start | bytes 147464 | tf_op jit(solution)/shard_map/ppermute | solution.py:52
  16.7 5.8 %collective-permute-start.1 = (bf16[64,384]{1,0:T(8,128)(2,1)S(1)}, bf16[64,384]{1,0:T(8,128)(2,1)S(1)}, u32[]{:S(2)}, u32[]{:S(2)}) collective-permute-start(bf16[64,384]{1,0:T(8,128)(2,1)S(1)} %shard_map.123.refs_0_), channel_id=1, source_target_pairs={{0,1},{1,0},{2,3},{3,2},{4,5},{5,4},{6,7},{7,6},{8,9},{9,8},{10,11... | collective-permute-start | bytes 147464 | tf_op jit(solution)/shard_map/ppermute | solution.py:52
  24.1 5.5 %collective-permute-start.10 = (f32[4,384]{1,0:T(4,128)S(1)}, f32[4,384]{1,0:T(4,128)S(1)}, u32[]{:S(2)}, u32[]{:S(2)}) collective-permute-start(f32[4,384]{1,0:T(4,128)S(1)} %get-tuple-element.27), channel_id=1, source_target_pairs={{0,3},{1,2},{2,1},{3,0},{4,7},{5,6},{6,5},{7,4},{8,11},{9,10},{10,... | collective-permute-start | bytes 18440 | tf_op jit(solution)/shard_map/ppermute | solution.py:52
  25.5 4.5 %collective-permute-start.9 = (f32[4,384]{1,0:T(4,128)S(1)}, f32[4,384]{1,0:T(4,128)S(1)}, u32[]{:S(2)}, u32[]{:S(2)}) collective-permute-start(f32[4,384]{1,0:T(4,128)S(1)} %get-tuple-element.27), channel_id=1, source_target_pairs={{0,2},{1,3},{2,0},{3,1},{4,6},{5,7},{6,4},{7,5},{8,10},{9,11},{10,... | collective-permute-start | bytes 18440 | tf_op jit(solution)/shard_map/ppermute | solution.py:52
  26.1 4.0 %collective-permute-start.8 = (f32[4,384]{1,0:T(4,128)S(1)}, f32[4,384]{1,0:T(4,128)S(1)}, u32[]{:S(2)}, u32[]{:S(2)}) collective-permute-start(f32[4,384]{1,0:T(4,128)S(1)} %get-tuple-element.27), channel_id=1, source_target_pairs={{0,1},{1,0},{2,3},{3,2},{4,5},{5,4},{6,7},{7,6},{8,9},{9,8},{10,11... | collective-permute-start | bytes 18440 | tf_op jit(solution)/shard_map/ppermute | solution.py:52

commit v6 on v5

--- a/solution.py
+++ b/solution.py
@@ -33,10 +33,9 @@
     return lax.dot_general(a, b, (((1,), (0,)), ((), ())), preferred_element_type=F32)
 
 
-def from_behind(shard, axis, by):
+def from_behind(shard, axis):
     count = lax.axis_size(axis)
-    pairs = [(i, i + by) for i in range(count) if 0 <= i + by < count]
-    return lax.ppermute(shard, axis, pairs)
+    return lax.ppermute(shard, axis, [(i, (i + 1) % count) for i in range(count)])
 
 
 def partners(axis):
@@ -201,6 +200,7 @@
     at_col = lax.broadcasted_iota(jnp.int32, (step, span), 1)
     near = (at_col > at_row) & (at_col <= at_row + WIN)
     self_pos = at_col == at_row + WIN
+    inside = lax.axis_index("seq") > 0
 
     def window(lo, hi, first):
         parts = []
@@ -214,6 +214,8 @@
     for start in starts:
         flags = window(2 * cols, 2 * cols + FLAG_ROWS, start).astype(F32)[:1]
         allowed = near & ((flags == 1.0) | self_pos)
+        if start < WIN:
+            allowed = allowed & ((at_col >= WIN - start) | inside)
         for head in range(cols // HD):
             lo = head * HD
             scores = dot_plain(q_ref[start : start + step, lo : lo + HD], window(lo, lo + HD, start)) * HD**-0.5
@@ -384,7 +386,7 @@
     width = history.shape[1]
     count = lax.axis_size("head")
     query, own, edge, half = front(history, w_query, w_key, w_value, pad_mask, w_out)
-    prev = from_behind(edge, "seq", 1)
+    prev = from_behind(edge, "seq")
     far = fetch_in_pairs(w_out, half)
     late = attend(attend_late_body, history.shape[0] - WIN, query, own)
     mine = attend(attend_early_body, history.shape[0], query, own, prev, late)

time: 31 us -> 30.6 us (0.987)
  starting transfers between devices: 17.3 us -> 15.1 us
  waiting for transfers between devices: 3.95 us -> 5.67 us
    ppermute x2, waiting for transfers between devices: 0.95 us -> 2.24 us  [fetch_in_pairs(): far.append(lax.ppermute(half if last else shard, ('seq', 'head'), route))]
    ppermute x1, starting transfers between devices: 1.28 us -> 0.01 us  [from_behind(): lax.ppermute(shard, axis, [(i, (i + 1) % count) for i in range(count)])]
    ppermute x2, starting transfers between devices: 1.43 us -> 0.51 us  [swap_in_pairs(): near.append(lax.ppermute(piece, 'seq', [(s, s ^ 1) for s in range(slabs)]))]
  transfers between devices with their start and end apart: 11 -> 11, of which waited for: 6 -> 6; matrix products, arithmetic and copies ran while one was open for 0% -> 0% of each run, Pallas kernels for 21% -> 22%
where the time goes in v6:
time: 30.6 us; the launch traced here: 30.3 us
  starting transfers between devices  15.1 us (49%)
  Pallas kernels  8.18 us (27%)
  waiting for transfers between devices  5.67 us (19%)
  between operations  0.71 us (2%)
  other arithmetic  0.66 us (2%)
    ppermute x6, starting transfers between devices, from_all(): pieces.append(lax.ppermute(shard, axis, pairs))  8.91 us
    ppermute x2, starting transfers between devices, fetch_in_pairs(): far.append(lax.ppermute(half if last else shard, ('seq', 'head'), route))  5.67 us
    ppermute x6, waiting for transfers between devices, from_all(): pieces.append(lax.ppermute(shard, axis, pairs))  3.25 us
    ppermute x2, waiting for transfers between devices, fetch_in_pairs(): far.append(lax.ppermute(half if last else shard, ('seq', 'head'), route))  2.24 us
    pallas_call x1, Pallas kernels, front(): pl.pallas_call(front_body, name='front', out_shape=(jax.ShapeDtypeStruct(...  1.91 us
    pallas_call x1, Pallas kernels, score(): pl.pallas_call(functools.partial(score_body, count), name='score', out_sh...  1.57 us
    pallas_call x1, Pallas kernels, premix(): pl.pallas_call(functools.partial(premix_body, count, (len(far), len(near)...  1.33 us
    pallas_call x2, Pallas kernels, attend(): pl.pallas_call(body, out_shape=jax.ShapeDtypeStruct((cols, width), BF16),...  1.29 us
  transfers between devices with their start and end apart: 11, of which 6 were waited for; matrix products, arithmetic and copies ran while one was open for 0% of the time, Pallas kernels for 22%

profile of v6, /device:TPU:0, one launch (start us, length us, event | category | flops | bytes accessed | tf_op | source)
XLA Modules:
  0.0 30.3 jit_solution(15824352387815854007)
XLA Ops:
  0.6 3.1 %collective-permute-start.4 = (bf16[64,1024]{1,0:T(8,128)(2,1)}, bf16[64,1024]{1,0:T(8,128)(2,1)S(1)}, u32[]{:S(2)}, u32[]{:S(2)}) collective-permute-start(bf16[64,1024]{1,0:T(8,128)(2,1)} %own_ref.1), channel_id=1, source_target_pairs={{0,1},{1,0},{2,3},{3,2},{4,6},{5,7},{6,4},{7,5},{8,9},{9,8},{10,11... | collective-permute-start | bytes 393224 | tf_op jit(solution)/shard_map/ppermute | solution.py:71
  3.7 1.9 %front.1 = (bf16[384,64]{1,0:T(8,128)(2,1)S(1)}, bf16[144,384]{1,0:T(8,128)(2,1)S(1)}, bf16[144,256]{1,0:T(8,128)(2,1)S(1)}, bf16[32,1024]{1,0:T(8,128)(2,1)S(1)}) custom-call(bf16[384,1024]{1,0:T(8,128)(2,1)} %refs_0_.1, bf16[64,1024]{1,0:T(8,128)(2,1)} %bitcast.10, bf16[64,1024]{1,0:T(8,128)(2,1)} %bitcast.11, bf16[64,1024]{1,0:T(8,128)(2,1)} %bitcast.12, ...), custom_call_target="tpu_custom_call" | custom-call | flops 4000000000 | bytes 1572864 | tf_op jit(solution)/shard_map/front/pallas_call | solution.py:123
  5.7 2.5 %collective-permute-start.5 = (bf16[32,1024]{1,0:T(8,128)(2,1)S(1)}, bf16[32,1024]{1,0:T(8,128)(2,1)S(1)}, u32[]{:S(2)}, u32[]{:S(2)}) collective-permute-start(bf16[32,1024]{1,0:T(8,128)(2,1)S(1)} %get-tuple-element.19), channel_id=1, source_target_pairs={{0,3},{1,2},{2,1},{3,0},{4,7},{5,6},{6,5},{7,4},{8,11},{9,10},{10,... | collective-permute-start | bytes 196616 | tf_op jit(solution)/shard_map/ppermute | solution.py:71
  8.2 0.0 collective-permute-start
  8.2 0.5 %shard_map.122.late_ref = bf16[64,128]{1,0:T(8,128)(2,1)S(1)} custom-call(bf16[384,64]{1,0:T(8,128)(2,1)S(1)} %get-tuple-element.15.q_ref, bf16[144,384]{1,0:T(8,128)(2,1)S(1)} %get-tuple-element.16.own_ref), custom_call_target="tpu_custom_call" | custom-call | flops 4000000000 | bytes 147456 | tf_op jit(solution)/shard_map/pallas_call | solution.py:243
  8.7 1.2 %prepare.1 = (s32[2048,128]{1,0:T(8,128)S(1)}, f32[256,384]{1,0:T(8,128)S(1)}, f32[1,256]{1,0:T(1,128)S(1)}, s32[1,384]{1,0:T(1,128)S(1)}, f32[1,1024]{1,0:T(1,128)S(1)}) custom-call(bf16[384,1024]{1,0:T(8,128)(2,1)} %pos_hbm.1, f32[1,1024]{1,0:T(1,128)} %bitcast.8, s32[16,128]{1,0:T(8,128)} %bitcast.7, s32[3,128]{1,0:T(4,128)} %bitcast.9), custom_call_target="tpu_custom_call" | custom-call | flops 98304 | bytes 196608 | tf_op jit(solution)/shard_map/prepare/pallas_call | solution.py:172
  9.9 0.0 copy-start
  10.0 0.0 copy-start.1
  10.0 2.2 %collective-permute-done.5.refs_1_ = bf16[32,1024]{1,0:T(8,128)(2,1)S(1)} collective-permute-done((bf16[32,1024]{1,0:T(8,128)(2,1)S(1)}, bf16[32,1024]{1,0:T(8,128)(2,1)S(1)}, u32[]{:S(2)}, u32[]{:S(2)}) %collective-permute-start.5) | collective-permute-done | bytes 65568 | tf_op jit(solution)/shard_map/ppermute | solution.py:71
  12.2 0.0 collective-permute-start.7
  12.2 0.0 collective-permute-done.4.refs_0_
  12.2 0.5 %collective-permute-start.6 = (bf16[64,1024]{1,0:T(8,128)(2,1)S(1)}, bf16[64,1024]{1,0:T(8,128)(2,1)S(1)}, u32[]{:S(2)}, u32[]{:S(2)}) collective-permute-start(bf16[64,1024]{1,0:T(8,128)(2,1)S(1)} %collective-permute-done.4.refs_0_), channel_id=1, source_target_pairs={{0,4},{4,0},{8,12},{12,8},{16,20},{20,16},{24,28},{28,24},{1,5},{5... | collective-permute-start | bytes 393224 | tf_op jit(solution)/shard_map/ppermute | solution.py:81
  12.7 0.2 collective-permute-done.prev_ref
  12.9 0.8 %shard_map.123.refs_0_ = bf16[64,384]{1,0:T(8,128)(2,1)S(1)} custom-call(bf16[384,64]{1,0:T(8,128)(2,1)S(1)} %get-tuple-element.15.q_ref, bf16[144,384]{1,0:T(8,128)(2,1)S(1)} %get-tuple-element.16.own_ref, bf16[144,256]{1,0:T(8,128)(2,1)S(1)} %collective-permute-done.prev_ref, bf16[64,128]{1,0:T(8,128)(2,1)S(1)} %shard_map.122.late_ref), custom_call_target="tpu_custom_call" | custom-call | flops 4000000000 | bytes 147456 | tf_op jit(solution)/shard_map/pallas_call | solution.py:243
  13.7 2.1 %collective-permute-start.3 = (bf16[64,384]{1,0:T(8,128)(2,1)S(1)}, bf16[64,384]{1,0:T(8,128)(2,1)S(1)}, u32[]{:S(2)}, u32[]{:S(2)}) collective-permute-start(bf16[64,384]{1,0:T(8,128)(2,1)S(1)} %shard_map.123.refs_0_), channel_id=1, source_target_pairs={{0,3},{1,2},{2,1},{3,0},{4,7},{5,6},{6,5},{7,4},{8,11},{9,10},{10,... | collective-permute-start | bytes 147464 | tf_op jit(solution)/shard_map/ppermute | solution.py:51
  15.8 0.3 collective-permute-start.2
  16.1 2.1 %collective-permute-start.1 = (bf16[64,384]{1,0:T(8,128)(2,1)S(1)}, bf16[64,384]{1,0:T(8,128)(2,1)S(1)}, u32[]{:S(2)}, u32[]{:S(2)}) collective-permute-start(bf16[64,384]{1,0:T(8,128)(2,1)S(1)} %shard_map.123.refs_0_), channel_id=1, source_target_pairs={{0,1},{1,0},{2,3},{3,2},{4,5},{5,4},{6,7},{7,6},{8,9},{9,8},{10,11... | collective-permute-start | bytes 147464 | tf_op jit(solution)/shard_map/ppermute | solution.py:51
  18.2 0.0 collective-permute-done.7.refs_3_
  18.2 0.0 collective-permute-done.6.refs_2_
  18.2 0.0 copy-done
  18.2 0.0 copy-done.1
  18.2 1.3 %premix.1 = (bf16[2048,256]{1,0:T(8,128)(2,1)S(1)}, bf16[1024,256]{1,0:T(8,128)(2,1)S(1)}) custom-call(bf16[2048,1024]{1,0:T(8,128)(2,1)S(1)} %copy-done, f32[1,1024]{1,0:T(1,128)S(1)} %get-tuple-element.18.gain_ref, bf16[64,1024]{1,0:T(8,128)(2,1)S(1)} %copy-done.1, bf16[64,1024]{1,0:T(8,128)(2,1)S(1)} %collective-permute-done.4.refs_0_, ...), custom_call_target="tpu_custom_call" | custom-call | flops 1073741824 | bytes 4194304 | tf_op jit(solution)/shard_map/premix/pallas_call | solution.py:285
  19.5 0.2 collective-permute-done.3.refs_3_
  19.7 1.6 %collective-permute-done.2.refs_2_ = bf16[64,384]{1,0:T(8,128)(2,1)S(1)} collective-permute-done((bf16[64,384]{1,0:T(8,128)(2,1)S(1)}, bf16[64,384]{1,0:T(8,128)(2,1)S(1)}, u32[]{:S(2)}, u32[]{:S(2)}) %collective-permute-start.2) | collective-permute-done | bytes 49184 | tf_op jit(solution)/shard_map/ppermute | solution.py:51
  21.3 0.0 collective-permute-done.1.refs_1_
  21.3 1.6 %score.1 = (f32[4,384]{1,0:T(4,128)S(1)}, f32[256,384]{1,0:T(8,128)S(1)}) custom-call(bf16[64,384]{1,0:T(8,128)(2,1)S(1)} %shard_map.123.refs_0_, bf16[64,384]{1,0:T(8,128)(2,1)S(1)} %collective-permute-done.1.refs_1_, bf16[64,384]{1,0:T(8,128)(2,1)S(1)} %collective-permute-done.2.refs_2_, bf16[64,384]{1,0:T(8,128)(2,1)S(1)} %collective-permute-done.3.refs_3_, ...), custom_call_target="tpu_custom_call" | custom-call | flops 603979776 | bytes 1048576 | tf_op jit(solution)/shard_map/score/pallas_call | solution.py:341
  22.9 2.2 %collective-permute-start.10 = (f32[4,384]{1,0:T(4,128)S(1)}, f32[4,384]{1,0:T(4,128)S(1)}, u32[]{:S(2)}, u32[]{:S(2)}) collective-permute-start(f32[4,384]{1,0:T(4,128)S(1)} %get-tuple-element.27), channel_id=1, source_target_pairs={{0,3},{1,2},{2,1},{3,0},{4,7},{5,6},{6,5},{7,4},{8,11},{9,10},{10,... | collective-permute-start | bytes 18440 | tf_op jit(solution)/shard_map/ppermute | solution.py:51
  25.1 0.2 collective-permute-start.9
  25.4 2.0 %collective-permute-start.8 = (f32[4,384]{1,0:T(4,128)S(1)}, f32[4,384]{1,0:T(4,128)S(1)}, u32[]{:S(2)}, u32[]{:S(2)}) collective-permute-start(f32[4,384]{1,0:T(4,128)S(1)} %get-tuple-element.27), channel_id=1, source_target_pairs={{0,1},{1,0},{2,3},{3,2},{4,5},{5,4},{6,7},{7,6},{8,9},{9,8},{10,11... | collective-permute-start | bytes 18440 | tf_op jit(solution)/shard_map/ppermute | solution.py:51
  27.3 0.8 %finish.1 = bf16[384,256]{1,0:T(8,128)(2,1)} custom-call(f32[256,384]{1,0:T(8,128)S(1)} %get-tuple-element.25.user_ref, f32[1,256]{1,0:T(1,128)S(1)} %get-tuple-element.26.gain_ref), custom_call_target="tpu_custom_call" | custom-call | flops 196608 | bytes 589824 | tf_op jit(solution)/shard_map/finish/pallas_call | solution.py:362
  28.2 0.2 collective-permute-done.10
  28.4 1.3 %collective-permute-done.9 = f32[4,384]{1,0:T(4,128)S(1)} collective-permute-done((f32[4,384]{1,0:T(4,128)S(1)}, f32[4,384]{1,0:T(4,128)S(1)}, u32[]{:S(2)}, u32[]{:S(2)}) %collective-permute-start.9) | collective-permute-done | bytes 6176 | tf_op jit(solution)/shard_map/ppermute | solution.py:51
  29.7 0.0 collective-permute-done.8
  29.7 0.1 slice_reduce_fusion.7
  29.7 0.6 %add_subtract_fusion = f32[384]{0:T(512)} fusion(f32[384]{0:T(512)S(1)} %get-tuple-element.30, f32[384]{0:T(512)S(1)} %get-tuple-element.36, f32[384]{0:T(512)S(1)} %get-tuple-element.35, f32[384]{0:T(512)S(1)} %get-tuple-element.34, f32[384]{0:T(512)S(1)} %get-tuple-element.33, f32[384]{0:T(512)S(1)} %get-tuple-element.32, f32[384]{0:T(512)S(1)} %get-tuple-element.31, ...), kind=kLoop, calls=%fused_computation | loop fusion | flops 7296 | bytes 15360 | tf_op jit(solution)/shard_map/sub | solution.py:403
Async XLA Ops:
  0.6 11.6 %collective-permute-start.4 = (bf16[64,1024]{1,0:T(8,128)(2,1)}, bf16[64,1024]{1,0:T(8,128)(2,1)S(1)}, u32[]{:S(2)}, u32[]{:S(2)}) collective-permute-start(bf16[64,1024]{1,0:T(8,128)(2,1)} %own_ref.1), channel_id=1, source_target_pairs={{0,1},{1,0},{2,3},{3,2},{4,6},{5,7},{6,4},{7,5},{8,9},{9,8},{10,11... | collective-permute-start | bytes 393224 | tf_op jit(solution)/shard_map/ppermute | solution.py:71
  5.7 6.5 %collective-permute-start.5 = (bf16[32,1024]{1,0:T(8,128)(2,1)S(1)}, bf16[32,1024]{1,0:T(8,128)(2,1)S(1)}, u32[]{:S(2)}, u32[]{:S(2)}) collective-permute-start(bf16[32,1024]{1,0:T(8,128)(2,1)S(1)} %get-tuple-element.19), channel_id=1, source_target_pairs={{0,3},{1,2},{2,1},{3,0},{4,7},{5,6},{6,5},{7,4},{8,11},{9,10},{10,... | collective-permute-start | bytes 196616 | tf_op jit(solution)/shard_map/ppermute | solution.py:71
  8.2 4.7 %collective-permute-start = (bf16[144,256]{1,0:T(8,128)(2,1)S(1)}, bf16[144,256]{1,0:T(8,128)(2,1)S(1)}, u32[]{:S(2)}, u32[]{:S(2)}) collective-permute-start(bf16[144,256]{1,0:T(8,128)(2,1)S(1)} %get-tuple-element.17), channel_id=1, source_target_pairs={{0,4},{4,8},{8,12},{12,16},{16,20},{20,24},{24,28},{28,0},{1,5},{5... | collective-permute-start | bytes 221192 | tf_op jit(solution)/shard_map/ppermute | solution.py:38
  9.9 8.2 %copy-start = (bf16[2048,1024]{1,0:T(8,128)(2,1)S(1)}, bf16[2048,1024]{1,0:T(8,128)(2,1)}, u32[]{:S(2)}) copy-start(bf16[2048,1024]{1,0:T(8,128)(2,1)} %neg_ref.1) | copy-start | bytes 12582916
  10.0 8.2 %copy-start.1 = (bf16[64,1024]{1,0:T(8,128)(2,1)S(1)}, bf16[64,1024]{1,0:T(8,128)(2,1)}, u32[]{:S(2)}) copy-start(bf16[64,1024]{1,0:T(8,128)(2,1)} %own_ref.1) | copy-start | bytes 393220
  12.2 6.0 %collective-permute-start.7 = (bf16[32,1024]{1,0:T(8,128)(2,1)S(1)}, bf16[32,1024]{1,0:T(8,128)(2,1)S(1)}, u32[]{:S(2)}, u32[]{:S(2)}) collective-permute-start(bf16[32,1024]{1,0:T(8,128)(2,1)S(1)} %collective-permute-done.5.refs_1_), channel_id=1, source_target_pairs={{0,4},{4,0},{8,12},{12,8},{16,20},{20,16},{24,28},{28,24},{1,5},{5... | collective-permute-start | bytes 196616 | tf_op jit(solution)/shard_map/ppermute | solution.py:81
  12.2 6.0 %collective-permute-start.6 = (bf16[64,1024]{1,0:T(8,128)(2,1)S(1)}, bf16[64,1024]{1,0:T(8,128)(2,1)S(1)}, u32[]{:S(2)}, u32[]{:S(2)}) collective-permute-start(bf16[64,1024]{1,0:T(8,128)(2,1)S(1)} %collective-permute-done.4.refs_0_), channel_id=1, source_target_pairs={{0,4},{4,0},{8,12},{12,8},{16,20},{20,16},{24,28},{28,24},{1,5},{5... | collective-permute-start | bytes 393224 | tf_op jit(solution)/shard_map/ppermute | solution.py:81
  13.7 6.0 %collective-permute-start.3 = (bf16[64,384]{1,0:T(8,128)(2,1)S(1)}, bf16[64,384]{1,0:T(8,128)(2,1)S(1)}, u32[]{:S(2)}, u32[]{:S(2)}) collective-permute-start(bf16[64,384]{1,0:T(8,128)(2,1)S(1)} %shard_map.123.refs_0_), channel_id=1, source_target_pairs={{0,3},{1,2},{2,1},{3,0},{4,7},{5,6},{6,5},{7,4},{8,11},{9,10},{10,... | collective-permute-start | bytes 147464 | tf_op jit(solution)/shard_map/ppermute | solution.py:51
  15.8 5.5 %collective-permute-start.2 = (bf16[64,384]{1,0:T(8,128)(2,1)S(1)}, bf16[64,384]{1,0:T(8,128)(2,1)S(1)}, u32[]{:S(2)}, u32[]{:S(2)}) collective-permute-start(bf16[64,384]{1,0:T(8,128)(2,1)S(1)} %shard_map.123.refs_0_), channel_id=1, source_target_pairs={{0,2},{1,3},{2,0},{3,1},{4,6},{5,7},{6,4},{7,5},{8,10},{9,11},{10,... | collective-permute-start | bytes 147464 | tf_op jit(solution)/shard_map/ppermute | solution.py:51
  16.1 5.2 %collective-permute-start.1 = (bf16[64,384]{1,0:T(8,128)(2,1)S(1)}, bf16[64,384]{1,0:T(8,128)(2,1)S(1)}, u32[]{:S(2)}, u32[]{:S(2)}) collective-permute-start(bf16[64,384]{1,0:T(8,128)(2,1)S(1)} %shard_map.123.refs_0_), channel_id=1, source_target_pairs={{0,1},{1,0},{2,3},{3,2},{4,5},{5,4},{6,7},{7,6},{8,9},{9,8},{10,11... | collective-permute-start | bytes 147464 | tf_op jit(solution)/shard_map/ppermute | solution.py:51
  22.9 5.5 %collective-permute-start.10 = (f32[4,384]{1,0:T(4,128)S(1)}, f32[4,384]{1,0:T(4,128)S(1)}, u32[]{:S(2)}, u32[]{:S(2)}) collective-permute-start(f32[4,384]{1,0:T(4,128)S(1)} %get-tuple-element.27), channel_id=1, source_target_pairs={{0,3},{1,2},{2,1},{3,0},{4,7},{5,6},{6,5},{7,4},{8,11},{9,10},{10,... | collective-permute-start | bytes 18440 | tf_op jit(solution)/shard_map/ppermute | solution.py:51
  25.1 4.5 %collective-permute-start.9 = (f32[4,384]{1,0:T(4,128)S(1)}, f32[4,384]{1,0:T(4,128)S(1)}, u32[]{:S(2)}, u32[]{:S(2)}) collective-permute-start(f32[4,384]{1,0:T(4,128)S(1)} %get-tuple-element.27), channel_id=1, source_target_pairs={{0,2},{1,3},{2,0},{3,1},{4,6},{5,7},{6,4},{7,5},{8,10},{9,11},{10,... | collective-permute-start | bytes 18440 | tf_op jit(solution)/shard_map/ppermute | solution.py:51
  25.4 4.3 %collective-permute-start.8 = (f32[4,384]{1,0:T(4,128)S(1)}, f32[4,384]{1,0:T(4,128)S(1)}, u32[]{:S(2)}, u32[]{:S(2)}) collective-permute-start(f32[4,384]{1,0:T(4,128)S(1)} %get-tuple-element.27), channel_id=1, source_target_pairs={{0,1},{1,0},{2,3},{3,2},{4,5},{5,4},{6,7},{7,6},{8,9},{9,8},{10,11... | collective-permute-start | bytes 18440 | tf_op jit(solution)/shard_map/ppermute | solution.py:51

commit v7 on v6

--- a/solution.py
+++ b/solution.py
@@ -13,6 +13,7 @@
 LANES = 128
 FLAG_ROWS = 16
 LOW = -1e30
+LOG2E = 1.4426950408889634
 MIB = 1 << 20
 AHEAD = 4 * 10**9
 F32 = jnp.float32
@@ -299,38 +300,38 @@
 
 def score_body(count, *refs):
     o_refs = refs[:count]
-    mix_ref, turned_ref, id_ref, pos_ref, target_ref, stat_ref, user_ref, attn, logits = refs[count:]
+    mix_ref, turned_ref, id_ref, pos_ref, target_ref, stat_ref, user_ref, attn = refs[count:]
     width, rows = attn.shape
     share = user_ref.shape[0]
     negs = mix_ref.shape[0]
     block = 256
+    tiles = lambda a: a.reshape(a.shape[0] // 8, 8, rows)
     heads = jnp.concatenate([ref[...] for ref in o_refs], 0)
     total = jnp.zeros((8, rows), F32)
     for start in range(0, width, block):
         part = dot_plain(turned_ref[start : start + block, :], heads)
         attn[start : start + block, :] = part
-        total += jnp.sum((part * part).reshape(block // 8, 8, rows), 0)
+        total += jnp.sum(tiles(part * part), 0)
     scale = lax.rsqrt(jnp.sum(total, 0, keepdims=True) / width + 1e-05)
+    power = scale * LOG2E
+    target = target_ref[...]
+    top = jnp.full((8, rows), LOW, F32)
+    mass = jnp.zeros((8, rows), F32)
+    for start in range(0, negs, block):
+        part = dot_plain(mix_ref[start : start + block, :], heads)
+        ids = id_ref[start : start + block, :]
+        hit = jnp.concatenate([ids] * (rows // LANES), 1) == target
+        part = tiles(jnp.where(hit, LOW, part))
+        above = jnp.maximum(top, jnp.max(part, 0))
+        mass = mass * jnp.exp2((top - above) * power) + jnp.sum(jnp.exp2((part - above[None]) * power[None]), 0)
+        top = above
+    above = jnp.max(top, 0, keepdims=True)
+    mass = jnp.sum(mass * jnp.exp2((top - above) * power), 0, keepdims=True)
     here = pl.multiple_of(lax.axis_index("head") * share, share)
     user = attn[pl.ds(here, share), :] * scale
     user_ref[...] = user
     pos = jnp.sum(user * pos_ref[...], 0, keepdims=True)
-    target = target_ref[...]
-    top = jnp.full((8, rows), LOW, F32)
-    for start in range(0, negs, block):
-        part = dot_plain(mix_ref[start : start + block, :], heads) * scale
-        ids = id_ref[start : start + block, :]
-        hit = jnp.concatenate([ids] * (rows // LANES), 1) == target
-        part = jnp.where(hit, LOW, part)
-        logits[start : start + block, :] = part
-        top = jnp.maximum(top, jnp.max(part.reshape(block // 8, 8, rows), 0))
-    top = jnp.max(top, 0, keepdims=True)
-    mass = jnp.zeros((8, rows), F32)
-    for start in range(0, negs, block):
-        part = jnp.exp(logits[start : start + block, :] - top)
-        mass += jnp.sum(part.reshape(block // 8, 8, rows), 0)
-    mass = jnp.sum(mass, 0, keepdims=True)
-    stat_ref[...] = jnp.concatenate([top, mass, pos, pos], 0)
+    stat_ref[...] = jnp.concatenate([above * scale, mass, pos, pos], 0)
 
 
 def score(heads, mix, turned, id_cols, pos_turned, target):
@@ -347,7 +348,7 @@
         ),
         in_specs=[WHOLE] * (count + 5),
         out_specs=(WHOLE, WHOLE),
-        scratch_shapes=[pltpu.VMEM((width, rows), F32), pltpu.VMEM((negs, rows), F32)],
+        scratch_shapes=[pltpu.VMEM((width, rows), F32)],
         compiler_params=pltpu.CompilerParams(vmem_limit_bytes=28 * MIB),
         cost_estimate=pl.CostEstimate(flops=2 * rows * deep * (negs + width), bytes_accessed=2 * negs * deep, transcendentals=negs * rows),
     )(*heads, mix, turned, id_cols, pos_turned, target)

time: 30.6 us -> 30.6 us (level)
  no operation moved by 1% of the time
where the time goes in v7:
time: 30.6 us; the launch traced here: 30.4 us
  starting transfers between devices  15.1 us (49%)
  Pallas kernels  8.28 us (27%)
  waiting for transfers between devices  5.66 us (18%)
  between operations  0.71 us (2%)
  other arithmetic  0.66 us (2%)
    ppermute x6, starting transfers between devices, from_all(): pieces.append(lax.ppermute(shard, axis, pairs))  8.9 us
    ppermute x2, starting transfers between devices, fetch_in_pairs(): far.append(lax.ppermute(half if last else shard, ('seq', 'head'), route))  5.67 us
    ppermute x6, waiting for transfers between devices, from_all(): pieces.append(lax.ppermute(shard, axis, pairs))  3.25 us
    ppermute x2, waiting for transfers between devices, fetch_in_pairs(): far.append(lax.ppermute(half if last else shard, ('seq', 'head'), route))  2.24 us
    pallas_call x1, Pallas kernels, front(): pl.pallas_call(front_body, name='front', out_shape=(jax.ShapeDtypeStruct(...  1.91 us
    pallas_call x1, Pallas kernels, score(): pl.pallas_call(functools.partial(score_body, count), name='score', out_sh...  1.66 us
    pallas_call x1, Pallas kernels, premix(): pl.pallas_call(functools.partial(premix_body, count, (len(far), len(near)...  1.33 us
    pallas_call x2, Pallas kernels, attend(): pl.pallas_call(body, out_shape=jax.ShapeDtypeStruct((cols, width), BF16),...  1.29 us
  transfers between devices with their start and end apart: 11, of which 6 were waited for; matrix products, arithmetic and copies ran while one was open for 0% of the time, Pallas kernels for 22%

profile of v7, /device:TPU:0, one launch (start us, length us, event | category | flops | bytes accessed | tf_op | source)
XLA Modules:
  0.0 30.4 jit_solution(7240104415944455253)
XLA Ops:
  0.6 3.1 %collective-permute-start.4 = (bf16[64,1024]{1,0:T(8,128)(2,1)}, bf16[64,1024]{1,0:T(8,128)(2,1)S(1)}, u32[]{:S(2)}, u32[]{:S(2)}) collective-permute-start(bf16[64,1024]{1,0:T(8,128)(2,1)} %own_ref.1), channel_id=1, source_target_pairs={{0,1},{1,0},{2,3},{3,2},{4,6},{5,7},{6,4},{7,5},{8,9},{9,8},{10,11... | collective-permute-start | bytes 393224 | tf_op jit(solution)/shard_map/ppermute | solution.py:72
  3.7 1.9 %front.1 = (bf16[384,64]{1,0:T(8,128)(2,1)S(1)}, bf16[144,384]{1,0:T(8,128)(2,1)S(1)}, bf16[144,256]{1,0:T(8,128)(2,1)S(1)}, bf16[32,1024]{1,0:T(8,128)(2,1)S(1)}) custom-call(bf16[384,1024]{1,0:T(8,128)(2,1)} %refs_0_.1, bf16[64,1024]{1,0:T(8,128)(2,1)} %bitcast.10, bf16[64,1024]{1,0:T(8,128)(2,1)} %bitcast.11, bf16[64,1024]{1,0:T(8,128)(2,1)} %bitcast.12, ...), custom_call_target="tpu_custom_call" | custom-call | flops 4000000000 | bytes 1572864 | tf_op jit(solution)/shard_map/front/pallas_call | solution.py:124
  5.7 2.5 %collective-permute-start.5 = (bf16[32,1024]{1,0:T(8,128)(2,1)S(1)}, bf16[32,1024]{1,0:T(8,128)(2,1)S(1)}, u32[]{:S(2)}, u32[]{:S(2)}) collective-permute-start(bf16[32,1024]{1,0:T(8,128)(2,1)S(1)} %get-tuple-element.19), channel_id=1, source_target_pairs={{0,3},{1,2},{2,1},{3,0},{4,7},{5,6},{6,5},{7,4},{8,11},{9,10},{10,... | collective-permute-start | bytes 196616 | tf_op jit(solution)/shard_map/ppermute | solution.py:72
  8.2 0.0 collective-permute-start
  8.2 0.5 %shard_map.122.late_ref = bf16[64,128]{1,0:T(8,128)(2,1)S(1)} custom-call(bf16[384,64]{1,0:T(8,128)(2,1)S(1)} %get-tuple-element.15.q_ref, bf16[144,384]{1,0:T(8,128)(2,1)S(1)} %get-tuple-element.16.own_ref), custom_call_target="tpu_custom_call" | custom-call | flops 4000000000 | bytes 147456 | tf_op jit(solution)/shard_map/pallas_call | solution.py:244
  8.7 1.2 %prepare.1 = (s32[2048,128]{1,0:T(8,128)S(1)}, f32[256,384]{1,0:T(8,128)S(1)}, f32[1,256]{1,0:T(1,128)S(1)}, s32[1,384]{1,0:T(1,128)S(1)}, f32[1,1024]{1,0:T(1,128)S(1)}) custom-call(bf16[384,1024]{1,0:T(8,128)(2,1)} %pos_hbm.1, f32[1,1024]{1,0:T(1,128)} %bitcast.8, s32[16,128]{1,0:T(8,128)} %bitcast.7, s32[3,128]{1,0:T(4,128)} %bitcast.9), custom_call_target="tpu_custom_call" | custom-call | flops 98304 | bytes 196608 | tf_op jit(solution)/shard_map/prepare/pallas_call | solution.py:173
  9.9 0.0 copy-start
  10.0 0.0 copy-start.1
  10.0 2.2 %collective-permute-done.5.refs_1_ = bf16[32,1024]{1,0:T(8,128)(2,1)S(1)} collective-permute-done((bf16[32,1024]{1,0:T(8,128)(2,1)S(1)}, bf16[32,1024]{1,0:T(8,128)(2,1)S(1)}, u32[]{:S(2)}, u32[]{:S(2)}) %collective-permute-start.5) | collective-permute-done | bytes 65568 | tf_op jit(solution)/shard_map/ppermute | solution.py:72
  12.2 0.0 collective-permute-start.7
  12.2 0.0 collective-permute-done.4.refs_0_
  12.2 0.5 %collective-permute-start.6 = (bf16[64,1024]{1,0:T(8,128)(2,1)S(1)}, bf16[64,1024]{1,0:T(8,128)(2,1)S(1)}, u32[]{:S(2)}, u32[]{:S(2)}) collective-permute-start(bf16[64,1024]{1,0:T(8,128)(2,1)S(1)} %collective-permute-done.4.refs_0_), channel_id=1, source_target_pairs={{0,4},{4,0},{8,12},{12,8},{16,20},{20,16},{24,28},{28,24},{1,5},{5... | collective-permute-start | bytes 393224 | tf_op jit(solution)/shard_map/ppermute | solution.py:82
  12.7 0.2 collective-permute-done.prev_ref
  12.9 0.8 %shard_map.123.refs_0_ = bf16[64,384]{1,0:T(8,128)(2,1)S(1)} custom-call(bf16[384,64]{1,0:T(8,128)(2,1)S(1)} %get-tuple-element.15.q_ref, bf16[144,384]{1,0:T(8,128)(2,1)S(1)} %get-tuple-element.16.own_ref, bf16[144,256]{1,0:T(8,128)(2,1)S(1)} %collective-permute-done.prev_ref, bf16[64,128]{1,0:T(8,128)(2,1)S(1)} %shard_map.122.late_ref), custom_call_target="tpu_custom_call" | custom-call | flops 4000000000 | bytes 147456 | tf_op jit(solution)/shard_map/pallas_call | solution.py:244
  13.7 2.1 %collective-permute-start.3 = (bf16[64,384]{1,0:T(8,128)(2,1)S(1)}, bf16[64,384]{1,0:T(8,128)(2,1)S(1)}, u32[]{:S(2)}, u32[]{:S(2)}) collective-permute-start(bf16[64,384]{1,0:T(8,128)(2,1)S(1)} %shard_map.123.refs_0_), channel_id=1, source_target_pairs={{0,3},{1,2},{2,1},{3,0},{4,7},{5,6},{6,5},{7,4},{8,11},{9,10},{10,... | collective-permute-start | bytes 147464 | tf_op jit(solution)/shard_map/ppermute | solution.py:52
  15.8 0.3 collective-permute-start.2
  16.1 2.1 %collective-permute-start.1 = (bf16[64,384]{1,0:T(8,128)(2,1)S(1)}, bf16[64,384]{1,0:T(8,128)(2,1)S(1)}, u32[]{:S(2)}, u32[]{:S(2)}) collective-permute-start(bf16[64,384]{1,0:T(8,128)(2,1)S(1)} %shard_map.123.refs_0_), channel_id=1, source_target_pairs={{0,1},{1,0},{2,3},{3,2},{4,5},{5,4},{6,7},{7,6},{8,9},{9,8},{10,11... | collective-permute-start | bytes 147464 | tf_op jit(solution)/shard_map/ppermute | solution.py:52
  18.2 0.0 collective-permute-done.7.refs_3_
  18.2 0.0 collective-permute-done.6.refs_2_
  18.2 0.0 copy-done
  18.2 0.0 copy-done.1
  18.2 1.3 %premix.1 = (bf16[2048,256]{1,0:T(8,128)(2,1)S(1)}, bf16[1024,256]{1,0:T(8,128)(2,1)S(1)}) custom-call(bf16[2048,1024]{1,0:T(8,128)(2,1)S(1)} %copy-done, f32[1,1024]{1,0:T(1,128)S(1)} %get-tuple-element.18.gain_ref, bf16[64,1024]{1,0:T(8,128)(2,1)S(1)} %copy-done.1, bf16[64,1024]{1,0:T(8,128)(2,1)S(1)} %collective-permute-done.4.refs_0_, ...), custom_call_target="tpu_custom_call" | custom-call | flops 1073741824 | bytes 4194304 | tf_op jit(solution)/shard_map/premix/pallas_call | solution.py:286
  19.5 0.2 collective-permute-done.3.refs_3_
  19.7 1.6 %collective-permute-done.2.refs_2_ = bf16[64,384]{1,0:T(8,128)(2,1)S(1)} collective-permute-done((bf16[64,384]{1,0:T(8,128)(2,1)S(1)}, bf16[64,384]{1,0:T(8,128)(2,1)S(1)}, u32[]{:S(2)}, u32[]{:S(2)}) %collective-permute-start.2) | collective-permute-done | bytes 49184 | tf_op jit(solution)/shard_map/ppermute | solution.py:52
  21.3 0.0 collective-permute-done.1.refs_1_
  21.3 1.7 %score.1 = (f32[4,384]{1,0:T(4,128)S(1)}, f32[256,384]{1,0:T(8,128)S(1)}) custom-call(bf16[64,384]{1,0:T(8,128)(2,1)S(1)} %shard_map.123.refs_0_, bf16[64,384]{1,0:T(8,128)(2,1)S(1)} %collective-permute-done.1.refs_1_, bf16[64,384]{1,0:T(8,128)(2,1)S(1)} %collective-permute-done.2.refs_2_, bf16[64,384]{1,0:T(8,128)(2,1)S(1)} %collective-permute-done.3.refs_3_, ...), custom_call_target="tpu_custom_call" | custom-call | flops 603979776 | bytes 1048576 | tf_op jit(solution)/shard_map/score/pallas_call | solution.py:342
  23.0 2.2 %collective-permute-start.10 = (f32[4,384]{1,0:T(4,128)S(1)}, f32[4,384]{1,0:T(4,128)S(1)}, u32[]{:S(2)}, u32[]{:S(2)}) collective-permute-start(f32[4,384]{1,0:T(4,128)S(1)} %get-tuple-element.27), channel_id=1, source_target_pairs={{0,3},{1,2},{2,1},{3,0},{4,7},{5,6},{6,5},{7,4},{8,11},{9,10},{10,... | collective-permute-start | bytes 18440 | tf_op jit(solution)/shard_map/ppermute | solution.py:52
  25.2 0.2 collective-permute-start.9
  25.5 2.0 %collective-permute-start.8 = (f32[4,384]{1,0:T(4,128)S(1)}, f32[4,384]{1,0:T(4,128)S(1)}, u32[]{:S(2)}, u32[]{:S(2)}) collective-permute-start(f32[4,384]{1,0:T(4,128)S(1)} %get-tuple-element.27), channel_id=1, source_target_pairs={{0,1},{1,0},{2,3},{3,2},{4,5},{5,4},{6,7},{7,6},{8,9},{9,8},{10,11... | collective-permute-start | bytes 18440 | tf_op jit(solution)/shard_map/ppermute | solution.py:52
  27.4 0.8 %finish.1 = bf16[384,256]{1,0:T(8,128)(2,1)} custom-call(f32[256,384]{1,0:T(8,128)S(1)} %get-tuple-element.25.user_ref, f32[1,256]{1,0:T(1,128)S(1)} %get-tuple-element.26.gain_ref), custom_call_target="tpu_custom_call" | custom-call | flops 196608 | bytes 589824 | tf_op jit(solution)/shard_map/finish/pallas_call | solution.py:363
  28.3 0.2 collective-permute-done.10
  28.5 1.3 %collective-permute-done.9 = f32[4,384]{1,0:T(4,128)S(1)} collective-permute-done((f32[4,384]{1,0:T(4,128)S(1)}, f32[4,384]{1,0:T(4,128)S(1)}, u32[]{:S(2)}, u32[]{:S(2)}) %collective-permute-start.9) | collective-permute-done | bytes 6176 | tf_op jit(solution)/shard_map/ppermute | solution.py:52
  29.7 0.0 collective-permute-done.8
  29.7 0.1 slice_reduce_fusion.7
  29.8 0.6 %add_subtract_fusion = f32[384]{0:T(512)} fusion(f32[384]{0:T(512)S(1)} %get-tuple-element.30, f32[384]{0:T(512)S(1)} %get-tuple-element.36, f32[384]{0:T(512)S(1)} %get-tuple-element.35, f32[384]{0:T(512)S(1)} %get-tuple-element.34, f32[384]{0:T(512)S(1)} %get-tuple-element.33, f32[384]{0:T(512)S(1)} %get-tuple-element.32, f32[384]{0:T(512)S(1)} %get-tuple-element.31, ...), kind=kLoop, calls=%fused_computation | loop fusion | flops 7296 | bytes 15360 | tf_op jit(solution)/shard_map/sub | solution.py:404
Async XLA Ops:
  0.6 11.6 %collective-permute-start.4 = (bf16[64,1024]{1,0:T(8,128)(2,1)}, bf16[64,1024]{1,0:T(8,128)(2,1)S(1)}, u32[]{:S(2)}, u32[]{:S(2)}) collective-permute-start(bf16[64,1024]{1,0:T(8,128)(2,1)} %own_ref.1), channel_id=1, source_target_pairs={{0,1},{1,0},{2,3},{3,2},{4,6},{5,7},{6,4},{7,5},{8,9},{9,8},{10,11... | collective-permute-start | bytes 393224 | tf_op jit(solution)/shard_map/ppermute | solution.py:72
  5.7 6.5 %collective-permute-start.5 = (bf16[32,1024]{1,0:T(8,128)(2,1)S(1)}, bf16[32,1024]{1,0:T(8,128)(2,1)S(1)}, u32[]{:S(2)}, u32[]{:S(2)}) collective-permute-start(bf16[32,1024]{1,0:T(8,128)(2,1)S(1)} %get-tuple-element.19), channel_id=1, source_target_pairs={{0,3},{1,2},{2,1},{3,0},{4,7},{5,6},{6,5},{7,4},{8,11},{9,10},{10,... | collective-permute-start | bytes 196616 | tf_op jit(solution)/shard_map/ppermute | solution.py:72
  8.2 4.7 %collective-permute-start = (bf16[144,256]{1,0:T(8,128)(2,1)S(1)}, bf16[144,256]{1,0:T(8,128)(2,1)S(1)}, u32[]{:S(2)}, u32[]{:S(2)}) collective-permute-start(bf16[144,256]{1,0:T(8,128)(2,1)S(1)} %get-tuple-element.17), channel_id=1, source_target_pairs={{0,4},{4,8},{8,12},{12,16},{16,20},{20,24},{24,28},{28,0},{1,5},{5... | collective-permute-start | bytes 221192 | tf_op jit(solution)/shard_map/ppermute | solution.py:39
  9.9 8.2 %copy-start = (bf16[2048,1024]{1,0:T(8,128)(2,1)S(1)}, bf16[2048,1024]{1,0:T(8,128)(2,1)}, u32[]{:S(2)}) copy-start(bf16[2048,1024]{1,0:T(8,128)(2,1)} %neg_ref.1) | copy-start | bytes 12582916
  10.0 8.2 %copy-start.1 = (bf16[64,1024]{1,0:T(8,128)(2,1)S(1)}, bf16[64,1024]{1,0:T(8,128)(2,1)}, u32[]{:S(2)}) copy-start(bf16[64,1024]{1,0:T(8,128)(2,1)} %own_ref.1) | copy-start | bytes 393220
  12.2 6.0 %collective-permute-start.7 = (bf16[32,1024]{1,0:T(8,128)(2,1)S(1)}, bf16[32,1024]{1,0:T(8,128)(2,1)S(1)}, u32[]{:S(2)}, u32[]{:S(2)}) collective-permute-start(bf16[32,1024]{1,0:T(8,128)(2,1)S(1)} %collective-permute-done.5.refs_1_), channel_id=1, source_target_pairs={{0,4},{4,0},{8,12},{12,8},{16,20},{20,16},{24,28},{28,24},{1,5},{5... | collective-permute-start | bytes 196616 | tf_op jit(solution)/shard_map/ppermute | solution.py:82
  12.2 6.0 %collective-permute-start.6 = (bf16[64,1024]{1,0:T(8,128)(2,1)S(1)}, bf16[64,1024]{1,0:T(8,128)(2,1)S(1)}, u32[]{:S(2)}, u32[]{:S(2)}) collective-permute-start(bf16[64,1024]{1,0:T(8,128)(2,1)S(1)} %collective-permute-done.4.refs_0_), channel_id=1, source_target_pairs={{0,4},{4,0},{8,12},{12,8},{16,20},{20,16},{24,28},{28,24},{1,5},{5... | collective-permute-start | bytes 393224 | tf_op jit(solution)/shard_map/ppermute | solution.py:82
  13.7 6.0 %collective-permute-start.3 = (bf16[64,384]{1,0:T(8,128)(2,1)S(1)}, bf16[64,384]{1,0:T(8,128)(2,1)S(1)}, u32[]{:S(2)}, u32[]{:S(2)}) collective-permute-start(bf16[64,384]{1,0:T(8,128)(2,1)S(1)} %shard_map.123.refs_0_), channel_id=1, source_target_pairs={{0,3},{1,2},{2,1},{3,0},{4,7},{5,6},{6,5},{7,4},{8,11},{9,10},{10,... | collective-permute-start | bytes 147464 | tf_op jit(solution)/shard_map/ppermute | solution.py:52
  15.8 5.5 %collective-permute-start.2 = (bf16[64,384]{1,0:T(8,128)(2,1)S(1)}, bf16[64,384]{1,0:T(8,128)(2,1)S(1)}, u32[]{:S(2)}, u32[]{:S(2)}) collective-permute-start(bf16[64,384]{1,0:T(8,128)(2,1)S(1)} %shard_map.123.refs_0_), channel_id=1, source_target_pairs={{0,2},{1,3},{2,0},{3,1},{4,6},{5,7},{6,4},{7,5},{8,10},{9,11},{10,... | collective-permute-start | bytes 147464 | tf_op jit(solution)/shard_map/ppermute | solution.py:52
  16.1 5.2 %collective-permute-start.1 = (bf16[64,384]{1,0:T(8,128)(2,1)S(1)}, bf16[64,384]{1,0:T(8,128)(2,1)S(1)}, u32[]{:S(2)}, u32[]{:S(2)}) collective-permute-start(bf16[64,384]{1,0:T(8,128)(2,1)S(1)} %shard_map.123.refs_0_), channel_id=1, source_target_pairs={{0,1},{1,0},{2,3},{3,2},{4,5},{5,4},{6,7},{7,6},{8,9},{9,8},{10,11... | collective-permute-start | bytes 147464 | tf_op jit(solution)/shard_map/ppermute | solution.py:52
  23.0 5.5 %collective-permute-start.10 = (f32[4,384]{1,0:T(4,128)S(1)}, f32[4,384]{1,0:T(4,128)S(1)}, u32[]{:S(2)}, u32[]{:S(2)}) collective-permute-start(f32[4,384]{1,0:T(4,128)S(1)} %get-tuple-element.27), channel_id=1, source_target_pairs={{0,3},{1,2},{2,1},{3,0},{4,7},{5,6},{6,5},{7,4},{8,11},{9,10},{10,... | collective-permute-start | bytes 18440 | tf_op jit(solution)/shard_map/ppermute | solution.py:52
  25.2 4.5 %collective-permute-start.9 = (f32[4,384]{1,0:T(4,128)S(1)}, f32[4,384]{1,0:T(4,128)S(1)}, u32[]{:S(2)}, u32[]{:S(2)}) collective-permute-start(f32[4,384]{1,0:T(4,128)S(1)} %get-tuple-element.27), channel_id=1, source_target_pairs={{0,2},{1,3},{2,0},{3,1},{4,6},{5,7},{6,4},{7,5},{8,10},{9,11},{10,... | collective-permute-start | bytes 18440 | tf_op jit(solution)/shard_map/ppermute | solution.py:52
  25.5 4.3 %collective-permute-start.8 = (f32[4,384]{1,0:T(4,128)S(1)}, f32[4,384]{1,0:T(4,128)S(1)}, u32[]{:S(2)}, u32[]{:S(2)}) collective-permute-start(f32[4,384]{1,0:T(4,128)S(1)} %get-tuple-element.27), channel_id=1, source_target_pairs={{0,1},{1,0},{2,3},{3,2},{4,5},{5,4},{6,7},{7,6},{8,9},{9,8},{10,11... | collective-permute-start | bytes 18440 | tf_op jit(solution)/shard_map/ppermute | solution.py:52
